TPU v7x, 32 devices: a whole 2x2x4 slice. The times are simulated.
32 devices in a mesh: group: 2 (over y), tp: 8 (over z, x), pair: 2 (over core).
Axes of the slice: x: 2, y: 2, z: 4, core: 2. Of those that a mesh axis runs over, the one named last changes fastest.
Arguments:
- hidden_in: bfloat16 [1024, 8192], P(('group', 'pair'), 'tp'), parts along dimension 0, may hold values from -2.5 to 2.5
- norm_gain: float32 [8192], replicated, may hold values from 0.1 to 1.9
- query_weight: bfloat16 [8192, 8192], P('tp', 'pair'), may hold values from -5 to 5
- key_weight: bfloat16 [1024, 8192], P('tp', 'pair'), may hold values from -1 to 1
- value_weight: bfloat16 [1024, 8192], P('tp', 'pair'), may hold values from -0.0625 to 0.0625
- output_weight: bfloat16 [8192, 8192], P('tp', 'pair'), may hold values from -0.0625 to 0.0625
- lengths: int32 [4, 4], P(('group', 'pair')), parts along dimension 0, may hold values from 1 to 128, 256 in all within a row
Outputs:
- layer_out: bfloat16 [1024, 8192], P(('group', 'pair'), 'tp'), parts along dimension 0
There are 2 independent parts, one for each index of `group`. A program takes and returns all parts, laid end to end along the dimension named above; an argument that names none is the same for every part. Nothing has to cross between parts.
Inputs may be any that keep to these rules, and one draw needn't show every extreme that they name: The 4 lengths of a prompt block sum to 256; one of them equals 128.
All inputs are finite; a program needn't handle non-finite values.
Results may differ from a plain program's by a relative error of at most 0.007.
Values may be sent and summed in bfloat16 or wider, within the bound.
No kernel may reach another device: no remote copies, remote signals or barrier semaphores. Data moves between devices by JAX's collectives and lax.ppermute only.
A program may use at most 128 MiB of HBM per device.

v0:
```python
import math

import jax
import jax.numpy as jnp
from jax import lax
from jax.experimental import pallas as pl
from jax.experimental.pallas import tpu as pltpu

from jax.sharding import PartitionSpec as P

HQ = 64
KVH = 8
HD = 128
STRETCH = 256


THETA = 500000.0


def shortened(shard):

    def short(part):
        return part.astype(jnp.bfloat16) if part.dtype == jnp.float32 else part

    return jax.tree.map(short, shard)


def partner(shard, axis, apart):
    return lax.ppermute(shard, axis, [(i, i ^ 1 << apart) for i in range(lax.axis_size(axis))])


def token_layout(lengths):
    ends = jnp.cumsum(lengths, axis=1)
    offsets = jnp.arange(STRETCH, dtype=jnp.int32)
    finished = ends[:, None, :] <= offsets[None, :, None]
    request = jnp.sum(finished.astype(jnp.int32), axis=2)
    position = offsets[None, :] - jnp.sum(jnp.where(finished, lengths[:, None, :], 0), axis=2)
    return (request, position)


def scaled_freq(dims):
    freq = jnp.exp(dims.astype(jnp.float32) * (-math.log(THETA) / HD))
    wavelen = 2.0 * math.pi / freq
    smooth = (8192.0 / wavelen - 1.0) / 3.0
    middle = (1.0 - smooth) * freq / 8.0 + smooth * freq
    return jnp.where(wavelen < 2048.0, freq, jnp.where(wavelen > 8192.0, freq / 8.0, middle))


def rotary(projected, position, dims):
    freq = scaled_freq(dims[0::2])
    angle = position.astype(jnp.float32)[:, None] * freq[None, :]
    cosine = jnp.cos(angle)
    sine = jnp.sin(angle)
    first = projected[:, 0::2]
    second = projected[:, 1::2]
    turned = jnp.stack([first * cosine - second * sine, first * sine + second * cosine], axis=-1)
    return turned.reshape(projected.shape)


def attend(query, key, value, request, stretches, heads, groups):
    repeat = heads // groups
    query_blocks = query.reshape(stretches, STRETCH, groups, repeat, HD)
    key_blocks = key.reshape(stretches, STRETCH, groups, HD)
    value_blocks = value.reshape(stretches, STRETCH, groups, HD)
    scores = jnp.einsum(
        "cqgrd,ckgd->cgrqk", query_blocks, key_blocks, preferred_element_type=jnp.float32
    ) * (1.0 / math.sqrt(HD))
    offsets = jnp.arange(STRETCH, dtype=jnp.int32)
    keep = (request[:, :, None] == request[:, None, :]) & (offsets[:, None] >= offsets[None, :])[
        None
    ]
    scores = jnp.where(keep[:, None, None], scores, -1e30)
    top = jnp.max(scores, axis=-1, keepdims=True)
    weights = jnp.exp(scores - top)
    probs = (weights / jnp.sum(weights, axis=-1, keepdims=True)).astype(jnp.bfloat16)
    attended = jnp.einsum(
        "cgrqk,ckgd->cqgrd", probs, value_blocks, preferred_element_type=jnp.float32
    )
    return attended.reshape(stretches * STRETCH, heads * HD).astype(jnp.bfloat16)


def contract(left, right):
    return lax.dot_general(
        left, right, (((1,), (1,)), ((), ())), preferred_element_type=jnp.float32
    )


def bit_count(number):
    return number.bit_length() - 1


def assemble(parts, needed_bits, device, axis):
    for bit_index in range(max(needed_bits)):
        moving = [piece for piece, needed in zip(parts, needed_bits) if bit_index < needed]
        widths = [piece.shape[axis] for piece in moving]
        sent = jnp.concatenate(moving, axis=axis)
        arrived = partner(shortened(sent), "tp", bit_index).astype(sent.dtype)
        upper = device // 2**bit_index % 2 == 1
        cuts = []
        running = 0
        for width in widths[:-1]:
            running = running + width
            cuts.append(running)
        received = jnp.split(arrived, cuts, axis=axis)
        joined = []
        counter = 0
        for piece, needed in zip(parts, needed_bits):
            if bit_index < needed:
                other = received[counter]
                counter = counter + 1
                piece = jnp.where(
                    upper,
                    jnp.concatenate([other, piece], axis=axis),
                    jnp.concatenate([piece, other], axis=axis),
                )
            joined.append(piece)
        parts = joined
    return parts


def project(normed, query_rows, key_rows, value_rows, output_rows):
    query_full, key_full, value_full, output_full = (
        lax.all_gather(query_rows, "pair", axis=1, tiled=True),
        lax.all_gather(key_rows, "pair", axis=1, tiled=True),
        lax.all_gather(value_rows, "pair", axis=1, tiled=True),
        lax.all_gather(output_rows, "pair", axis=1, tiled=True),
    )
    query_pre = contract(normed, query_full)
    key_pre = contract(normed, key_full)
    value_pre = contract(normed, value_full)
    return (query_pre, key_pre, value_pre, output_full)


def general_body(hidden_in, norm_gain, query_weight, key_weight, value_weight, output_weight, lengths):
    tp_count = lax.axis_size("tp")
    device = lax.axis_index("tp")
    query_bits = bit_count(max(1, tp_count // HQ))
    group_bits = bit_count(max(1, tp_count // KVH))
    needed_bits = [query_bits, group_bits, group_bits]
    query_cols = query_weight.shape[0]
    stretches = lengths.shape[0]
    request, position = token_layout(lengths)
    position = position.reshape(-1)
    full_rows = lax.all_gather(hidden_in, "tp", axis=1, tiled=True)
    stream = full_rows.astype(jnp.float32)
    mean_square = jnp.mean(stream * stream, axis=1, keepdims=True)
    normed = (stream * lax.rsqrt(mean_square + 1e-05) * norm_gain[None, :]).astype(jnp.bfloat16)
    query_block, key_block, value_block = assemble(
        [query_weight, key_weight, value_weight], needed_bits, device, 0
    )
    query_pre, key_pre, value_pre, output_full = project(
        normed, query_block, key_block, value_block, output_weight
    )
    query_dims = jnp.arange(query_pre.shape[1], dtype=jnp.int32) % HD
    key_dims = jnp.arange(key_pre.shape[1], dtype=jnp.int32) % HD
    query = rotary(query_pre, position, query_dims).astype(jnp.bfloat16)
    key = rotary(key_pre, position, key_dims).astype(jnp.bfloat16)
    value = value_pre.astype(jnp.bfloat16)
    heads = query.shape[1] // HD
    groups = key.shape[1] // HD
    attended = attend(query, key, value, request, stretches, heads, groups)
    own_start = device * query_cols % (heads * HD)
    own_columns = lax.dynamic_slice_in_dim(attended, own_start, query_cols, 1)
    projected = contract(lax.all_gather(own_columns, "tp", axis=1, tiled=True), output_full)
    return (hidden_in.astype(jnp.float32) + projected).astype(jnp.bfloat16)


RING = 8
ROWS = STRETCH // 2
UNIT = 1024
ORDER = (0, 1, -1, -2, 2, 3, -3, -4)


def ring_place(t):
    return t // 2 if t % 2 == 0 else RING - 1 - t // 2


def ring_member(place):
    return 2 * place if place < RING // 2 else 2 * RING - 1 - 2 * place


def ring_swap(later):
    pairs = []
    for t in range(RING):
        for p in range(2):
            place = ring_place(t)
            step = 1 if (place + p + later) % 2 == 0 else -1
            pairs.append((t * 2 + p, ring_member((place + step) % RING) * 2 + p))
    return pairs


def swapped(shard, later):
    return lax.ppermute(shard, ("tp", "pair"), ring_swap(later))


def unit_of(index):
    t = lax.axis_index("tp")
    place = jnp.where(t % 2 == 0, t // 2, RING - 1 - t // 2)
    step = 1 - 2 * ((place + lax.axis_index("pair")) % 2)
    offset = jnp.int32(ORDER[0])
    for k in range(1, len(ORDER)):
        offset = jnp.where(index == k, ORDER[k], offset)
    where = (place + offset * step + RING) % RING
    return jnp.where(where < RING // 2, 2 * where, 2 * RING - 1 - 2 * where)


def columns_of(index):
    t = unit_of(index)
    mine = t // (RING // 2) == lax.axis_index("pair")
    return mine, pl.ds(pl.multiple_of(t % (RING // 2) * UNIT, UNIT), UNIT)


def copy_either(own, other, rows, index, target, sem):
    mine, cols = columns_of(index)

    @pl.when(mine)
    def _():
        pltpu.make_async_copy(own.at[rows, cols], target, sem).start()

    @pl.when(jnp.logical_not(mine))
    def _():
        pltpu.make_async_copy(other.at[rows, cols], target, sem).start()


def contract_units(xs, acc, weights, buf, sems, count):
    for u in range(count):
        prefetch(weights, buf, sems, 0, u, False)
        columns = slice(u * UNIT, (u + 1) * UNIT)
        product = contract(xs[:, columns], buf[:, columns])
        acc[...] = product if u == 0 else acc[...] + product


def prefetch(weights, target, sems, first, u, go):
    at = 0
    for n, (own, other) in enumerate(weights):
        rows = own.shape[0]
        where = target.at[pl.ds(at, rows), pl.ds(u * UNIT, UNIT)]
        if go:
            copy_either(own, other, pl.ds(0, rows), first + u, where, sems.at[n, u])
        else:
            source = own.at[:, pl.ds(0, UNIT)]
            pltpu.make_async_copy(source, where, sems.at[n, u]).wait()
        at += rows


def normed_unit(part, factor, gain_ref, index):
    base = unit_of(index) * (UNIT // 128)
    stream = part.astype(jnp.float32)
    lanes = []
    for k in range(UNIT // 128):
        gain = gain_ref[pl.ds(base + k, 1), :]
        lanes.append((stream[:, k * 128 : (k + 1) * 128] * factor * gain).astype(jnp.bfloat16))
    return lanes


def place_unit(xs, rows, n, part, factor, gain, index):
    for k, lane in enumerate(normed_unit(part, factor, gain, index)):
        at = n * UNIT + k * 128
        xs[rows, at : at + 128] = lane


VM = pl.BlockSpec(memory_space=pltpu.VMEM)
HBM = pl.BlockSpec(memory_space=pl.ANY)
SM = pl.BlockSpec(memory_space=pltpu.SMEM)


def params(mib):
    return pltpu.CompilerParams(vmem_limit_bytes=mib * 2**20)


def cost(rows, units, width):
    return pl.CostEstimate(
        flops=2 * rows * units * UNIT * width,
        bytes_accessed=2 * units * UNIT * width + 4 * rows * width,
        transcendentals=0,
    )


def paired(refs):
    return tuple((refs[n], refs[n + 1]) for n in range(0, len(refs), 2))


def unit_scratch(count, width, kinds):
    return [
        pltpu.VMEM((STRETCH, count * UNIT), jnp.bfloat16),
        pltpu.VMEM((width, count * UNIT), jnp.bfloat16),
        pltpu.SemaphoreType.DMA((kinds, count)),
        pltpu.SemaphoreType.DMA((kinds, count)),
    ]


def stream_rows(s):
    return slice(s * ROWS, (s + 1) * ROWS)


def early_kernel(a0, b0, a1, b1, a2, b2, gain, factor, *refs):
    *weights, acc, late, xs, buf, sems, late_sems = refs
    weights = paired(weights)
    for u in range(4):
        prefetch(weights, buf, sems, 0, u, True)
    for u in range(4):
        prefetch(weights, late, late_sems, 4, u, True)
    for s, (own, first, second) in enumerate(((a0, a1, a2), (b0, b1, b2))):
        rows = stream_rows(s)
        scale = factor[rows, :]
        place_unit(xs, rows, 0, own[...], scale, gain, 0)
        place_unit(xs, rows, 1, first[...], scale, gain, 1)
        place_unit(xs, rows, 2, second[:ROWS, :], scale, gain, 2)
        place_unit(xs, rows, 3, second[ROWS:, :], scale, gain, 3)
    contract_units(xs, acc, weights, buf, sems, 4)
    for u in range(4):
        prefetch(weights, late, late_sems, 4, u, False)


def middle_kernel(a3, b3, gain, factor, acc_in, late, acc, xs):
    for s, ref in enumerate((a3, b3)):
        for n in range(2):
            part = ref[n * ROWS : (n + 1) * ROWS, :]
            place_unit(xs, stream_rows(s), n, part, factor[stream_rows(s), :], gain, 4 + n)
    acc[...] = acc_in[...] + contract(xs[...], late[:, : 2 * UNIT])


def turned_heads(part, cosine, sine):
    lane = lax.broadcasted_iota(jnp.int32, part.shape, 1)
    other = jnp.where(lane % 2 == 0, pltpu.roll(part, HD - 1, 1), pltpu.roll(part, 1, 1))
    return (part * cosine + other * sine).astype(jnp.bfloat16)


def last_kernel(half, lens, new, gain, factor, acc_in, late, cosine, sine, *refs):
    if half:
        key_early, value_early = refs[:2]
        refs = refs[2:]
    attended, key_out, value_out, xs, acc = refs
    rows = stream_rows(half)
    for n in range(2):
        part = new[n * ROWS : (n + 1) * ROWS, :]
        place_unit(xs, slice(0, ROWS), n, part, factor[rows, :], gain, 6 + n)
    acc[...] = acc_in[rows, :] + contract(xs[...], late[:, 2 * UNIT :])
    heads = UNIT // HD
    cos, sin = cosine[rows, :], sine[rows, :]
    key = turned_heads(acc[:, UNIT : UNIT + HD], cos, sin)
    value = acc[:, UNIT + HD :].astype(jnp.bfloat16)
    key_out[...] = key
    value_out[...] = value
    if half:
        key = jnp.concatenate([key_early[...], key], axis=0)
        value = jnp.concatenate([value_early[...], value], axis=0)
    shape = (ROWS, (half + 1) * ROWS)
    row = lax.broadcasted_iota(jnp.int32, shape, 0) + half * ROWS
    col = lax.broadcasted_iota(jnp.int32, shape, 1)
    row_request = jnp.zeros(shape, jnp.int32)
    col_request = jnp.zeros(shape, jnp.int32)
    end = jnp.int32(0)
    for k in range(lens.shape[1]):
        end = end + lens[0, k]
        row_request += (row >= end).astype(jnp.int32)
        col_request += (col >= end).astype(jnp.int32)
    keep = (row_request == col_request) & (row >= col)
    queries = [turned_heads(acc[:, h * HD : (h + 1) * HD], cos, sin) for h in range(heads)]
    scores = contract(jnp.concatenate(queries, axis=0), key) * (1.0 / math.sqrt(HD))
    scores = jnp.where(keep[None], scores.reshape(heads, *shape), -1e30)
    weights = jnp.exp(scores - jnp.max(scores, axis=2, keepdims=True))
    probs = (weights / jnp.sum(weights, axis=2, keepdims=True)).astype(jnp.bfloat16)
    probs = probs.reshape(heads * ROWS, shape[1])
    out = jnp.dot(probs, value, preferred_element_type=jnp.float32).astype(jnp.bfloat16)
    for h in range(heads):
        attended[:, h * HD : (h + 1) * HD] = out[h * ROWS : (h + 1) * ROWS, :]


def out_early_kernel(a0, b0, a1, b1, a2, b2, w0, w1, acc, late, xs, buf, sems, late_sems):
    weights = ((w0, w1),)
    for u in range(4):
        prefetch(weights, buf, sems, 0, u, True)
    for u in range(4):
        prefetch(weights, late, late_sems, 4, u, True)
    for s, (own, first, second) in enumerate(((a0, a1, a2), (b0, b1, b2))):
        rows = stream_rows(s)
        xs[rows, 0:UNIT] = own[...]
        xs[rows, UNIT : 2 * UNIT] = first[...]
        xs[rows, 2 * UNIT : 3 * UNIT] = second[:ROWS, :]
        xs[rows, 3 * UNIT :] = second[ROWS:, :]
    contract_units(xs, acc, weights, buf, sems, 4)
    for u in range(4):
        prefetch(weights, late, late_sems, 4, u, False)


def out_middle_kernel(a3, b3, acc_in, late, acc, xs):
    for s, ref in enumerate((a3, b3)):
        xs[stream_rows(s), :UNIT] = ref[:ROWS, :]
        xs[stream_rows(s), UNIT:] = ref[ROWS:, :]
    acc[...] = acc_in[...] + contract(xs[...], late[:, : 2 * UNIT])


def out_last_kernel(half, new, hidden, acc_in, late, *refs):
    out = refs[-1]
    total = acc_in[stream_rows(half), :]
    for u in range(2):
        part = new[u * ROWS : (u + 1) * ROWS, :]
        total = total + contract(part, late[:, (u + 2) * UNIT : (u + 3) * UNIT])
    out[...] = (hidden[...].astype(jnp.float32) + total).astype(jnp.bfloat16)


def summed_over_tp(value):
    for bits in ((1, 2), (2, 1), (4, 4)):
        pairs = [(t * 2 + p, (t ^ bits[p]) * 2 + p) for t in range(RING) for p in range(2)]
        value = value + lax.ppermute(value, ("tp", "pair"), pairs)
    return value


def kernel_call(kernel, **options):
    return pl.pallas_call(kernel, **options)


def in_hbm(value):
    return pltpu.with_memory_space_constraint(value, pltpu.HBM)


def in_vmem(value):
    return pltpu.with_memory_space_constraint(value, pltpu.VMEM)


def after(value, *others):
    return lax.optimization_barrier((value, *others))


def ring_body(*args):
    return ring_layer(*args)


def ring_layer(hidden_in, norm_gain, query_weight, key_weight, value_weight, output_weight, lengths):
    f32, bf16 = jnp.float32, jnp.bfloat16
    a0, b0 = hidden_in[:ROWS], hidden_in[ROWS:]
    a1, b1 = swapped(a0, 0), swapped(b0, 0)
    weights = []
    for w in (key_weight, value_weight, query_weight):
        weights = [in_hbm(w), in_vmem(partner(w, "pair", 0))] + weights
    weights = weights[:2] + weights[4:] + weights[2:4]
    qkv = sum(w.shape[0] for w in weights[::2])
    stream = hidden_in.astype(f32)
    squares = jnp.sum(stream * stream, axis=1).reshape(2, 128)
    factor = lax.rsqrt(summed_over_tp(squares) / (RING * UNIT) + 1e-05)
    factor = jnp.broadcast_to(factor.reshape(STRETCH, 1), (STRETCH, 128))
    a2 = swapped(jnp.concatenate([a0, a1], axis=0), 1)
    b2 = swapped(jnp.concatenate([b0, b1], axis=0), 1)
    gain = norm_gain.reshape(RING * UNIT // 128, 128)
    _, position = token_layout(lengths)
    lane = jnp.arange(HD, dtype=jnp.int32)
    angle = position.reshape(-1).astype(f32)[:, None] * scaled_freq(lane - lane % 2)[None, :]
    cosine = jnp.cos(angle)
    sine = jnp.sin(angle) * jnp.where(lane % 2 == 0, -1.0, 1.0)[None, :]
    a3, b3 = swapped(a2, 0), swapped(b2, 0)

    factor, cosine, sine, lengths = after(factor, cosine, sine, lengths)
    acc_shape = jax.ShapeDtypeStruct((STRETCH, qkv), f32)
    acc, late = kernel_call(
        early_kernel,
        out_shape=(acc_shape, jax.ShapeDtypeStruct((qkv, 4 * UNIT), bf16)),
        in_specs=[VM] * 8 + [HBM, VM] * 3,
        out_specs=(VM, VM),
        scratch_shapes=unit_scratch(4, qkv, 3),
        compiler_params=params(24),
        cost_estimate=cost(STRETCH, 4, qkv),
    )(a0, b0, a1, b1, a2, b2, gain, factor, *weights)
    a3, acc = after(a3, acc)
    a4, b4 = swapped(a3, 1), swapped(b3, 1)
    acc = kernel_call(
        middle_kernel,
        out_shape=acc_shape,
        in_specs=[VM] * 6,
        out_specs=VM,
        scratch_shapes=[pltpu.VMEM((STRETCH, 2 * UNIT), bf16)],
        compiler_params=params(16),
        cost_estimate=cost(STRETCH, 2, qkv),
    )(a3, b3, gain, factor, acc, late)

    def last(half, new, early):
        kv = jax.ShapeDtypeStruct((ROWS, HD), bf16)
        return kernel_call(
            lambda *refs: last_kernel(half, *refs),
            out_shape=(jax.ShapeDtypeStruct((ROWS, UNIT), bf16), kv, kv),
            in_specs=[SM] + [VM] * (7 + len(early)),
            out_specs=(VM, VM, VM),
            scratch_shapes=[pltpu.VMEM((ROWS, 2 * UNIT), bf16), pltpu.VMEM((ROWS, qkv), f32)],
            compiler_params=params(20),
            cost_estimate=cost(ROWS, 4, qkv),
        )(lengths, new, gain, factor, acc, late, cosine, sine, *early)

    a0, key_a, value_a = last(0, a4, ())
    b0, _, _ = last(1, b4, (key_a, value_a))

    other_output = in_vmem(partner(output_weight, "pair", 0))
    output_weight = in_hbm(output_weight)
    a1, b1 = swapped(a0, 0), swapped(b0, 0)
    a2 = swapped(jnp.concatenate([a0, a1], axis=0), 1)
    b2 = swapped(jnp.concatenate([b0, b1], axis=0), 1)
    a3, b3 = swapped(a2, 0), swapped(b2, 0)
    width = output_weight.shape[0]
    acc_shape = jax.ShapeDtypeStruct((STRETCH, width), f32)
    acc, late = kernel_call(
        out_early_kernel,
        out_shape=(acc_shape, jax.ShapeDtypeStruct((width, 4 * UNIT), bf16)),
        in_specs=[VM] * 6 + [HBM, VM],
        out_specs=(VM, VM),
        scratch_shapes=unit_scratch(4, width, 1),
        compiler_params=params(22),
        cost_estimate=cost(STRETCH, 4, width),
    )(a0, b0, a1, b1, a2, b2, output_weight, other_output)
    a3, acc = after(a3, acc)
    a4, b4 = swapped(a3, 1), swapped(b3, 1)
    acc = kernel_call(
        out_middle_kernel,
        out_shape=acc_shape,
        in_specs=[VM] * 4,
        out_specs=VM,
        scratch_shapes=[pltpu.VMEM((STRETCH, 2 * UNIT), bf16)],
        compiler_params=params(16),
        cost_estimate=cost(STRETCH, 2, width),
    )(a3, b3, acc, late)

    def out_last(half, new, *partial):
        part = pl.BlockSpec((ROWS, UNIT), lambda i: (half, 0))
        return kernel_call(
            lambda *refs: out_last_kernel(half, *refs),
            grid=(1,),
            out_shape=jax.ShapeDtypeStruct((STRETCH, UNIT), bf16),
            in_specs=[VM, part, VM, VM] + [HBM] * half,
            out_specs=part,
            input_output_aliases={4: 0} if half else {},
            compiler_params=params(16),
            cost_estimate=cost(ROWS, 4, width),
        )(new, hidden_in, acc, late, *partial)

    return out_last(1, b4, out_last(0, a4))


def fits_ring(mesh):
    return dict(mesh.shape)["tp"] == RING and dict(mesh.shape)["pair"] == 2


def solution(mesh):
    placed = (
        P(("group", "pair"), "tp"),
        P(),
        P("tp", "pair"),
        P("tp", "pair"),
        P("tp", "pair"),
        P("tp", "pair"),
        P(("group", "pair"), None),
    )
    body = ring_body if fits_ring(mesh) else general_body
    return jax.shard_map(
        body, mesh=mesh, in_specs=placed, out_specs=P(("group", "pair"), "tp"), check_vma=False
    )
```

profile of v0, /device:TPU:0, one launch (start us, length us, event | category | flops | bytes accessed | tf_op | source)
XLA Modules:
  0.0 118.1 jit_solution(17313647277288851372)
XLA Ops:
  1.6 3.1 %collective-permute-start.7 = (bf16[128,1024]{1,0:T(8,128)(2,1)S(1)}, bf16[128,1024]{1,0:T(8,128)(2,1)S(1)}, u32[]{:S(2)}, u32[]{:S(2)}) collective-permute-start(bf16[128,1024]{1,0:T(8,128)(2,1)S(1)} %get-tuple-element.37.a0), channel_id=1, source_target_pairs={{0,4},{1,3},{2,6},{3,1},{4,0},{5,9},{6,2},{7,11},{8,12},{9,5},{10,... | collective-permute-start | bytes 786440 | tf_op jit(solution)/shard_map/ppermute | solution.py:193
  7.5 1.6 %collective-permute-done.7.a1 = bf16[128,1024]{1,0:T(8,128)(2,1)S(1)} collective-permute-done((bf16[128,1024]{1,0:T(8,128)(2,1)S(1)}, bf16[128,1024]{1,0:T(8,128)(2,1)S(1)}, u32[]{:S(2)}, u32[]{:S(2)}) %collective-permute-start.7) | collective-permute-done | bytes 262176 | tf_op jit(solution)/shard_map/ppermute | solution.py:193
  9.1 2.0 %collective-permute-start.8 = (bf16[256,1024]{1,0:T(8,128)(2,1)S(1)}, bf16[256,1024]{1,0:T(8,128)(2,1)}, u32[]{:S(2)}, u32[]{:S(2)}) collective-permute-start(bf16[256,1024]{1,0:T(8,128)(2,1)S(1)} %pad_maximum_fusion.1), channel_id=1, source_target_pairs={{0,2},{1,5},{2,0},{3,7},{4,8},{5,1},{6,10},{7,3},{8,4},{9,13},{10,... | collective-permute-start | bytes 1572872 | tf_op jit(solution)/shard_map/ppermute | solution.py:193
  11.1 1.7 %collective-permute-start.1 = (f32[2,128]{1,0:T(2,128)S(1)}, f32[2,128]{1,0:T(2,128)S(1)}, u32[]{:S(2)}, u32[]{:S(2)}) collective-permute-start(f32[2,128]{1,0:T(2,128)S(1)} %bitcast_add_fusion), channel_id=1, source_target_pairs={{0,4},{1,3},{2,6},{3,1},{4,0},{5,7},{6,2},{7,5},{8,12},{9,11},{10,... | collective-permute-start | bytes 3080 | tf_op jit(solution)/shard_map/ppermute | solution.py:406
  14.7 2.1 %collective-permute-start.2 = (f32[2,128]{1,0:T(2,128)S(1)}, f32[2,128]{1,0:T(2,128)S(1)}, u32[]{:S(2)}, u32[]{:S(2)}) collective-permute-start(f32[2,128]{1,0:T(2,128)S(1)} %fusion.5), channel_id=1, source_target_pairs={{0,8},{1,9},{2,10},{3,11},{4,12},{5,13},{6,14},{7,15},{8,0},{9,1},... | collective-permute-start | bytes 3080 | tf_op jit(solution)/shard_map/ppermute | solution.py:406
  16.8 5.8 %collective-permute-done.2 = f32[2,128]{1,0:T(2,128)S(1)} collective-permute-done((f32[2,128]{1,0:T(2,128)S(1)}, f32[2,128]{1,0:T(2,128)S(1)}, u32[]{:S(2)}, u32[]{:S(2)}) %collective-permute-start.2) | collective-permute-done | bytes 1056 | tf_op jit(solution)/shard_map/ppermute | solution.py:406
  26.7 6.8 %collective-permute-done.4.b2 = bf16[256,1024]{1,0:T(8,128)(2,1)} collective-permute-done((bf16[256,1024]{1,0:T(8,128)(2,1)}, bf16[256,1024]{1,0:T(8,128)(2,1)}, u32[]{:S(2)}, u32[]{:S(2)}) %collective-permute-start.4) | collective-permute-done | bytes 524320 | tf_op jit(solution)/shard_map/ppermute | solution.py:193
  34.1 2.1 %collective-permute-start.5 = (bf16[256,1024]{1,0:T(8,128)(2,1)}, bf16[256,1024]{1,0:T(8,128)(2,1)S(1)}, u32[]{:S(2)}, u32[]{:S(2)}) collective-permute-start(bf16[256,1024]{1,0:T(8,128)(2,1)} %collective-permute-done.4.b2), channel_id=1, source_target_pairs={{0,4},{1,3},{2,6},{3,1},{4,0},{5,9},{6,2},{7,11},{8,12},{9,5},{10,... | collective-permute-start | bytes 1572872 | tf_op jit(solution)/shard_map/ppermute | solution.py:193
  37.0 10.5 %shard_map.73 = (f32[256,1280]{1,0:T(8,128)S(1)}, bf16[1280,4096]{1,0:T(8,128)(2,1)S(1)}) custom-call(bf16[128,1024]{1,0:T(8,128)(2,1)S(1)} %get-tuple-element.37.a0, bf16[128,1024]{1,0:T(8,128)(2,1)S(1)} %get-tuple-element.38.b0, bf16[128,1024]{1,0:T(8,128)(2,1)S(1)} %collective-permute-done.7.a1, bf16[128,1024]{1,0:T(8,128)(2,1)S(1)} %collective-permute-done.3.b1, ...), custom_call_target="tpu_custom_call" | custom-call | flops 2684354560 | bytes 11796480 | tf_op jit(solution)/shard_map/pallas_call | solution.py:455
  49.6 1.8 %shard_map.74.refs_4_ = f32[256,1280]{1,0:T(8,128)S(1)} custom-call(bf16[256,1024]{1,0:T(8,128)(2,1)S(1)} %collective-permute-done.9.a3, bf16[256,1024]{1,0:T(8,128)(2,1)S(1)} %collective-permute-done.5.b3, f32[64,128]{1,0:T(8,128)S(1)} %bitcast.10, f32[256,128]{1,0:T(8,128)S(1)} %broadcast_in_dim.33.factor.refs_3_, ...), custom_call_target="tpu_custom_call" | custom-call | flops 1342177280 | bytes 6553600 | tf_op jit(solution)/shard_map/pallas_call | solution.py:466
  51.4 5.4 %collective-permute-done.13.refs_1_ = bf16[256,1024]{1,0:T(8,128)(2,1)S(1)} collective-permute-done((bf16[256,1024]{1,0:T(8,128)(2,1)S(1)}, bf16[256,1024]{1,0:T(8,128)(2,1)S(1)}, u32[]{:S(2)}, u32[]{:S(2)}) %collective-permute-start.13) | collective-permute-done | bytes 524320 | tf_op jit(solution)/shard_map/ppermute | solution.py:193
  56.8 3.2 %shard_map.75 = (bf16[128,1024]{1,0:T(8,128)(2,1)S(1)}, bf16[128,128]{1,0:T(8,128)(2,1)S(1)}, bf16[128,128]{1,0:T(8,128)(2,1)S(1)}) custom-call(s32[1,4]{1,0:T(1,128)S(1)} %copy-done.2, bf16[256,1024]{1,0:T(8,128)(2,1)S(1)} %collective-permute-done.13.refs_1_, f32[64,128]{1,0:T(8,128)S(1)} %bitcast.11, f32[256,128]{1,0:T(8,128)S(1)} %broadcast_in_dim.33.factor.refs_3_, ...), custom_call_target="tpu_custom_call" | custom-call | flops 1342177280 | bytes 11141120 | tf_op jit(solution)/shard_map/pallas_call | solution.py:478
  60.1 4.1 %collective-permute-done.6.refs_1_ = bf16[256,1024]{1,0:T(8,128)(2,1)S(1)} collective-permute-done((bf16[256,1024]{1,0:T(8,128)(2,1)S(1)}, bf16[256,1024]{1,0:T(8,128)(2,1)S(1)}, u32[]{:S(2)}, u32[]{:S(2)}) %collective-permute-start.6) | collective-permute-done | bytes 524320 | tf_op jit(solution)/shard_map/ppermute | solution.py:193
  64.2 3.6 %shard_map.76 = (bf16[128,1024]{1,0:T(8,128)(2,1)S(1)}, bf16[128,128]{1,0:T(8,128)(2,1)}, bf16[128,128]{1,0:T(8,128)(2,1)}) custom-call(s32[1,4]{1,0:T(1,128)S(1)} %copy-done.2, bf16[256,1024]{1,0:T(8,128)(2,1)S(1)} %collective-permute-done.6.refs_1_, f32[64,128]{1,0:T(8,128)S(1)} %bitcast.12, f32[256,128]{1,0:T(8,128)S(1)} %broadcast_in_dim.33.factor.refs_3_, ...), custom_call_target="tpu_custom_call" | custom-call | flops 1342177280 | bytes 11141120 | tf_op jit(solution)/shard_map/pallas_call | solution.py:478
  67.9 1.7 %collective-permute-start.19 = (bf16[256,1024]{1,0:T(8,128)(2,1)S(1)}, bf16[256,1024]{1,0:T(8,128)(2,1)S(1)}, u32[]{:S(2)}, u32[]{:S(2)}) collective-permute-start(bf16[256,1024]{1,0:T(8,128)(2,1)S(1)} %pad_maximum_fusion.3), channel_id=1, source_target_pairs={{0,2},{1,5},{2,0},{3,7},{4,8},{5,1},{6,10},{7,3},{8,4},{9,13},{10,... | collective-permute-start | bytes 1572872 | tf_op jit(solution)/shard_map/ppermute | solution.py:193
  69.5 7.4 %collective-permute-done.14.b1 = bf16[128,1024]{1,0:T(8,128)(2,1)S(1)} collective-permute-done((bf16[128,1024]{1,0:T(8,128)(2,1)S(1)}, bf16[128,1024]{1,0:T(8,128)(2,1)S(1)}, u32[]{:S(2)}, u32[]{:S(2)}) %collective-permute-start.14) | collective-permute-done | bytes 262176 | tf_op jit(solution)/shard_map/ppermute | solution.py:193
  77.0 1.6 %collective-permute-start.15 = (bf16[256,1024]{1,0:T(8,128)(2,1)S(1)}, bf16[256,1024]{1,0:T(8,128)(2,1)S(1)}, u32[]{:S(2)}, u32[]{:S(2)}) collective-permute-start(bf16[256,1024]{1,0:T(8,128)(2,1)S(1)} %pad_maximum_fusion.2), channel_id=1, source_target_pairs={{0,2},{1,5},{2,0},{3,7},{4,8},{5,1},{6,10},{7,3},{8,4},{9,13},{10,... | collective-permute-start | bytes 1572872 | tf_op jit(solution)/shard_map/ppermute | solution.py:193
  79.1 12.8 %collective-permute-done.15.b2 = bf16[256,1024]{1,0:T(8,128)(2,1)S(1)} collective-permute-done((bf16[256,1024]{1,0:T(8,128)(2,1)S(1)}, bf16[256,1024]{1,0:T(8,128)(2,1)S(1)}, u32[]{:S(2)}, u32[]{:S(2)}) %collective-permute-start.15) | collective-permute-done | bytes 524320 | tf_op jit(solution)/shard_map/ppermute | solution.py:193
  91.9 8.1 %shard_map.77 = (f32[256,1024]{1,0:T(8,128)S(1)}, bf16[1024,4096]{1,0:T(8,128)(2,1)S(1)}) custom-call(bf16[128,1024]{1,0:T(8,128)(2,1)S(1)} %get-tuple-element.32.a0, bf16[128,1024]{1,0:T(8,128)(2,1)S(1)} %get-tuple-element.31.b0, bf16[128,1024]{1,0:T(8,128)(2,1)S(1)} %collective-permute-done.18.a1, bf16[128,1024]{1,0:T(8,128)(2,1)S(1)} %collective-permute-done.14.b1, ...), custom_call_target="tpu_custom_call" | custom-call | flops 2147483648 | bytes 9437184 | tf_op jit(solution)/shard_map/pallas_call | solution.py:499
  100.0 1.7 %collective-permute-start.22 = (bf16[256,1024]{1,0:T(8,128)(2,1)S(1)}, bf16[256,1024]{1,0:T(8,128)(2,1)S(1)}, u32[]{:S(2)}, u32[]{:S(2)}) collective-permute-start(bf16[256,1024]{1,0:T(8,128)(2,1)S(1)} %collective-permute-done.20.a3), channel_id=1, source_target_pairs={{0,2},{1,5},{2,0},{3,7},{4,8},{5,1},{6,10},{7,3},{8,4},{9,13},{10,... | collective-permute-start | bytes 1572872 | tf_op jit(solution)/shard_map/ppermute | solution.py:193
  101.7 5.0 %collective-permute-done.16.b3 = bf16[256,1024]{1,0:T(8,128)(2,1)S(1)} collective-permute-done((bf16[256,1024]{1,0:T(8,128)(2,1)S(1)}, bf16[256,1024]{1,0:T(8,128)(2,1)S(1)}, u32[]{:S(2)}, u32[]{:S(2)}) %collective-permute-start.16) | collective-permute-done | bytes 524320 | tf_op jit(solution)/shard_map/ppermute | solution.py:193
  109.5 2.2 %shard_map.79.refs_4_ = bf16[256,1024]{1,0:T(8,128)(2,1)} custom-call(bf16[256,1024]{1,0:T(8,128)(2,1)S(1)} %collective-permute-done.22.refs_0_, bf16[256,1024]{1,0:T(8,128)(2,1)S(1)} %copy-done, f32[256,1024]{1,0:T(8,128)S(1)} %shard_map.78.refs_2_, bf16[1024,4096]{1,0:T(8,128)(2,1)S(1)} %get-tuple-element.36.late.refs_3_), custom_call_target="tpu_custom_call" | custom-call | flops 1073741824 | bytes 8912896 | tf_op jit(solution)/shard_map/pallas_call | solution.py:522
  111.7 4.1 %collective-permute-done.17.refs_0_ = bf16[256,1024]{1,0:T(8,128)(2,1)S(1)} collective-permute-done((bf16[256,1024]{1,0:T(8,128)(2,1)S(1)}, bf16[256,1024]{1,0:T(8,128)(2,1)S(1)}, u32[]{:S(2)}, u32[]{:S(2)}) %collective-permute-start.17) | collective-permute-done | bytes 524320 | tf_op jit(solution)/shard_map/ppermute | solution.py:193
  115.9 2.2 %shard_map.80 = bf16[256,1024]{1,0:T(8,128)(2,1)} custom-call(bf16[256,1024]{1,0:T(8,128)(2,1)S(1)} %collective-permute-done.17.refs_0_, bf16[256,1024]{1,0:T(8,128)(2,1)S(1)} %copy-done, f32[256,1024]{1,0:T(8,128)S(1)} %shard_map.78.refs_2_, bf16[1024,4096]{1,0:T(8,128)(2,1)S(1)} %get-tuple-element.36.late.refs_3_, ...), custom_call_target="tpu_custom_call", output_to_operand_aliasing={{}: (4, {})} | custom-call | flops 1073741824 | bytes 8912896 | tf_op jit(solution)/shard_map/pallas_call | solution.py:522
  (51 shorter events, 17.4 us)
Async XLA Ops:
  0.0 36.3 %collective-permute-start.10 = (bf16[1024,4096]{1,0:T(8,128)(2,1)}, bf16[1024,4096]{1,0:T(8,128)(2,1)}, u32[]{:S(2)}, u32[]{:S(2)}) collective-permute-start(bf16[1024,4096]{1,0:T(8,128)(2,1)} %refs_0_.1), channel_id=1, source_target_pairs={{0,1},{1,0},{2,3},{3,2},{4,5},{5,4},{6,7},{7,6},{8,9},{9,8},{10,11... | collective-permute-start | bytes 25165832 | tf_op jit(solution)/shard_map/ppermute | solution.py:29
  0.5 91.4 %collective-permute-start.21 = (bf16[1024,4096]{1,0:T(8,128)(2,1)}, bf16[1024,4096]{1,0:T(8,128)(2,1)}, u32[]{:S(2)}, u32[]{:S(2)}) collective-permute-start(bf16[1024,4096]{1,0:T(8,128)(2,1)} %w0.1), channel_id=1, source_target_pairs={{0,1},{1,0},{2,3},{3,2},{4,5},{5,4},{6,7},{7,6},{8,9},{9,8},{10,11... | collective-permute-start | bytes 25165832 | tf_op jit(solution)/shard_map/ppermute | solution.py:29
  1.6 7.5 %collective-permute-start.7 = (bf16[128,1024]{1,0:T(8,128)(2,1)S(1)}, bf16[128,1024]{1,0:T(8,128)(2,1)S(1)}, u32[]{:S(2)}, u32[]{:S(2)}) collective-permute-start(bf16[128,1024]{1,0:T(8,128)(2,1)S(1)} %get-tuple-element.37.a0), channel_id=1, source_target_pairs={{0,4},{1,3},{2,6},{3,1},{4,0},{5,9},{6,2},{7,11},{8,12},{9,5},{10,... | collective-permute-start | bytes 786440 | tf_op jit(solution)/shard_map/ppermute | solution.py:193
  5.9 5.2 %collective-permute-start = (f32[2,128]{1,0:T(2,128)S(1)}, f32[2,128]{1,0:T(2,128)S(1)}, u32[]{:S(2)}, u32[]{:S(2)}) collective-permute-start(f32[2,128]{1,0:T(2,128)S(1)} %bitcast.14), channel_id=1, source_target_pairs={{0,2},{1,5},{2,0},{3,7},{4,6},{5,1},{6,4},{7,3},{8,10},{9,13},{10,... | collective-permute-start | bytes 3080 | tf_op jit(solution)/shard_map/ppermute | solution.py:406
  9.1 14.9 %collective-permute-start.8 = (bf16[256,1024]{1,0:T(8,128)(2,1)S(1)}, bf16[256,1024]{1,0:T(8,128)(2,1)}, u32[]{:S(2)}, u32[]{:S(2)}) collective-permute-start(bf16[256,1024]{1,0:T(8,128)(2,1)S(1)} %pad_maximum_fusion.1), channel_id=1, source_target_pairs={{0,2},{1,5},{2,0},{3,7},{4,8},{5,1},{6,10},{7,3},{8,4},{9,13},{10,... | collective-permute-start | bytes 1572872 | tf_op jit(solution)/shard_map/ppermute | solution.py:193
  11.1 3.6 %collective-permute-start.1 = (f32[2,128]{1,0:T(2,128)S(1)}, f32[2,128]{1,0:T(2,128)S(1)}, u32[]{:S(2)}, u32[]{:S(2)}) collective-permute-start(f32[2,128]{1,0:T(2,128)S(1)} %bitcast_add_fusion), channel_id=1, source_target_pairs={{0,4},{1,3},{2,6},{3,1},{4,0},{5,7},{6,2},{7,5},{8,12},{9,11},{10,... | collective-permute-start | bytes 3080 | tf_op jit(solution)/shard_map/ppermute | solution.py:406
  12.8 9.9 %collective-permute-start.3 = (bf16[128,1024]{1,0:T(8,128)(2,1)S(1)}, bf16[128,1024]{1,0:T(8,128)(2,1)S(1)}, u32[]{:S(2)}, u32[]{:S(2)}) collective-permute-start(bf16[128,1024]{1,0:T(8,128)(2,1)S(1)} %get-tuple-element.38.b0), channel_id=1, source_target_pairs={{0,4},{1,3},{2,6},{3,1},{4,0},{5,9},{6,2},{7,11},{8,12},{9,5},{10,... | collective-permute-start | bytes 786440 | tf_op jit(solution)/shard_map/ppermute | solution.py:193
  14.7 8.0 %collective-permute-start.2 = (f32[2,128]{1,0:T(2,128)S(1)}, f32[2,128]{1,0:T(2,128)S(1)}, u32[]{:S(2)}, u32[]{:S(2)}) collective-permute-start(f32[2,128]{1,0:T(2,128)S(1)} %fusion.5), channel_id=1, source_target_pairs={{0,8},{1,9},{2,10},{3,11},{4,12},{5,13},{6,14},{7,15},{8,0},{9,1},... | collective-permute-start | bytes 3080 | tf_op jit(solution)/shard_map/ppermute | solution.py:406
  22.7 11.4 %collective-permute-start.11 = (bf16[128,4096]{1,0:T(8,128)(2,1)}, bf16[128,4096]{1,0:T(8,128)(2,1)S(1)}, u32[]{:S(2)}, u32[]{:S(2)}) collective-permute-start(bf16[128,4096]{1,0:T(8,128)(2,1)} %refs_2_.1), channel_id=1, source_target_pairs={{0,1},{1,0},{2,3},{3,2},{4,5},{5,4},{6,7},{7,6},{8,9},{9,8},{10,11... | collective-permute-start | bytes 3145736 | tf_op jit(solution)/shard_map/ppermute | solution.py:29
  22.7 13.6 %collective-permute-start.12 = (bf16[128,4096]{1,0:T(8,128)(2,1)}, bf16[128,4096]{1,0:T(8,128)(2,1)S(1)}, u32[]{:S(2)}, u32[]{:S(2)}) collective-permute-start(bf16[128,4096]{1,0:T(8,128)(2,1)} %refs_4_.1), channel_id=1, source_target_pairs={{0,1},{1,0},{2,3},{3,2},{4,5},{5,4},{6,7},{7,6},{8,9},{9,8},{10,11... | collective-permute-start | bytes 3145736 | tf_op jit(solution)/shard_map/ppermute | solution.py:29
  24.0 9.5 %collective-permute-start.4 = (bf16[256,1024]{1,0:T(8,128)(2,1)}, bf16[256,1024]{1,0:T(8,128)(2,1)}, u32[]{:S(2)}, u32[]{:S(2)}) collective-permute-start(bf16[256,1024]{1,0:T(8,128)(2,1)} %pad_maximum_fusion), channel_id=1, source_target_pairs={{0,2},{1,5},{2,0},{3,7},{4,8},{5,1},{6,10},{7,3},{8,4},{9,13},{10,... | collective-permute-start | bytes 1572872 | tf_op jit(solution)/shard_map/ppermute | solution.py:193
  33.5 14.0 %collective-permute-start.9 = (bf16[256,1024]{1,0:T(8,128)(2,1)}, bf16[256,1024]{1,0:T(8,128)(2,1)S(1)}, u32[]{:S(2)}, u32[]{:S(2)}) collective-permute-start(bf16[256,1024]{1,0:T(8,128)(2,1)} %collective-permute-done.8.a2), channel_id=1, source_target_pairs={{0,4},{1,3},{2,6},{3,1},{4,0},{5,9},{6,2},{7,11},{8,12},{9,5},{10,... | collective-permute-start | bytes 1572872 | tf_op jit(solution)/shard_map/ppermute | solution.py:193
  34.1 14.6 %collective-permute-start.5 = (bf16[256,1024]{1,0:T(8,128)(2,1)}, bf16[256,1024]{1,0:T(8,128)(2,1)S(1)}, u32[]{:S(2)}, u32[]{:S(2)}) collective-permute-start(bf16[256,1024]{1,0:T(8,128)(2,1)} %collective-permute-done.4.b2), channel_id=1, source_target_pairs={{0,4},{1,3},{2,6},{3,1},{4,0},{5,9},{6,2},{7,11},{8,12},{9,5},{10,... | collective-permute-start | bytes 1572872 | tf_op jit(solution)/shard_map/ppermute | solution.py:193
  47.5 9.2 %collective-permute-start.13 = (bf16[256,1024]{1,0:T(8,128)(2,1)S(1)}, bf16[256,1024]{1,0:T(8,128)(2,1)S(1)}, u32[]{:S(2)}, u32[]{:S(2)}) collective-permute-start(bf16[256,1024]{1,0:T(8,128)(2,1)S(1)} %collective-permute-done.9.a3), channel_id=1, source_target_pairs={{0,2},{1,5},{2,0},{3,7},{4,8},{5,1},{6,10},{7,3},{8,4},{9,13},{10,... | collective-permute-start | bytes 1572872 | tf_op jit(solution)/shard_map/ppermute | solution.py:193
  48.7 15.5 %collective-permute-start.6 = (bf16[256,1024]{1,0:T(8,128)(2,1)S(1)}, bf16[256,1024]{1,0:T(8,128)(2,1)S(1)}, u32[]{:S(2)}, u32[]{:S(2)}) collective-permute-start(bf16[256,1024]{1,0:T(8,128)(2,1)S(1)} %collective-permute-done.5.b3), channel_id=1, source_target_pairs={{0,2},{1,5},{2,0},{3,7},{4,8},{5,1},{6,10},{7,3},{8,4},{9,13},{10,... | collective-permute-start | bytes 1572872 | tf_op jit(solution)/shard_map/ppermute | solution.py:193
  60.0 7.8 %collective-permute-start.18 = (bf16[128,1024]{1,0:T(8,128)(2,1)S(1)}, bf16[128,1024]{1,0:T(8,128)(2,1)S(1)}, u32[]{:S(2)}, u32[]{:S(2)}) collective-permute-start(bf16[128,1024]{1,0:T(8,128)(2,1)S(1)} %get-tuple-element.32.a0), channel_id=1, source_target_pairs={{0,4},{1,3},{2,6},{3,1},{4,0},{5,9},{6,2},{7,11},{8,12},{9,5},{10,... | collective-permute-start | bytes 786440 | tf_op jit(solution)/shard_map/ppermute | solution.py:193
  67.8 9.2 %collective-permute-start.14 = (bf16[128,1024]{1,0:T(8,128)(2,1)S(1)}, bf16[128,1024]{1,0:T(8,128)(2,1)S(1)}, u32[]{:S(2)}, u32[]{:S(2)}) collective-permute-start(bf16[128,1024]{1,0:T(8,128)(2,1)S(1)} %get-tuple-element.31.b0), channel_id=1, source_target_pairs={{0,4},{1,3},{2,6},{3,1},{4,0},{5,9},{6,2},{7,11},{8,12},{9,5},{10,... | collective-permute-start | bytes 786440 | tf_op jit(solution)/shard_map/ppermute | solution.py:193
  67.9 10.7 %collective-permute-start.19 = (bf16[256,1024]{1,0:T(8,128)(2,1)S(1)}, bf16[256,1024]{1,0:T(8,128)(2,1)S(1)}, u32[]{:S(2)}, u32[]{:S(2)}) collective-permute-start(bf16[256,1024]{1,0:T(8,128)(2,1)S(1)} %pad_maximum_fusion.3), channel_id=1, source_target_pairs={{0,2},{1,5},{2,0},{3,7},{4,8},{5,1},{6,10},{7,3},{8,4},{9,13},{10,... | collective-permute-start | bytes 1572872 | tf_op jit(solution)/shard_map/ppermute | solution.py:193
  77.0 14.9 %collective-permute-start.15 = (bf16[256,1024]{1,0:T(8,128)(2,1)S(1)}, bf16[256,1024]{1,0:T(8,128)(2,1)S(1)}, u32[]{:S(2)}, u32[]{:S(2)}) collective-permute-start(bf16[256,1024]{1,0:T(8,128)(2,1)S(1)} %pad_maximum_fusion.2), channel_id=1, source_target_pairs={{0,2},{1,5},{2,0},{3,7},{4,8},{5,1},{6,10},{7,3},{8,4},{9,13},{10,... | collective-permute-start | bytes 1572872 | tf_op jit(solution)/shard_map/ppermute | solution.py:193
  78.6 21.4 %collective-permute-start.20 = (bf16[256,1024]{1,0:T(8,128)(2,1)S(1)}, bf16[256,1024]{1,0:T(8,128)(2,1)S(1)}, u32[]{:S(2)}, u32[]{:S(2)}) collective-permute-start(bf16[256,1024]{1,0:T(8,128)(2,1)S(1)} %collective-permute-done.19.a2), channel_id=1, source_target_pairs={{0,4},{1,3},{2,6},{3,1},{4,0},{5,9},{6,2},{7,11},{8,12},{9,5},{10,... | collective-permute-start | bytes 1572872 | tf_op jit(solution)/shard_map/ppermute | solution.py:193
  91.9 14.8 %collective-permute-start.16 = (bf16[256,1024]{1,0:T(8,128)(2,1)S(1)}, bf16[256,1024]{1,0:T(8,128)(2,1)S(1)}, u32[]{:S(2)}, u32[]{:S(2)}) collective-permute-start(bf16[256,1024]{1,0:T(8,128)(2,1)S(1)} %collective-permute-done.15.b2), channel_id=1, source_target_pairs={{0,4},{1,3},{2,6},{3,1},{4,0},{5,9},{6,2},{7,11},{8,12},{9,5},{10,... | collective-permute-start | bytes 1572872 | tf_op jit(solution)/shard_map/ppermute | solution.py:193
  100.0 9.6 %copy-start = (bf16[256,1024]{1,0:T(8,128)(2,1)S(1)}, bf16[256,1024]{1,0:T(8,128)(2,1)}, u32[]{:S(2)}) copy-start(bf16[256,1024]{1,0:T(8,128)(2,1)} %refs_1_.3) | copy-start | bytes 1572868
  100.0 9.5 %collective-permute-start.22 = (bf16[256,1024]{1,0:T(8,128)(2,1)S(1)}, bf16[256,1024]{1,0:T(8,128)(2,1)S(1)}, u32[]{:S(2)}, u32[]{:S(2)}) collective-permute-start(bf16[256,1024]{1,0:T(8,128)(2,1)S(1)} %collective-permute-done.20.a3), channel_id=1, source_target_pairs={{0,2},{1,5},{2,0},{3,7},{4,8},{5,1},{6,10},{7,3},{8,4},{9,13},{10,... | collective-permute-start | bytes 1572872 | tf_op jit(solution)/shard_map/ppermute | solution.py:193
  106.7 9.2 %collective-permute-start.17 = (bf16[256,1024]{1,0:T(8,128)(2,1)S(1)}, bf16[256,1024]{1,0:T(8,128)(2,1)S(1)}, u32[]{:S(2)}, u32[]{:S(2)}) collective-permute-start(bf16[256,1024]{1,0:T(8,128)(2,1)S(1)} %collective-permute-done.16.b3), channel_id=1, source_target_pairs={{0,2},{1,5},{2,0},{3,7},{4,8},{5,1},{6,10},{7,3},{8,4},{9,13},{10,... | collective-permute-start | bytes 1572872 | tf_op jit(solution)/shard_map/ppermute | solution.py:193
  (2 other events, 10.0 us)
where the time goes:
time: 118 us
  waiting for transfers between devices  54.6 us (46%)
  Pallas kernels  32.8 us (28%)
  starting transfers between devices  24.2 us (21%)
  other arithmetic  4.3 us (4%)
  local copies, waits for them, and re-layouts  1.92 us (2%)
    ppermute x16, waiting for transfers between devices, swapped(): return lax.ppermute(shard, ('tp', 'pair'), ring_swap(later))  47.3 us
    ppermute x16, starting transfers between devices, swapped(): return lax.ppermute(shard, ('tp', 'pair'), ring_swap(later))  17.8 us
    pallas_call x1, Pallas kernels, ring_layer(): kernel_call(early_kernel, out_shape=(acc_shape, jax.ShapeDtypeStruct((qkv...  10.5 us
    pallas_call x1, Pallas kernels, ring_layer(): kernel_call(out_early_kernel, out_shape=(acc_shape, jax.ShapeDtypeStruct(...  8.05 us
    ppermute x3, waiting for transfers between devices, summed_over_tp(): value = value + lax.ppermute(value, ('tp', 'pair'), pairs)  7.37 us
    pallas_call x2, Pallas kernels, last(): kernel_call(lambda *refs: last_kernel(half, *refs), out_shape=(jax.ShapeD...  6.82 us
    ppermute x3, starting transfers between devices, summed_over_tp(): value = value + lax.ppermute(value, ('tp', 'pair'), pairs)  5.36 us
    pallas_call x2, Pallas kernels, out_last(): kernel_call(lambda *refs: out_last_kernel(half, *refs), grid=(1,), out_sh...  4.42 us
  transfers between devices with their start and end apart: 23, of which 10 were waited for; matrix products, arithmetic and copies ran while one was open for 5% of the time, Pallas kernels for 26%

commit v1 on v0

--- a/solution.py
+++ b/solution.py
@@ -210,37 +210,36 @@
     return mine, pl.ds(pl.multiple_of(t % (RING // 2) * UNIT, UNIT), UNIT)
 
 
-def copy_either(own, other, rows, index, target, sem):
-    mine, cols = columns_of(index)
-
-    @pl.when(mine)
-    def _():
-        pltpu.make_async_copy(own.at[rows, cols], target, sem).start()
-
-    @pl.when(jnp.logical_not(mine))
-    def _():
-        pltpu.make_async_copy(other.at[rows, cols], target, sem).start()
-
-
-def contract_units(xs, acc, weights, buf, sems, count):
-    for u in range(count):
-        prefetch(weights, buf, sems, 0, u, False)
-        columns = slice(u * UNIT, (u + 1) * UNIT)
-        product = contract(xs[:, columns], buf[:, columns])
-        acc[...] = product if u == 0 else acc[...] + product
-
-
-def prefetch(weights, target, sems, first, u, go):
+def add_units(xs, acc, own, others, first, count):
+    def unit_step(u, carry):
+        mine, cols = columns_of(first + u)
+        for here, parts in ((mine, (own,)), (jnp.logical_not(mine), others)):
+
+            @pl.when(here)
+            def _(parts=parts):
+                at = 0
+                for part in parts:
+                    rows = part.shape[0]
+                    acc[:, at : at + rows] += contract(xs[u], part[:, cols])
+                    at += rows
+
+        return carry
+
+    lax.fori_loop(0, count, unit_step, 0)
+
+
+def load_kernel(*refs):
+    *sources, target, sems = refs
+    copies = []
     at = 0
-    for n, (own, other) in enumerate(weights):
-        rows = own.shape[0]
-        where = target.at[pl.ds(at, rows), pl.ds(u * UNIT, UNIT)]
-        if go:
-            copy_either(own, other, pl.ds(0, rows), first + u, where, sems.at[n, u])
-        else:
-            source = own.at[:, pl.ds(0, UNIT)]
-            pltpu.make_async_copy(source, where, sems.at[n, u]).wait()
+    for n, source in enumerate(sources):
+        rows = source.shape[0]
+        copies.append(pltpu.make_async_copy(source, target.at[pl.ds(at, rows), :], sems.at[n]))
         at += rows
+    for copy in copies:
+        copy.start()
+    for copy in copies:
+        copy.wait()
 
 
 def normed_unit(part, factor, gain_ref, index):
@@ -255,8 +254,7 @@
 
 def place_unit(xs, rows, n, part, factor, gain, index):
     for k, lane in enumerate(normed_unit(part, factor, gain, index)):
-        at = n * UNIT + k * 128
-        xs[rows, at : at + 128] = lane
+        xs[n, rows, k * 128 : (k + 1) * 128] = lane
 
 
 VM = pl.BlockSpec(memory_space=pltpu.VMEM)
@@ -276,30 +274,12 @@
     )
 
 
-def paired(refs):
-    return tuple((refs[n], refs[n + 1]) for n in range(0, len(refs), 2))
-
-
-def unit_scratch(count, width, kinds):
-    return [
-        pltpu.VMEM((STRETCH, count * UNIT), jnp.bfloat16),
-        pltpu.VMEM((width, count * UNIT), jnp.bfloat16),
-        pltpu.SemaphoreType.DMA((kinds, count)),
-        pltpu.SemaphoreType.DMA((kinds, count)),
-    ]
-
-
 def stream_rows(s):
     return slice(s * ROWS, (s + 1) * ROWS)
 
 
 def early_kernel(a0, b0, a1, b1, a2, b2, gain, factor, *refs):
-    *weights, acc, late, xs, buf, sems, late_sems = refs
-    weights = paired(weights)
-    for u in range(4):
-        prefetch(weights, buf, sems, 0, u, True)
-    for u in range(4):
-        prefetch(weights, late, late_sems, 4, u, True)
+    *weights, acc, xs = refs
     for s, (own, first, second) in enumerate(((a0, a1, a2), (b0, b1, b2))):
         rows = stream_rows(s)
         scale = factor[rows, :]
@@ -307,17 +287,18 @@
         place_unit(xs, rows, 1, first[...], scale, gain, 1)
         place_unit(xs, rows, 2, second[:ROWS, :], scale, gain, 2)
         place_unit(xs, rows, 3, second[ROWS:, :], scale, gain, 3)
-    contract_units(xs, acc, weights, buf, sems, 4)
-    for u in range(4):
-        prefetch(weights, late, late_sems, 4, u, False)
-
-
-def middle_kernel(a3, b3, gain, factor, acc_in, late, acc, xs):
+    acc[...] = jnp.zeros_like(acc)
+    add_units(xs, acc, weights[0], weights[1:], 0, 4)
+
+
+def middle_kernel(a3, b3, gain, factor, acc_in, *refs):
+    *weights, acc, xs = refs
     for s, ref in enumerate((a3, b3)):
         for n in range(2):
             part = ref[n * ROWS : (n + 1) * ROWS, :]
             place_unit(xs, stream_rows(s), n, part, factor[stream_rows(s), :], gain, 4 + n)
-    acc[...] = acc_in[...] + contract(xs[...], late[:, : 2 * UNIT])
+    acc[...] = acc_in[...]
+    add_units(xs, acc, weights[0], weights[1:], 4, 2)
 
 
 def turned_heads(part, cosine, sine):
@@ -326,16 +307,17 @@
     return (part * cosine + other * sine).astype(jnp.bfloat16)
 
 
-def last_kernel(half, lens, new, gain, factor, acc_in, late, cosine, sine, *refs):
+def last_kernel(half, lens, new, gain, factor, acc_in, cosine, sine, *refs):
     if half:
         key_early, value_early = refs[:2]
         refs = refs[2:]
-    attended, key_out, value_out, xs, acc = refs
+    *weights, attended, key_out, value_out, xs, acc = refs
     rows = stream_rows(half)
     for n in range(2):
         part = new[n * ROWS : (n + 1) * ROWS, :]
         place_unit(xs, slice(0, ROWS), n, part, factor[rows, :], gain, 6 + n)
-    acc[...] = acc_in[rows, :] + contract(xs[...], late[:, 2 * UNIT :])
+    acc[...] = acc_in[rows, :]
+    add_units(xs, acc, weights[0], weights[1:], 6, 2)
     heads = UNIT // HD
     cos, sin = cosine[rows, :], sine[rows, :]
     key = turned_heads(acc[:, UNIT : UNIT + HD], cos, sin)
@@ -367,37 +349,32 @@
         attended[:, h * HD : (h + 1) * HD] = out[h * ROWS : (h + 1) * ROWS, :]
 
 
-def out_early_kernel(a0, b0, a1, b1, a2, b2, w0, w1, acc, late, xs, buf, sems, late_sems):
-    weights = ((w0, w1),)
-    for u in range(4):
-        prefetch(weights, buf, sems, 0, u, True)
-    for u in range(4):
-        prefetch(weights, late, late_sems, 4, u, True)
+def out_early_kernel(a0, b0, a1, b1, a2, b2, w0, w1, acc, xs):
     for s, (own, first, second) in enumerate(((a0, a1, a2), (b0, b1, b2))):
         rows = stream_rows(s)
-        xs[rows, 0:UNIT] = own[...]
-        xs[rows, UNIT : 2 * UNIT] = first[...]
-        xs[rows, 2 * UNIT : 3 * UNIT] = second[:ROWS, :]
-        xs[rows, 3 * UNIT :] = second[ROWS:, :]
-    contract_units(xs, acc, weights, buf, sems, 4)
-    for u in range(4):
-        prefetch(weights, late, late_sems, 4, u, False)
-
-
-def out_middle_kernel(a3, b3, acc_in, late, acc, xs):
+        xs[0, rows, :] = own[...]
+        xs[1, rows, :] = first[...]
+        xs[2, rows, :] = second[:ROWS, :]
+        xs[3, rows, :] = second[ROWS:, :]
+    acc[...] = jnp.zeros_like(acc)
+    add_units(xs, acc, w0, (w1,), 0, 4)
+
+
+def out_middle_kernel(a3, b3, acc_in, w0, w1, acc, xs):
     for s, ref in enumerate((a3, b3)):
-        xs[stream_rows(s), :UNIT] = ref[:ROWS, :]
-        xs[stream_rows(s), UNIT:] = ref[ROWS:, :]
-    acc[...] = acc_in[...] + contract(xs[...], late[:, : 2 * UNIT])
-
-
-def out_last_kernel(half, new, hidden, acc_in, late, *refs):
-    out = refs[-1]
-    total = acc_in[stream_rows(half), :]
-    for u in range(2):
-        part = new[u * ROWS : (u + 1) * ROWS, :]
-        total = total + contract(part, late[:, (u + 2) * UNIT : (u + 3) * UNIT])
-    out[...] = (hidden[...].astype(jnp.float32) + total).astype(jnp.bfloat16)
+        xs[0, stream_rows(s), :] = ref[:ROWS, :]
+        xs[1, stream_rows(s), :] = ref[ROWS:, :]
+    acc[...] = acc_in[...]
+    add_units(xs, acc, w0, (w1,), 4, 2)
+
+
+def out_last_kernel(half, new, hidden, acc_in, w0, w1, *refs):
+    out, xs, acc = refs[-3:]
+    xs[0] = new[:ROWS, :]
+    xs[1] = new[ROWS:, :]
+    acc[...] = acc_in[stream_rows(half), :] + hidden[...].astype(jnp.float32)
+    add_units(xs, acc, w0, (w1,), 6, 2)
+    out[...] = acc[...].astype(jnp.bfloat16)
 
 
 def summed_over_tp(value):
@@ -411,12 +388,30 @@
     return pl.pallas_call(kernel, **options)
 
 
-def in_hbm(value):
-    return pltpu.with_memory_space_constraint(value, pltpu.HBM)
-
-
 def in_vmem(value):
     return pltpu.with_memory_space_constraint(value, pltpu.VMEM)
+
+
+def load(arrays):
+    rows = sum(w.shape[0] for w in arrays)
+    return kernel_call(
+        load_kernel,
+        out_shape=jax.ShapeDtypeStruct((rows, arrays[0].shape[1]), arrays[0].dtype),
+        in_specs=[HBM] * len(arrays),
+        out_specs=VM,
+        scratch_shapes=[pltpu.SemaphoreType.DMA((len(arrays),))],
+        compiler_params=params(2),
+        cost_estimate=cost(0, rows * arrays[0].shape[1] // UNIT, 1),
+    )(*(pltpu.with_memory_space_constraint(w, pltpu.HBM) for w in arrays))
+
+
+def token_position(lengths):
+    count = lengths.shape[0]
+    upto = jnp.arange(count)[:, None] >= jnp.arange(count)[None, :]
+    ends = jnp.sum(jnp.where(upto, lengths[None, :], 0), axis=1)
+    offsets = jnp.arange(STRETCH, dtype=jnp.int32)
+    finished = ends[None, :] <= offsets[:, None]
+    return offsets - jnp.sum(jnp.where(finished, lengths[None, :], 0), axis=1)
 
 
 def after(value, *others):
@@ -431,34 +426,36 @@
     f32, bf16 = jnp.float32, jnp.bfloat16
     a0, b0 = hidden_in[:ROWS], hidden_in[ROWS:]
     a1, b1 = swapped(a0, 0), swapped(b0, 0)
-    weights = []
-    for w in (key_weight, value_weight, query_weight):
-        weights = [in_hbm(w), in_vmem(partner(w, "pair", 0))] + weights
-    weights = weights[:2] + weights[4:] + weights[2:4]
-    qkv = sum(w.shape[0] for w in weights[::2])
+    projections = (query_weight, key_weight, value_weight)
+    others = [in_vmem(partner(w, "pair", 0)) for w in projections]
+    qkv = sum(w.shape[0] for w in projections)
     stream = hidden_in.astype(f32)
     squares = jnp.sum(stream * stream, axis=1).reshape(2, 128)
-    factor = lax.rsqrt(summed_over_tp(squares) / (RING * UNIT) + 1e-05)
+    squares = summed_over_tp(squares)
+    factor = lax.rsqrt(squares / (RING * UNIT) + 1e-05)
     factor = jnp.broadcast_to(factor.reshape(STRETCH, 1), (STRETCH, 128))
     a2 = swapped(jnp.concatenate([a0, a1], axis=0), 1)
     b2 = swapped(jnp.concatenate([b0, b1], axis=0), 1)
     gain = norm_gain.reshape(RING * UNIT // 128, 128)
-    _, position = token_layout(lengths)
+    position = token_position(lengths[0])
     lane = jnp.arange(HD, dtype=jnp.int32)
-    angle = position.reshape(-1).astype(f32)[:, None] * scaled_freq(lane - lane % 2)[None, :]
+    angle = position.astype(f32)[:, None] * scaled_freq(lane - lane % 2)[None, :]
     cosine = jnp.cos(angle)
     sine = jnp.sin(angle) * jnp.where(lane % 2 == 0, -1.0, 1.0)[None, :]
+    own = load(projections)
+    a2, own = after(a2, own)
+    weights = (own, *others)
     a3, b3 = swapped(a2, 0), swapped(b2, 0)
 
     factor, cosine, sine, lengths = after(factor, cosine, sine, lengths)
     acc_shape = jax.ShapeDtypeStruct((STRETCH, qkv), f32)
-    acc, late = kernel_call(
+    acc = kernel_call(
         early_kernel,
-        out_shape=(acc_shape, jax.ShapeDtypeStruct((qkv, 4 * UNIT), bf16)),
-        in_specs=[VM] * 8 + [HBM, VM] * 3,
-        out_specs=(VM, VM),
-        scratch_shapes=unit_scratch(4, qkv, 3),
-        compiler_params=params(24),
+        out_shape=acc_shape,
+        in_specs=[VM] * 12,
+        out_specs=VM,
+        scratch_shapes=[pltpu.VMEM((4, STRETCH, UNIT), bf16)],
+        compiler_params=params(12),
         cost_estimate=cost(STRETCH, 4, qkv),
     )(a0, b0, a1, b1, a2, b2, gain, factor, *weights)
     a3, acc = after(a3, acc)
@@ -466,56 +463,57 @@
     acc = kernel_call(
         middle_kernel,
         out_shape=acc_shape,
-        in_specs=[VM] * 6,
+        in_specs=[VM] * 9,
         out_specs=VM,
-        scratch_shapes=[pltpu.VMEM((STRETCH, 2 * UNIT), bf16)],
-        compiler_params=params(16),
+        scratch_shapes=[pltpu.VMEM((2, STRETCH, UNIT), bf16)],
+        compiler_params=params(12),
         cost_estimate=cost(STRETCH, 2, qkv),
-    )(a3, b3, gain, factor, acc, late)
+    )(a3, b3, gain, factor, acc, *weights)
 
     def last(half, new, early):
         kv = jax.ShapeDtypeStruct((ROWS, HD), bf16)
         return kernel_call(
             lambda *refs: last_kernel(half, *refs),
             out_shape=(jax.ShapeDtypeStruct((ROWS, UNIT), bf16), kv, kv),
-            in_specs=[SM] + [VM] * (7 + len(early)),
+            in_specs=[SM] + [VM] * (10 + len(early)),
             out_specs=(VM, VM, VM),
-            scratch_shapes=[pltpu.VMEM((ROWS, 2 * UNIT), bf16), pltpu.VMEM((ROWS, qkv), f32)],
-            compiler_params=params(20),
+            scratch_shapes=[pltpu.VMEM((2, ROWS, UNIT), bf16), pltpu.VMEM((ROWS, qkv), f32)],
+            compiler_params=params(14),
             cost_estimate=cost(ROWS, 4, qkv),
-        )(lengths, new, gain, factor, acc, late, cosine, sine, *early)
+        )(lengths, new, gain, factor, acc, cosine, sine, *early, *weights)
 
     a0, key_a, value_a = last(0, a4, ())
     b0, _, _ = last(1, b4, (key_a, value_a))
 
     other_output = in_vmem(partner(output_weight, "pair", 0))
-    output_weight = in_hbm(output_weight)
     a1, b1 = swapped(a0, 0), swapped(b0, 0)
     a2 = swapped(jnp.concatenate([a0, a1], axis=0), 1)
     b2 = swapped(jnp.concatenate([b0, b1], axis=0), 1)
+    own = load((output_weight,))
+    a2, own = after(a2, own)
     a3, b3 = swapped(a2, 0), swapped(b2, 0)
     width = output_weight.shape[0]
     acc_shape = jax.ShapeDtypeStruct((STRETCH, width), f32)
-    acc, late = kernel_call(
+    acc = kernel_call(
         out_early_kernel,
-        out_shape=(acc_shape, jax.ShapeDtypeStruct((width, 4 * UNIT), bf16)),
-        in_specs=[VM] * 6 + [HBM, VM],
-        out_specs=(VM, VM),
-        scratch_shapes=unit_scratch(4, width, 1),
-        compiler_params=params(22),
+        out_shape=acc_shape,
+        in_specs=[VM] * 8,
+        out_specs=VM,
+        scratch_shapes=[pltpu.VMEM((4, STRETCH, UNIT), bf16)],
+        compiler_params=params(12),
         cost_estimate=cost(STRETCH, 4, width),
-    )(a0, b0, a1, b1, a2, b2, output_weight, other_output)
+    )(a0, b0, a1, b1, a2, b2, own, other_output)
     a3, acc = after(a3, acc)
     a4, b4 = swapped(a3, 1), swapped(b3, 1)
     acc = kernel_call(
         out_middle_kernel,
         out_shape=acc_shape,
-        in_specs=[VM] * 4,
+        in_specs=[VM] * 5,
         out_specs=VM,
-        scratch_shapes=[pltpu.VMEM((STRETCH, 2 * UNIT), bf16)],
-        compiler_params=params(16),
+        scratch_shapes=[pltpu.VMEM((2, STRETCH, UNIT), bf16)],
+        compiler_params=params(12),
         cost_estimate=cost(STRETCH, 2, width),
-    )(a3, b3, acc, late)
+    )(a3, b3, acc, own, other_output)
 
     def out_last(half, new, *partial):
         part = pl.BlockSpec((ROWS, UNIT), lambda i: (half, 0))
@@ -523,12 +521,13 @@
             lambda *refs: out_last_kernel(half, *refs),
             grid=(1,),
             out_shape=jax.ShapeDtypeStruct((STRETCH, UNIT), bf16),
-            in_specs=[VM, part, VM, VM] + [HBM] * half,
+            in_specs=[VM, part, VM, VM, VM] + [HBM] * half,
             out_specs=part,
-            input_output_aliases={4: 0} if half else {},
-            compiler_params=params(16),
+            scratch_shapes=[pltpu.VMEM((2, ROWS, UNIT), bf16), pltpu.VMEM((ROWS, width), f32)],
+            input_output_aliases={5: 0} if half else {},
+            compiler_params=params(12),
             cost_estimate=cost(ROWS, 4, width),
-        )(new, hidden_in, acc, late, *partial)
+        )(new, hidden_in, acc, own, other_output, *partial)
 
     return out_last(1, b4, out_last(0, a4))
 
@@ -548,6 +547,9 @@
         P(("group", "pair"), None),
     )
     body = ring_body if fits_ring(mesh) else general_body
-    return jax.shard_map(
+    step = jax.shard_map(
         body, mesh=mesh, in_specs=placed, out_specs=P(("group", "pair"), "tp"), check_vma=False
     )
+    if not fits_ring(mesh):
+        return step
+    return step

time: 118 us -> 123 us (1.042)
  waiting for transfers between devices: 54.6 us -> 63.2 us
  other arithmetic: 4.3 us -> 2.14 us
  starting transfers between devices: 24.2 us -> 22.9 us
    ppermute x16, waiting for transfers between devices: 47.3 us -> 55.9 us  [swapped(): return lax.ppermute(shard, ('tp', 'pair'), ring_swap(later))]
    pallas_call x4 -> x6, Pallas kernels: 21.6 us -> 19.6 us  [the longest x2 7.32 us: load(): kernel_call(load_kernel, out_shape=jax.ShapeDtypeStruct((rows, arrays[0]....]
    ppermute x16, starting transfers between devices: 17.8 us -> 16.4 us  [swapped(): return lax.ppermute(shard, ('tp', 'pair'), ring_swap(later))]
  transfers between devices with their start and end apart: 23 -> 23, of which waited for: 10 -> 11; matrix products, arithmetic and copies ran while one was open for 5% -> 3% of each run, Pallas kernels for 26% -> 25%
where the time goes in v1:
time: 123 us; the launch traced here: 122 us
  waiting for transfers between devices  63.2 us (51%)
  Pallas kernels  32.7 us (27%)
  starting transfers between devices  22.9 us (19%)
  other arithmetic  2.14 us (2%)
    ppermute x16, waiting for transfers between devices, swapped(): return lax.ppermute(shard, ('tp', 'pair'), ring_swap(later))  55.9 us
    ppermute x16, starting transfers between devices, swapped(): return lax.ppermute(shard, ('tp', 'pair'), ring_swap(later))  16.4 us
    pallas_call x2, Pallas kernels, last(): kernel_call(lambda *refs: last_kernel(half, *refs), out_shape=(jax.ShapeD...  8.04 us
    pallas_call x2, Pallas kernels, load(): kernel_call(load_kernel, out_shape=jax.ShapeDtypeStruct((rows, arrays[0]....  7.32 us
    ppermute x3, waiting for transfers between devices, summed_over_tp(): value = value + lax.ppermute(value, ('tp', 'pair'), pairs)  7.3 us
    ppermute x3, starting transfers between devices, summed_over_tp(): value = value + lax.ppermute(value, ('tp', 'pair'), pairs)  5.42 us
    pallas_call x2, Pallas kernels, out_last(): kernel_call(lambda *refs: out_last_kernel(half, *refs), grid=(1,), out_sh...  5.11 us
    pallas_call x1, Pallas kernels, ring_layer(): kernel_call(early_kernel, out_shape=acc_shape, in_specs=[VM] * 12, out_sp...  4.66 us
  transfers between devices with their start and end apart: 23, of which 11 were waited for; matrix products, arithmetic and copies ran while one was open for 3% of the time, Pallas kernels for 25%

profile of v1, /device:TPU:0, one launch (start us, length us, event | category | flops | bytes accessed | tf_op | source)
XLA Modules:
  0.0 122.3 jit_solution(3926268757790450474)
XLA Ops:
  1.6 3.1 %collective-permute-start.7 = (bf16[128,1024]{1,0:T(8,128)(2,1)S(1)}, bf16[128,1024]{1,0:T(8,128)(2,1)S(1)}, u32[]{:S(2)}, u32[]{:S(2)}) collective-permute-start(bf16[128,1024]{1,0:T(8,128)(2,1)S(1)} %get-tuple-element.37.a0), channel_id=1, source_target_pairs={{0,4},{1,3},{2,6},{3,1},{4,0},{5,9},{6,2},{7,11},{8,12},{9,5},{10,... | collective-permute-start | bytes 786440 | tf_op jit(solution)/shard_map/ppermute | solution.py:193
  9.1 2.0 %collective-permute-start.8 = (bf16[256,1024]{1,0:T(8,128)(2,1)S(1)}, bf16[256,1024]{1,0:T(8,128)(2,1)S(1)}, u32[]{:S(2)}, u32[]{:S(2)}) collective-permute-start(bf16[256,1024]{1,0:T(8,128)(2,1)S(1)} %pad_maximum_fusion.1), channel_id=1, source_target_pairs={{0,2},{1,5},{2,0},{3,7},{4,8},{5,1},{6,10},{7,3},{8,4},{9,13},{10,... | collective-permute-start | bytes 1572872 | tf_op jit(solution)/shard_map/ppermute | solution.py:193
  11.1 1.7 %collective-permute-start.1 = (f32[2,128]{1,0:T(2,128)S(1)}, f32[2,128]{1,0:T(2,128)S(1)}, u32[]{:S(2)}, u32[]{:S(2)}) collective-permute-start(f32[2,128]{1,0:T(2,128)S(1)} %bitcast_add_fusion), channel_id=1, source_target_pairs={{0,4},{1,3},{2,6},{3,1},{4,0},{5,7},{6,2},{7,5},{8,12},{9,11},{10,... | collective-permute-start | bytes 3080 | tf_op jit(solution)/shard_map/ppermute | solution.py:383
  14.7 2.2 %collective-permute-start.2 = (f32[2,128]{1,0:T(2,128)S(1)}, f32[2,128]{1,0:T(2,128)S(1)}, u32[]{:S(2)}, u32[]{:S(2)}) collective-permute-start(f32[2,128]{1,0:T(2,128)S(1)} %fusion.5), channel_id=1, source_target_pairs={{0,8},{1,9},{2,10},{3,11},{4,12},{5,13},{6,14},{7,15},{8,0},{9,1},... | collective-permute-start | bytes 3080 | tf_op jit(solution)/shard_map/ppermute | solution.py:383
  16.9 5.7 %collective-permute-done.2 = f32[2,128]{1,0:T(2,128)S(1)} collective-permute-done((f32[2,128]{1,0:T(2,128)S(1)}, f32[2,128]{1,0:T(2,128)S(1)}, u32[]{:S(2)}, u32[]{:S(2)}) %collective-permute-start.2) | collective-permute-done | bytes 1056 | tf_op jit(solution)/shard_map/ppermute | solution.py:383
  22.7 3.9 %shard_map.73.refs_0_.refs_7_.refs_9_ = bf16[1280,4096]{1,0:T(8,128)(2,1)S(1)} custom-call(bf16[1024,4096]{1,0:T(8,128)(2,1)} %refs_0_.2, bf16[128,4096]{1,0:T(8,128)(2,1)} %refs_1_.3, bf16[128,4096]{1,0:T(8,128)(2,1)} %refs_2_.1), custom_call_target="tpu_custom_call" | custom-call | bytes 10485760 | tf_op jit(solution)/shard_map/pallas_call | solution.py:397
  28.6 7.9 %collective-permute-done.4.b2 = bf16[256,1024]{1,0:T(8,128)(2,1)S(1)} collective-permute-done((bf16[256,1024]{1,0:T(8,128)(2,1)S(1)}, bf16[256,1024]{1,0:T(8,128)(2,1)S(1)}, u32[]{:S(2)}, u32[]{:S(2)}) %collective-permute-start.4) | collective-permute-done | bytes 524320 | tf_op jit(solution)/shard_map/ppermute | solution.py:193
  37.0 2.1 %collective-permute-start.5 = (bf16[256,1024]{1,0:T(8,128)(2,1)S(1)}, bf16[256,1024]{1,0:T(8,128)(2,1)S(1)}, u32[]{:S(2)}, u32[]{:S(2)}) collective-permute-start(bf16[256,1024]{1,0:T(8,128)(2,1)S(1)} %collective-permute-done.4.b2), channel_id=1, source_target_pairs={{0,4},{1,3},{2,6},{3,1},{4,0},{5,9},{6,2},{7,11},{8,12},{9,5},{10,... | collective-permute-start | bytes 1572872 | tf_op jit(solution)/shard_map/ppermute | solution.py:193
  39.3 4.7 %shard_map.74.acc_in = f32[256,1280]{1,0:T(8,128)S(1)} custom-call(bf16[128,1024]{1,0:T(8,128)(2,1)S(1)} %get-tuple-element.37.a0, bf16[128,1024]{1,0:T(8,128)(2,1)S(1)} %get-tuple-element.38.b0, bf16[128,1024]{1,0:T(8,128)(2,1)S(1)} %collective-permute-done.7.a1, bf16[128,1024]{1,0:T(8,128)(2,1)S(1)} %collective-permute-done.3.b1, ...), custom_call_target="tpu_custom_call" | custom-call | flops 2684354560 | bytes 11796480 | tf_op jit(solution)/shard_map/pallas_call | solution.py:452
  43.9 1.7 %collective-permute-done.9.a3 = bf16[256,1024]{1,0:T(8,128)(2,1)S(1)} collective-permute-done((bf16[256,1024]{1,0:T(8,128)(2,1)S(1)}, bf16[256,1024]{1,0:T(8,128)(2,1)S(1)}, u32[]{:S(2)}, u32[]{:S(2)}) %collective-permute-start.9) | collective-permute-done | bytes 524320 | tf_op jit(solution)/shard_map/ppermute | solution.py:193
  46.7 9.3 %collective-permute-done.5.b3 = bf16[256,1024]{1,0:T(8,128)(2,1)S(1)} collective-permute-done((bf16[256,1024]{1,0:T(8,128)(2,1)S(1)}, bf16[256,1024]{1,0:T(8,128)(2,1)S(1)}, u32[]{:S(2)}, u32[]{:S(2)}) %collective-permute-start.5) | collective-permute-done | bytes 524320 | tf_op jit(solution)/shard_map/ppermute | solution.py:193
  57.1 2.5 %shard_map.75.refs_4_ = f32[256,1280]{1,0:T(8,128)S(1)} custom-call(bf16[256,1024]{1,0:T(8,128)(2,1)S(1)} %collective-permute-done.9.a3, bf16[256,1024]{1,0:T(8,128)(2,1)S(1)} %collective-permute-done.5.b3, f32[64,128]{1,0:T(8,128)S(1)} %bitcast.9, f32[256,128]{1,0:T(8,128)S(1)} %broadcast_in_dim.45.factor.refs_3_, f32[256,1280]{1,0:T(8,128)S(1)} %shard_map.74.acc_in, ...), custom_call_target="tpu_custom_call" | custom-call | flops 1342177280 | bytes 6553600 | tf_op jit(solution)/shard_map/pallas_call | solution.py:463
  59.6 3.6 %shard_map.76 = (bf16[128,1024]{1,0:T(8,128)(2,1)S(1)}, bf16[128,128]{1,0:T(8,128)(2,1)S(1)}, bf16[128,128]{1,0:T(8,128)(2,1)S(1)}) custom-call(s32[1,4]{1,0:T(1,128)S(1)} %copy-done.2, bf16[256,1024]{1,0:T(8,128)(2,1)S(1)} %collective-permute-done.13.refs_1_, f32[64,128]{1,0:T(8,128)S(1)} %bitcast.10, f32[256,128]{1,0:T(8,128)S(1)} %broadcast_in_dim.45.factor.refs_3_, ...), custom_call_target="tpu_custom_call" | custom-call | flops 1342177280 | bytes 11141120 | tf_op jit(solution)/shard_map/pallas_call | solution.py:475
  63.3 4.0 %collective-permute-done.6.refs_1_ = bf16[256,1024]{1,0:T(8,128)(2,1)S(1)} collective-permute-done((bf16[256,1024]{1,0:T(8,128)(2,1)S(1)}, bf16[256,1024]{1,0:T(8,128)(2,1)S(1)}, u32[]{:S(2)}, u32[]{:S(2)}) %collective-permute-start.6) | collective-permute-done | bytes 524320 | tf_op jit(solution)/shard_map/ppermute | solution.py:193
  67.3 4.4 %shard_map.77 = (bf16[128,1024]{1,0:T(8,128)(2,1)S(1)}, bf16[128,128]{1,0:T(8,128)(2,1)}, bf16[128,128]{1,0:T(8,128)(2,1)}) custom-call(s32[1,4]{1,0:T(1,128)S(1)} %copy-done.2, bf16[256,1024]{1,0:T(8,128)(2,1)S(1)} %collective-permute-done.6.refs_1_, f32[64,128]{1,0:T(8,128)S(1)} %bitcast.11, f32[256,128]{1,0:T(8,128)S(1)} %broadcast_in_dim.45.factor.refs_3_, ...), custom_call_target="tpu_custom_call" | custom-call | flops 1342177280 | bytes 11141120 | tf_op jit(solution)/shard_map/pallas_call | solution.py:475
  72.9 8.0 %collective-permute-done.14.b1 = bf16[128,1024]{1,0:T(8,128)(2,1)S(1)} collective-permute-done((bf16[128,1024]{1,0:T(8,128)(2,1)S(1)}, bf16[128,1024]{1,0:T(8,128)(2,1)S(1)}, u32[]{:S(2)}, u32[]{:S(2)}) %collective-permute-start.14) | collective-permute-done | bytes 262176 | tf_op jit(solution)/shard_map/ppermute | solution.py:193
  82.0 3.4 %shard_map.78.w0.refs_3_ = bf16[1024,4096]{1,0:T(8,128)(2,1)S(1)} custom-call(bf16[1024,4096]{1,0:T(8,128)(2,1)} %refs_0_.5), custom_call_target="tpu_custom_call" | custom-call | bytes 8388608 | tf_op jit(solution)/shard_map/pallas_call | solution.py:397
  86.1 9.7 %collective-permute-done.15.b2 = bf16[256,1024]{1,0:T(8,128)(2,1)S(1)} collective-permute-done((bf16[256,1024]{1,0:T(8,128)(2,1)S(1)}, bf16[256,1024]{1,0:T(8,128)(2,1)S(1)}, u32[]{:S(2)}, u32[]{:S(2)}) %collective-permute-start.15) | collective-permute-done | bytes 524320 | tf_op jit(solution)/shard_map/ppermute | solution.py:193
  96.5 3.4 %shard_map.79.acc_in = f32[256,1024]{1,0:T(8,128)S(1)} custom-call(bf16[128,1024]{1,0:T(8,128)(2,1)S(1)} %get-tuple-element.32.a0, bf16[128,1024]{1,0:T(8,128)(2,1)S(1)} %get-tuple-element.31.b0, bf16[128,1024]{1,0:T(8,128)(2,1)S(1)} %collective-permute-done.18.a1, bf16[128,1024]{1,0:T(8,128)(2,1)S(1)} %collective-permute-done.14.b1, ...), custom_call_target="tpu_custom_call" | custom-call | flops 2147483648 | bytes 9437184 | tf_op jit(solution)/shard_map/pallas_call | solution.py:497
  100.7 9.9 %collective-permute-done.16.b3 = bf16[256,1024]{1,0:T(8,128)(2,1)S(1)} collective-permute-done((bf16[256,1024]{1,0:T(8,128)(2,1)S(1)}, bf16[256,1024]{1,0:T(8,128)(2,1)S(1)}, u32[]{:S(2)}, u32[]{:S(2)}) %collective-permute-start.16) | collective-permute-done | bytes 524320 | tf_op jit(solution)/shard_map/ppermute | solution.py:193
  111.6 1.7 %shard_map.80.refs_2_ = f32[256,1024]{1,0:T(8,128)S(1)} custom-call(bf16[256,1024]{1,0:T(8,128)(2,1)S(1)} %collective-permute-done.20.a3, bf16[256,1024]{1,0:T(8,128)(2,1)S(1)} %collective-permute-done.16.b3, f32[256,1024]{1,0:T(8,128)S(1)} %shard_map.79.acc_in, bf16[1024,4096]{1,0:T(8,128)(2,1)S(1)} %shard_map.78.w0.refs_3_, ...), custom_call_target="tpu_custom_call" | custom-call | flops 1073741824 | bytes 5242880 | tf_op jit(solution)/shard_map/pallas_call | solution.py:508
  113.4 2.6 %shard_map.81.refs_5_ = bf16[256,1024]{1,0:T(8,128)(2,1)} custom-call(bf16[256,1024]{1,0:T(8,128)(2,1)S(1)} %collective-permute-done.22.refs_0_, bf16[256,1024]{1,0:T(8,128)(2,1)S(1)} %copy-done, f32[256,1024]{1,0:T(8,128)S(1)} %shard_map.80.refs_2_, bf16[1024,4096]{1,0:T(8,128)(2,1)S(1)} %shard_map.78.w0.refs_3_, ...), custom_call_target="tpu_custom_call" | custom-call | flops 1073741824 | bytes 8912896 | tf_op jit(solution)/shard_map/pallas_call | solution.py:520
  116.0 3.8 %collective-permute-done.17.refs_0_ = bf16[256,1024]{1,0:T(8,128)(2,1)S(1)} collective-permute-done((bf16[256,1024]{1,0:T(8,128)(2,1)S(1)}, bf16[256,1024]{1,0:T(8,128)(2,1)S(1)}, u32[]{:S(2)}, u32[]{:S(2)}) %collective-permute-start.17) | collective-permute-done | bytes 524320 | tf_op jit(solution)/shard_map/ppermute | solution.py:193
  119.8 2.6 %shard_map.82 = bf16[256,1024]{1,0:T(8,128)(2,1)} custom-call(bf16[256,1024]{1,0:T(8,128)(2,1)S(1)} %collective-permute-done.17.refs_0_, bf16[256,1024]{1,0:T(8,128)(2,1)S(1)} %copy-done, f32[256,1024]{1,0:T(8,128)S(1)} %shard_map.80.refs_2_, bf16[1024,4096]{1,0:T(8,128)(2,1)S(1)} %shard_map.78.w0.refs_3_, ...), custom_call_target="tpu_custom_call", output_to_operand_aliasing={{}: (5, {})} | custom-call | flops 1073741824 | bytes 8912896 | tf_op jit(solution)/shard_map/pallas_call | solution.py:520
  (55 shorter events, 18.3 us)
Async XLA Ops:
  0.0 39.3 %collective-permute-start.10 = (bf16[1024,4096]{1,0:T(8,128)(2,1)}, bf16[1024,4096]{1,0:T(8,128)(2,1)S(1)}, u32[]{:S(2)}, u32[]{:S(2)}) collective-permute-start(bf16[1024,4096]{1,0:T(8,128)(2,1)} %refs_0_.2), channel_id=1, source_target_pairs={{0,1},{1,0},{2,3},{3,2},{4,5},{5,4},{6,7},{7,6},{8,9},{9,8},{10,11... | collective-permute-start | bytes 25165832 | tf_op jit(solution)/shard_map/ppermute | solution.py:29
  0.5 96.0 %collective-permute-start.21 = (bf16[1024,4096]{1,0:T(8,128)(2,1)}, bf16[1024,4096]{1,0:T(8,128)(2,1)S(1)}, u32[]{:S(2)}, u32[]{:S(2)}) collective-permute-start(bf16[1024,4096]{1,0:T(8,128)(2,1)} %refs_0_.5), channel_id=1, source_target_pairs={{0,1},{1,0},{2,3},{3,2},{4,5},{5,4},{6,7},{7,6},{8,9},{9,8},{10,11... | collective-permute-start | bytes 25165832 | tf_op jit(solution)/shard_map/ppermute | solution.py:29
  1.6 7.5 %collective-permute-start.7 = (bf16[128,1024]{1,0:T(8,128)(2,1)S(1)}, bf16[128,1024]{1,0:T(8,128)(2,1)S(1)}, u32[]{:S(2)}, u32[]{:S(2)}) collective-permute-start(bf16[128,1024]{1,0:T(8,128)(2,1)S(1)} %get-tuple-element.37.a0), channel_id=1, source_target_pairs={{0,4},{1,3},{2,6},{3,1},{4,0},{5,9},{6,2},{7,11},{8,12},{9,5},{10,... | collective-permute-start | bytes 786440 | tf_op jit(solution)/shard_map/ppermute | solution.py:193
  5.9 5.2 %collective-permute-start = (f32[2,128]{1,0:T(2,128)S(1)}, f32[2,128]{1,0:T(2,128)S(1)}, u32[]{:S(2)}, u32[]{:S(2)}) collective-permute-start(f32[2,128]{1,0:T(2,128)S(1)} %bitcast.14), channel_id=1, source_target_pairs={{0,2},{1,5},{2,0},{3,7},{4,6},{5,1},{6,4},{7,3},{8,10},{9,13},{10,... | collective-permute-start | bytes 3080 | tf_op jit(solution)/shard_map/ppermute | solution.py:383
  9.1 18.1 %collective-permute-start.8 = (bf16[256,1024]{1,0:T(8,128)(2,1)S(1)}, bf16[256,1024]{1,0:T(8,128)(2,1)S(1)}, u32[]{:S(2)}, u32[]{:S(2)}) collective-permute-start(bf16[256,1024]{1,0:T(8,128)(2,1)S(1)} %pad_maximum_fusion.1), channel_id=1, source_target_pairs={{0,2},{1,5},{2,0},{3,7},{4,8},{5,1},{6,10},{7,3},{8,4},{9,13},{10,... | collective-permute-start | bytes 1572872 | tf_op jit(solution)/shard_map/ppermute | solution.py:193
  11.1 3.6 %collective-permute-start.1 = (f32[2,128]{1,0:T(2,128)S(1)}, f32[2,128]{1,0:T(2,128)S(1)}, u32[]{:S(2)}, u32[]{:S(2)}) collective-permute-start(f32[2,128]{1,0:T(2,128)S(1)} %bitcast_add_fusion), channel_id=1, source_target_pairs={{0,4},{1,3},{2,6},{3,1},{4,0},{5,7},{6,2},{7,5},{8,12},{9,11},{10,... | collective-permute-start | bytes 3080 | tf_op jit(solution)/shard_map/ppermute | solution.py:383
  12.8 13.8 %collective-permute-start.3 = (bf16[128,1024]{1,0:T(8,128)(2,1)S(1)}, bf16[128,1024]{1,0:T(8,128)(2,1)S(1)}, u32[]{:S(2)}, u32[]{:S(2)}) collective-permute-start(bf16[128,1024]{1,0:T(8,128)(2,1)S(1)} %get-tuple-element.38.b0), channel_id=1, source_target_pairs={{0,4},{1,3},{2,6},{3,1},{4,0},{5,9},{6,2},{7,11},{8,12},{9,5},{10,... | collective-permute-start | bytes 786440 | tf_op jit(solution)/shard_map/ppermute | solution.py:193
  14.7 24.6 %copy-start.1 = (f32[8192]{0:T(1024)S(1)}, f32[8192]{0:T(1024)}, u32[]{:S(2)}) copy-start(f32[8192]{0:T(1024)} %param.8) | copy-start | bytes 98308
  14.7 7.9 %collective-permute-start.2 = (f32[2,128]{1,0:T(2,128)S(1)}, f32[2,128]{1,0:T(2,128)S(1)}, u32[]{:S(2)}, u32[]{:S(2)}) collective-permute-start(f32[2,128]{1,0:T(2,128)S(1)} %fusion.5), channel_id=1, source_target_pairs={{0,8},{1,9},{2,10},{3,11},{4,12},{5,13},{6,14},{7,15},{8,0},{9,1},... | collective-permute-start | bytes 3080 | tf_op jit(solution)/shard_map/ppermute | solution.py:383
  22.7 14.4 %collective-permute-start.11 = (bf16[128,4096]{1,0:T(8,128)(2,1)}, bf16[128,4096]{1,0:T(8,128)(2,1)S(1)}, u32[]{:S(2)}, u32[]{:S(2)}) collective-permute-start(bf16[128,4096]{1,0:T(8,128)(2,1)} %refs_1_.3), channel_id=1, source_target_pairs={{0,1},{1,0},{2,3},{3,2},{4,5},{5,4},{6,7},{7,6},{8,9},{9,8},{10,11... | collective-permute-start | bytes 3145736 | tf_op jit(solution)/shard_map/ppermute | solution.py:29
  26.6 12.6 %collective-permute-start.12 = (bf16[128,4096]{1,0:T(8,128)(2,1)S(1)}, bf16[128,4096]{1,0:T(8,128)(2,1)S(1)}, u32[]{:S(2)}, u32[]{:S(2)}) collective-permute-start(bf16[128,4096]{1,0:T(8,128)(2,1)S(1)} %copy-done.3), channel_id=1, source_target_pairs={{0,1},{1,0},{2,3},{3,2},{4,5},{5,4},{6,7},{7,6},{8,9},{9,8},{10,11... | collective-permute-start | bytes 3145736 | tf_op jit(solution)/shard_map/ppermute | solution.py:29
  27.2 9.2 %collective-permute-start.4 = (bf16[256,1024]{1,0:T(8,128)(2,1)S(1)}, bf16[256,1024]{1,0:T(8,128)(2,1)S(1)}, u32[]{:S(2)}, u32[]{:S(2)}) collective-permute-start(bf16[256,1024]{1,0:T(8,128)(2,1)S(1)} %pad_maximum_fusion), channel_id=1, source_target_pairs={{0,2},{1,5},{2,0},{3,7},{4,8},{5,1},{6,10},{7,3},{8,4},{9,13},{10,... | collective-permute-start | bytes 1572872 | tf_op jit(solution)/shard_map/ppermute | solution.py:193
  36.5 9.2 %collective-permute-start.9 = (bf16[256,1024]{1,0:T(8,128)(2,1)S(1)}, bf16[256,1024]{1,0:T(8,128)(2,1)S(1)}, u32[]{:S(2)}, u32[]{:S(2)}) collective-permute-start(bf16[256,1024]{1,0:T(8,128)(2,1)S(1)} %collective-permute-done.8.a2), channel_id=1, source_target_pairs={{0,4},{1,3},{2,6},{3,1},{4,0},{5,9},{6,2},{7,11},{8,12},{9,5},{10,... | collective-permute-start | bytes 1572872 | tf_op jit(solution)/shard_map/ppermute | solution.py:193
  37.0 19.0 %collective-permute-start.5 = (bf16[256,1024]{1,0:T(8,128)(2,1)S(1)}, bf16[256,1024]{1,0:T(8,128)(2,1)S(1)}, u32[]{:S(2)}, u32[]{:S(2)}) collective-permute-start(bf16[256,1024]{1,0:T(8,128)(2,1)S(1)} %collective-permute-done.4.b2), channel_id=1, source_target_pairs={{0,4},{1,3},{2,6},{3,1},{4,0},{5,9},{6,2},{7,11},{8,12},{9,5},{10,... | collective-permute-start | bytes 1572872 | tf_op jit(solution)/shard_map/ppermute | solution.py:193
  45.7 13.9 %collective-permute-start.13 = (bf16[256,1024]{1,0:T(8,128)(2,1)S(1)}, bf16[256,1024]{1,0:T(8,128)(2,1)S(1)}, u32[]{:S(2)}, u32[]{:S(2)}) collective-permute-start(bf16[256,1024]{1,0:T(8,128)(2,1)S(1)} %collective-permute-done.9.a3), channel_id=1, source_target_pairs={{0,2},{1,5},{2,0},{3,7},{4,8},{5,1},{6,10},{7,3},{8,4},{9,13},{10,... | collective-permute-start | bytes 1572872 | tf_op jit(solution)/shard_map/ppermute | solution.py:193
  56.0 11.3 %collective-permute-start.6 = (bf16[256,1024]{1,0:T(8,128)(2,1)S(1)}, bf16[256,1024]{1,0:T(8,128)(2,1)S(1)}, u32[]{:S(2)}, u32[]{:S(2)}) collective-permute-start(bf16[256,1024]{1,0:T(8,128)(2,1)S(1)} %collective-permute-done.5.b3), channel_id=1, source_target_pairs={{0,2},{1,5},{2,0},{3,7},{4,8},{5,1},{6,10},{7,3},{8,4},{9,13},{10,... | collective-permute-start | bytes 1572872 | tf_op jit(solution)/shard_map/ppermute | solution.py:193
  63.2 8.5 %collective-permute-start.18 = (bf16[128,1024]{1,0:T(8,128)(2,1)S(1)}, bf16[128,1024]{1,0:T(8,128)(2,1)S(1)}, u32[]{:S(2)}, u32[]{:S(2)}) collective-permute-start(bf16[128,1024]{1,0:T(8,128)(2,1)S(1)} %get-tuple-element.32.a0), channel_id=1, source_target_pairs={{0,4},{1,3},{2,6},{3,1},{4,0},{5,9},{6,2},{7,11},{8,12},{9,5},{10,... | collective-permute-start | bytes 786440 | tf_op jit(solution)/shard_map/ppermute | solution.py:193
  71.7 9.2 %collective-permute-start.14 = (bf16[128,1024]{1,0:T(8,128)(2,1)S(1)}, bf16[128,1024]{1,0:T(8,128)(2,1)S(1)}, u32[]{:S(2)}, u32[]{:S(2)}) collective-permute-start(bf16[128,1024]{1,0:T(8,128)(2,1)S(1)} %get-tuple-element.31.b0), channel_id=1, source_target_pairs={{0,4},{1,3},{2,6},{3,1},{4,0},{5,9},{6,2},{7,11},{8,12},{9,5},{10,... | collective-permute-start | bytes 786440 | tf_op jit(solution)/shard_map/ppermute | solution.py:193
  71.8 13.7 %collective-permute-start.19 = (bf16[256,1024]{1,0:T(8,128)(2,1)S(1)}, bf16[256,1024]{1,0:T(8,128)(2,1)S(1)}, u32[]{:S(2)}, u32[]{:S(2)}) collective-permute-start(bf16[256,1024]{1,0:T(8,128)(2,1)S(1)} %pad_maximum_fusion.3), channel_id=1, source_target_pairs={{0,2},{1,5},{2,0},{3,7},{4,8},{5,1},{6,10},{7,3},{8,4},{9,13},{10,... | collective-permute-start | bytes 1572872 | tf_op jit(solution)/shard_map/ppermute | solution.py:193
  80.9 14.9 %collective-permute-start.15 = (bf16[256,1024]{1,0:T(8,128)(2,1)S(1)}, bf16[256,1024]{1,0:T(8,128)(2,1)S(1)}, u32[]{:S(2)}, u32[]{:S(2)}) collective-permute-start(bf16[256,1024]{1,0:T(8,128)(2,1)S(1)} %pad_maximum_fusion.2), channel_id=1, source_target_pairs={{0,2},{1,5},{2,0},{3,7},{4,8},{5,1},{6,10},{7,3},{8,4},{9,13},{10,... | collective-permute-start | bytes 1572872 | tf_op jit(solution)/shard_map/ppermute | solution.py:193
  85.5 14.4 %collective-permute-start.20 = (bf16[256,1024]{1,0:T(8,128)(2,1)S(1)}, bf16[256,1024]{1,0:T(8,128)(2,1)S(1)}, u32[]{:S(2)}, u32[]{:S(2)}) collective-permute-start(bf16[256,1024]{1,0:T(8,128)(2,1)S(1)} %collective-permute-done.19.a2), channel_id=1, source_target_pairs={{0,4},{1,3},{2,6},{3,1},{4,0},{5,9},{6,2},{7,11},{8,12},{9,5},{10,... | collective-permute-start | bytes 1572872 | tf_op jit(solution)/shard_map/ppermute | solution.py:193
  95.8 14.8 %collective-permute-start.16 = (bf16[256,1024]{1,0:T(8,128)(2,1)S(1)}, bf16[256,1024]{1,0:T(8,128)(2,1)S(1)}, u32[]{:S(2)}, u32[]{:S(2)}) collective-permute-start(bf16[256,1024]{1,0:T(8,128)(2,1)S(1)} %collective-permute-done.15.b2), channel_id=1, source_target_pairs={{0,4},{1,3},{2,6},{3,1},{4,0},{5,9},{6,2},{7,11},{8,12},{9,5},{10,... | collective-permute-start | bytes 1572872 | tf_op jit(solution)/shard_map/ppermute | solution.py:193
  99.9 13.5 %collective-permute-start.22 = (bf16[256,1024]{1,0:T(8,128)(2,1)S(1)}, bf16[256,1024]{1,0:T(8,128)(2,1)S(1)}, u32[]{:S(2)}, u32[]{:S(2)}) collective-permute-start(bf16[256,1024]{1,0:T(8,128)(2,1)S(1)} %collective-permute-done.20.a3), channel_id=1, source_target_pairs={{0,2},{1,5},{2,0},{3,7},{4,8},{5,1},{6,10},{7,3},{8,4},{9,13},{10,... | collective-permute-start | bytes 1572872 | tf_op jit(solution)/shard_map/ppermute | solution.py:193
  110.6 9.2 %collective-permute-start.17 = (bf16[256,1024]{1,0:T(8,128)(2,1)S(1)}, bf16[256,1024]{1,0:T(8,128)(2,1)S(1)}, u32[]{:S(2)}, u32[]{:S(2)}) collective-permute-start(bf16[256,1024]{1,0:T(8,128)(2,1)S(1)} %collective-permute-done.16.b3), channel_id=1, source_target_pairs={{0,2},{1,5},{2,0},{3,7},{4,8},{5,1},{6,10},{7,3},{8,4},{9,13},{10,... | collective-permute-start | bytes 1572872 | tf_op jit(solution)/shard_map/ppermute | solution.py:193
  (3 other events, 39.2 us)

commit v2 on v1

--- a/solution.py
+++ b/solution.py
@@ -307,17 +307,21 @@
     return (part * cosine + other * sine).astype(jnp.bfloat16)
 
 
-def last_kernel(half, lens, new, gain, factor, acc_in, cosine, sine, *refs):
-    if half:
-        key_early, value_early = refs[:2]
-        refs = refs[2:]
-    *weights, attended, key_out, value_out, xs, acc = refs
+def project_kernel(half, new, gain, factor, acc_in, *refs):
+    *weights, acc, xs = refs
     rows = stream_rows(half)
     for n in range(2):
         part = new[n * ROWS : (n + 1) * ROWS, :]
         place_unit(xs, slice(0, ROWS), n, part, factor[rows, :], gain, 6 + n)
     acc[...] = acc_in[rows, :]
     add_units(xs, acc, weights[0], weights[1:], 6, 2)
+
+
+def attend_kernel(half, lens, acc, cosine, sine, *refs):
+    if half:
+        key_early, value_early = refs[:2]
+    attended, key_out, value_out = refs[-3:]
+    rows = stream_rows(half)
     heads = UNIT // HD
     cos, sin = cosine[rows, :], sine[rows, :]
     key = turned_heads(acc[:, UNIT : UNIT + HD], cos, sin)
@@ -360,19 +364,19 @@
     add_units(xs, acc, w0, (w1,), 0, 4)
 
 
-def out_middle_kernel(a3, b3, acc_in, w0, w1, acc, xs):
+def out_middle_kernel(a3, b3, acc_in, hidden, w0, w1, acc, xs):
     for s, ref in enumerate((a3, b3)):
         xs[0, stream_rows(s), :] = ref[:ROWS, :]
         xs[1, stream_rows(s), :] = ref[ROWS:, :]
-    acc[...] = acc_in[...]
+    acc[...] = acc_in[...] + hidden[...].astype(jnp.float32)
     add_units(xs, acc, w0, (w1,), 4, 2)
 
 
-def out_last_kernel(half, new, hidden, acc_in, w0, w1, *refs):
+def out_last_kernel(half, new, acc_in, w0, w1, *refs):
     out, xs, acc = refs[-3:]
     xs[0] = new[:ROWS, :]
     xs[1] = new[ROWS:, :]
-    acc[...] = acc_in[stream_rows(half), :] + hidden[...].astype(jnp.float32)
+    acc[...] = acc_in[stream_rows(half), :]
     add_units(xs, acc, w0, (w1,), 6, 2)
     out[...] = acc[...].astype(jnp.bfloat16)
 
@@ -427,7 +431,9 @@
     a0, b0 = hidden_in[:ROWS], hidden_in[ROWS:]
     a1, b1 = swapped(a0, 0), swapped(b0, 0)
     projections = (query_weight, key_weight, value_weight)
-    others = [in_vmem(partner(w, "pair", 0)) for w in projections]
+    others = []
+    for w in projections:
+        others.append(in_vmem(partner(w, "pair", 0)))
     qkv = sum(w.shape[0] for w in projections)
     stream = hidden_in.astype(f32)
     squares = jnp.sum(stream * stream, axis=1).reshape(2, 128)
@@ -442,6 +448,7 @@
     angle = position.astype(f32)[:, None] * scaled_freq(lane - lane % 2)[None, :]
     cosine = jnp.cos(angle)
     sine = jnp.sin(angle) * jnp.where(lane % 2 == 0, -1.0, 1.0)[None, :]
+    other_output = in_vmem(partner(output_weight, "pair", 0))
     own = load(projections)
     a2, own = after(a2, own)
     weights = (own, *others)
@@ -470,27 +477,36 @@
         cost_estimate=cost(STRETCH, 2, qkv),
     )(a3, b3, gain, factor, acc, *weights)
 
-    def last(half, new, early):
+    def project(half, new):
+        return kernel_call(
+            lambda *refs: project_kernel(half, *refs),
+            out_shape=jax.ShapeDtypeStruct((ROWS, qkv), f32),
+            in_specs=[VM] * 8,
+            out_specs=VM,
+            scratch_shapes=[pltpu.VMEM((2, ROWS, UNIT), bf16)],
+            compiler_params=params(12),
+            cost_estimate=cost(ROWS, 2, qkv),
+        )(new, gain, factor, acc, *weights)
+
+    def attend_stream(half, projected, early):
         kv = jax.ShapeDtypeStruct((ROWS, HD), bf16)
         return kernel_call(
-            lambda *refs: last_kernel(half, *refs),
+            lambda *refs: attend_kernel(half, *refs),
             out_shape=(jax.ShapeDtypeStruct((ROWS, UNIT), bf16), kv, kv),
-            in_specs=[SM] + [VM] * (10 + len(early)),
+            in_specs=[SM] + [VM] * (3 + len(early)),
             out_specs=(VM, VM, VM),
-            scratch_shapes=[pltpu.VMEM((2, ROWS, UNIT), bf16), pltpu.VMEM((ROWS, qkv), f32)],
-            compiler_params=params(14),
-            cost_estimate=cost(ROWS, 4, qkv),
-        )(lengths, new, gain, factor, acc, cosine, sine, *early, *weights)
-
-    a0, key_a, value_a = last(0, a4, ())
-    b0, _, _ = last(1, b4, (key_a, value_a))
-
-    other_output = in_vmem(partner(output_weight, "pair", 0))
-    a1, b1 = swapped(a0, 0), swapped(b0, 0)
+            compiler_params=params(12),
+            cost_estimate=cost(ROWS, 2, qkv),
+        )(lengths, projected, cosine, sine, *early)
+
+    a0, key_a, value_a = attend_stream(0, project(0, a4), ())
+    a1 = swapped(a0, 0)
+    projected = project(1, b4)
+    a1, projected = after(a1, projected)
     a2 = swapped(jnp.concatenate([a0, a1], axis=0), 1)
+    b0, _, _ = attend_stream(1, projected, (key_a, value_a))
+    b1 = swapped(b0, 0)
     b2 = swapped(jnp.concatenate([b0, b1], axis=0), 1)
-    own = load((output_weight,))
-    a2, own = after(a2, own)
     a3, b3 = swapped(a2, 0), swapped(b2, 0)
     width = output_weight.shape[0]
     acc_shape = jax.ShapeDtypeStruct((STRETCH, width), f32)
@@ -502,18 +518,18 @@
         scratch_shapes=[pltpu.VMEM((4, STRETCH, UNIT), bf16)],
         compiler_params=params(12),
         cost_estimate=cost(STRETCH, 4, width),
-    )(a0, b0, a1, b1, a2, b2, own, other_output)
+    )(a0, b0, a1, b1, a2, b2, output_weight, other_output)
     a3, acc = after(a3, acc)
     a4, b4 = swapped(a3, 1), swapped(b3, 1)
     acc = kernel_call(
         out_middle_kernel,
         out_shape=acc_shape,
-        in_specs=[VM] * 5,
+        in_specs=[VM] * 6,
         out_specs=VM,
         scratch_shapes=[pltpu.VMEM((2, STRETCH, UNIT), bf16)],
         compiler_params=params(12),
         cost_estimate=cost(STRETCH, 2, width),
-    )(a3, b3, acc, own, other_output)
+    )(a3, b3, acc, hidden_in, output_weight, other_output)
 
     def out_last(half, new, *partial):
         part = pl.BlockSpec((ROWS, UNIT), lambda i: (half, 0))
@@ -521,13 +537,13 @@
             lambda *refs: out_last_kernel(half, *refs),
             grid=(1,),
             out_shape=jax.ShapeDtypeStruct((STRETCH, UNIT), bf16),
-            in_specs=[VM, part, VM, VM, VM] + [HBM] * half,
+            in_specs=[VM, VM, VM, VM] + [HBM] * half,
             out_specs=part,
             scratch_shapes=[pltpu.VMEM((2, ROWS, UNIT), bf16), pltpu.VMEM((ROWS, width), f32)],
-            input_output_aliases={5: 0} if half else {},
+            input_output_aliases={4: 0} if half else {},
             compiler_params=params(12),
             cost_estimate=cost(ROWS, 4, width),
-        )(new, hidden_in, acc, own, other_output, *partial)
+        )(new, acc, output_weight, other_output, *partial)
 
     return out_last(1, b4, out_last(0, a4))
 

time: 123 us -> 119 us (0.967)
  Pallas kernels: 32.7 us -> 29.1 us
  starting transfers between devices: 22.9 us -> 21.3 us
  waiting for transfers between devices: 63.2 us -> 64.5 us
    ppermute x16, waiting for transfers between devices: 55.9 us -> 60.7 us  [swapped(): return lax.ppermute(shard, ('tp', 'pair'), ring_swap(later))]
    ppermute x3, waiting for transfers between devices: 7.3 us -> 3.82 us  [summed_over_tp(): value = value + lax.ppermute(value, ('tp', 'pair'), pairs)]
    pallas_call x2 -> x1, Pallas kernels: 7.32 us -> 3.93 us  [load(): kernel_call(load_kernel, out_shape=jax.ShapeDtypeStruct((rows, arrays[0]....]
    ppermute x16, starting transfers between devices: 16.4 us -> 14.6 us  [swapped(): return lax.ppermute(shard, ('tp', 'pair'), ring_swap(later))]
    pallas_call x3 -> x5, Pallas kernels: 9.78 us -> 9.72 us  [the longest x2 4.42 us: project(): kernel_call(lambda *refs: project_kernel(half, *refs), out_shape=jax.Shap...]
  transfers between devices with their start and end apart: 23 -> 23, of which waited for: 11 -> 10; matrix products, arithmetic and copies ran while one was open for 3% -> 3% of each run, Pallas kernels for 25% -> 22%
where the time goes in v2:
time: 119 us
  waiting for transfers between devices  64.5 us (54%)
  Pallas kernels  29.1 us (24%)
  starting transfers between devices  21.3 us (18%)
  other arithmetic  2.14 us (2%)
  local copies, waits for them, and re-layouts  1.19 us (1%)
    ppermute x16, waiting for transfers between devices, swapped(): return lax.ppermute(shard, ('tp', 'pair'), ring_swap(later))  60.7 us
    ppermute x16, starting transfers between devices, swapped(): return lax.ppermute(shard, ('tp', 'pair'), ring_swap(later))  14.6 us
    ppermute x3, starting transfers between devices, summed_over_tp(): value = value + lax.ppermute(value, ('tp', 'pair'), pairs)  5.7 us
    pallas_call x2, Pallas kernels, out_last(): kernel_call(lambda *refs: out_last_kernel(half, *refs), grid=(1,), out_sh...  5.05 us
    pallas_call x1, Pallas kernels, ring_layer(): kernel_call(early_kernel, out_shape=acc_shape, in_specs=[VM] * 12, out_sp...  4.54 us
    pallas_call x2, Pallas kernels, project(): kernel_call(lambda *refs: project_kernel(half, *refs), out_shape=jax.Shap...  4.42 us
    pallas_call x1, Pallas kernels, load(): kernel_call(load_kernel, out_shape=jax.ShapeDtypeStruct((rows, arrays[0]....  3.93 us
    ppermute x3, waiting for transfers between devices, summed_over_tp(): value = value + lax.ppermute(value, ('tp', 'pair'), pairs)  3.82 us
  transfers between devices with their start and end apart: 23, of which 10 were waited for; matrix products, arithmetic and copies ran while one was open for 3% of the time, Pallas kernels for 22%

profile of v2, /device:TPU:0, one launch (start us, length us, event | category | flops | bytes accessed | tf_op | source)
XLA Modules:
  0.0 118.6 jit_solution(15569686049889561828)
XLA Ops:
  1.6 3.1 %collective-permute-start.3 = (bf16[128,1024]{1,0:T(8,128)(2,1)S(1)}, bf16[128,1024]{1,0:T(8,128)(2,1)S(1)}, u32[]{:S(2)}, u32[]{:S(2)}) collective-permute-start(bf16[128,1024]{1,0:T(8,128)(2,1)S(1)} %get-tuple-element.38.a0), channel_id=1, source_target_pairs={{0,4},{1,3},{2,6},{3,1},{4,0},{5,9},{6,2},{7,11},{8,12},{9,5},{10,... | collective-permute-start | bytes 786440 | tf_op jit(solution)/shard_map/ppermute | solution.py:193
  9.1 2.0 %collective-permute-start.4 = (bf16[256,1024]{1,0:T(8,128)(2,1)S(1)}, bf16[256,1024]{1,0:T(8,128)(2,1)S(1)}, u32[]{:S(2)}, u32[]{:S(2)}) collective-permute-start(bf16[256,1024]{1,0:T(8,128)(2,1)S(1)} %pad_maximum_fusion), channel_id=1, source_target_pairs={{0,2},{1,5},{2,0},{3,7},{4,8},{5,1},{6,10},{7,3},{8,4},{9,13},{10,... | collective-permute-start | bytes 1572872 | tf_op jit(solution)/shard_map/ppermute | solution.py:193
  11.1 1.7 %collective-permute-start.1 = (f32[2,128]{1,0:T(2,128)S(1)}, f32[2,128]{1,0:T(2,128)S(1)}, u32[]{:S(2)}, u32[]{:S(2)}) collective-permute-start(f32[2,128]{1,0:T(2,128)S(1)} %bitcast_add_fusion), channel_id=1, source_target_pairs={{0,4},{1,3},{2,6},{3,1},{4,0},{5,7},{6,2},{7,5},{8,12},{9,11},{10,... | collective-permute-start | bytes 3080 | tf_op jit(solution)/shard_map/ppermute | solution.py:387
  12.8 3.8 %collective-permute-done.1 = f32[2,128]{1,0:T(2,128)S(1)} collective-permute-done((f32[2,128]{1,0:T(2,128)S(1)}, f32[2,128]{1,0:T(2,128)S(1)}, u32[]{:S(2)}, u32[]{:S(2)}) %collective-permute-start.1) | collective-permute-done | bytes 1056 | tf_op jit(solution)/shard_map/ppermute | solution.py:387
  16.6 2.5 %collective-permute-start.2 = (f32[2,128]{1,0:T(2,128)S(1)}, f32[2,128]{1,0:T(2,128)S(1)}, u32[]{:S(2)}, u32[]{:S(2)}) collective-permute-start(f32[2,128]{1,0:T(2,128)S(1)} %fusion.5), channel_id=1, source_target_pairs={{0,8},{1,9},{2,10},{3,11},{4,12},{5,13},{6,14},{7,15},{8,0},{9,1},... | collective-permute-start | bytes 3080 | tf_op jit(solution)/shard_map/ppermute | solution.py:387
  19.1 3.9 %shard_map.73.refs_0_.refs_4_ = bf16[1280,4096]{1,0:T(8,128)(2,1)S(1)} custom-call(bf16[1024,4096]{1,0:T(8,128)(2,1)} %refs_0_.1, bf16[128,4096]{1,0:T(8,128)(2,1)} %refs_1_.1, bf16[128,4096]{1,0:T(8,128)(2,1)} %refs_2_.3), custom_call_target="tpu_custom_call" | custom-call | bytes 10485760 | tf_op jit(solution)/shard_map/pallas_call | solution.py:401
  24.0 8.9 %collective-permute-done.7.b2 = bf16[256,1024]{1,0:T(8,128)(2,1)S(1)} collective-permute-done((bf16[256,1024]{1,0:T(8,128)(2,1)S(1)}, bf16[256,1024]{1,0:T(8,128)(2,1)S(1)}, u32[]{:S(2)}, u32[]{:S(2)}) %collective-permute-start.7) | collective-permute-done | bytes 524320 | tf_op jit(solution)/shard_map/ppermute | solution.py:193
  33.6 2.1 %collective-permute-start.12 = (bf16[256,1024]{1,0:T(8,128)(2,1)S(1)}, bf16[256,1024]{1,0:T(8,128)(2,1)S(1)}, u32[]{:S(2)}, u32[]{:S(2)}) collective-permute-start(bf16[256,1024]{1,0:T(8,128)(2,1)S(1)} %collective-permute-done.7.b2), channel_id=1, source_target_pairs={{0,4},{1,3},{2,6},{3,1},{4,0},{5,9},{6,2},{7,11},{8,12},{9,5},{10,... | collective-permute-start | bytes 1572872 | tf_op jit(solution)/shard_map/ppermute | solution.py:193
  35.7 4.5 %shard_map.74.acc_in = f32[256,1280]{1,0:T(8,128)S(1)} custom-call(bf16[128,1024]{1,0:T(8,128)(2,1)S(1)} %get-tuple-element.38.a0, bf16[128,1024]{1,0:T(8,128)(2,1)S(1)} %get-tuple-element.37.b0, bf16[128,1024]{1,0:T(8,128)(2,1)S(1)} %collective-permute-done.3.a1, bf16[128,1024]{1,0:T(8,128)(2,1)S(1)} %collective-permute-done.6.b1, ...), custom_call_target="tpu_custom_call" | custom-call | flops 2684354560 | bytes 11796480 | tf_op jit(solution)/shard_map/pallas_call | solution.py:459
  40.3 1.9 %collective-permute-done.5.a3 = bf16[256,1024]{1,0:T(8,128)(2,1)S(1)} collective-permute-done((bf16[256,1024]{1,0:T(8,128)(2,1)S(1)}, bf16[256,1024]{1,0:T(8,128)(2,1)S(1)}, u32[]{:S(2)}, u32[]{:S(2)}) %collective-permute-start.5) | collective-permute-done | bytes 524320 | tf_op jit(solution)/shard_map/ppermute | solution.py:193
  42.1 10.2 %collective-permute-done.12.b3 = bf16[256,1024]{1,0:T(8,128)(2,1)S(1)} collective-permute-done((bf16[256,1024]{1,0:T(8,128)(2,1)S(1)}, bf16[256,1024]{1,0:T(8,128)(2,1)S(1)}, u32[]{:S(2)}, u32[]{:S(2)}) %collective-permute-start.12) | collective-permute-done | bytes 524320 | tf_op jit(solution)/shard_map/ppermute | solution.py:193
  52.4 2.5 %shard_map.75.refs_3_ = f32[256,1280]{1,0:T(8,128)S(1)} custom-call(bf16[256,1024]{1,0:T(8,128)(2,1)S(1)} %collective-permute-done.5.a3, bf16[256,1024]{1,0:T(8,128)(2,1)S(1)} %collective-permute-done.12.b3, f32[64,128]{1,0:T(8,128)S(1)} %bitcast.11, f32[256,128]{1,0:T(8,128)S(1)} %broadcast_in_dim.45.factor.refs_2_, f32[256,1280]{1,0:T(8,128)S(1)} %shard_map.74.acc_in, ...), custom_call_target="tpu_custom_call" | custom-call | flops 1342177280 | bytes 6553600 | tf_op jit(solution)/shard_map/pallas_call | solution.py:470
  54.9 2.2 %shard_map.76.refs_1_ = f32[128,1280]{1,0:T(8,128)S(1)} custom-call(bf16[256,1024]{1,0:T(8,128)(2,1)S(1)} %collective-permute-done.11.refs_0_, f32[64,128]{1,0:T(8,128)S(1)} %bitcast.12, f32[256,128]{1,0:T(8,128)S(1)} %broadcast_in_dim.45.factor.refs_2_, f32[256,1280]{1,0:T(8,128)S(1)} %shard_map.75.refs_3_, ...), custom_call_target="tpu_custom_call" | custom-call | flops 671088640 | bytes 5898240 | tf_op jit(solution)/shard_map/pallas_call | solution.py:481
  59.5 4.1 %collective-permute-done.14.refs_0_ = bf16[256,1024]{1,0:T(8,128)(2,1)S(1)} collective-permute-done((bf16[256,1024]{1,0:T(8,128)(2,1)S(1)}, bf16[256,1024]{1,0:T(8,128)(2,1)S(1)}, u32[]{:S(2)}, u32[]{:S(2)}) %collective-permute-start.14) | collective-permute-done | bytes 524320 | tf_op jit(solution)/shard_map/ppermute | solution.py:193
  63.6 2.2 %shard_map.78.refs_1_ = f32[128,1280]{1,0:T(8,128)S(1)} custom-call(bf16[256,1024]{1,0:T(8,128)(2,1)S(1)} %collective-permute-done.14.refs_0_, f32[64,128]{1,0:T(8,128)S(1)} %bitcast.13, f32[256,128]{1,0:T(8,128)S(1)} %broadcast_in_dim.45.factor.refs_2_, f32[256,1280]{1,0:T(8,128)S(1)} %shard_map.75.refs_3_, ...), custom_call_target="tpu_custom_call" | custom-call | flops 671088640 | bytes 5898240 | tf_op jit(solution)/shard_map/pallas_call | solution.py:481
  65.8 2.1 %shard_map.79 = (bf16[128,1024]{1,0:T(8,128)(2,1)S(1)}, bf16[128,128]{1,0:T(8,128)(2,1)}, bf16[128,128]{1,0:T(8,128)(2,1)}) custom-call(s32[1,4]{1,0:T(1,128)S(1)} %copy-done.2, f32[128,1280]{1,0:T(8,128)S(1)} %shard_map.78.refs_1_, f32[256,128]{1,0:T(8,128)S(1)} %get-tuple-element.27.refs_2_, f32[256,128]{1,0:T(8,128)S(1)} %get-tuple-element.28.refs_3_, ...), custom_call_target="tpu_custom_call" | custom-call | flops 671088640 | bytes 5898240 | tf_op jit(solution)/shard_map/pallas_call | solution.py:493
  69.3 7.8 %collective-permute-done.15.b1 = bf16[128,1024]{1,0:T(8,128)(2,1)S(1)} collective-permute-done((bf16[128,1024]{1,0:T(8,128)(2,1)S(1)}, bf16[128,1024]{1,0:T(8,128)(2,1)S(1)}, u32[]{:S(2)}, u32[]{:S(2)}) %collective-permute-start.15) | collective-permute-done | bytes 262176 | tf_op jit(solution)/shard_map/ppermute | solution.py:193
  79.3 12.8 %collective-permute-done.16.b2 = bf16[256,1024]{1,0:T(8,128)(2,1)S(1)} collective-permute-done((bf16[256,1024]{1,0:T(8,128)(2,1)S(1)}, bf16[256,1024]{1,0:T(8,128)(2,1)S(1)}, u32[]{:S(2)}, u32[]{:S(2)}) %collective-permute-start.16) | collective-permute-done | bytes 524320 | tf_op jit(solution)/shard_map/ppermute | solution.py:193
  92.1 3.4 %shard_map.80.acc_in = f32[256,1024]{1,0:T(8,128)S(1)} custom-call(bf16[128,1024]{1,0:T(8,128)(2,1)S(1)} %get-tuple-element.29.a0, bf16[128,1024]{1,0:T(8,128)(2,1)S(1)} %get-tuple-element.33.b0, bf16[128,1024]{1,0:T(8,128)(2,1)S(1)} %collective-permute-done.13.a1, bf16[128,1024]{1,0:T(8,128)(2,1)S(1)} %collective-permute-done.15.b1, ...), custom_call_target="tpu_custom_call" | custom-call | flops 2147483648 | bytes 9437184 | tf_op jit(solution)/shard_map/pallas_call | solution.py:513
  96.8 10.1 %collective-permute-done.17.b3 = bf16[256,1024]{1,0:T(8,128)(2,1)S(1)} collective-permute-done((bf16[256,1024]{1,0:T(8,128)(2,1)S(1)}, bf16[256,1024]{1,0:T(8,128)(2,1)S(1)}, u32[]{:S(2)}, u32[]{:S(2)}) %collective-permute-start.17) | collective-permute-done | bytes 524320 | tf_op jit(solution)/shard_map/ppermute | solution.py:193
  108.1 1.7 %shard_map.81.refs_1_ = f32[256,1024]{1,0:T(8,128)S(1)} custom-call(bf16[256,1024]{1,0:T(8,128)(2,1)S(1)} %collective-permute-done.20.a3, bf16[256,1024]{1,0:T(8,128)(2,1)S(1)} %collective-permute-done.17.b3, f32[256,1024]{1,0:T(8,128)S(1)} %shard_map.80.acc_in, bf16[256,1024]{1,0:T(8,128)(2,1)S(1)} %copy-done, bf16[1024,4096]{1,0:T(8,128)(2,1)S(1)} %bitcast.9, ...), custom_call_target="tpu_custom_call" | custom-call | flops 1073741824 | bytes 5242880 | tf_op jit(solution)/shard_map/pallas_call | solution.py:524
  109.8 2.5 %shard_map.82.refs_4_ = bf16[256,1024]{1,0:T(8,128)(2,1)} custom-call(bf16[256,1024]{1,0:T(8,128)(2,1)S(1)} %collective-permute-done.22.refs_0_, f32[256,1024]{1,0:T(8,128)S(1)} %shard_map.81.refs_1_, bf16[1024,4096]{1,0:T(8,128)(2,1)S(1)} %bitcast.9, bf16[1024,4096]{1,0:T(8,128)(2,1)S(1)} %collective-permute-done.21.w1.refs_3_), custom_call_target="tpu_custom_call" | custom-call | flops 1073741824 | bytes 8912896 | tf_op jit(solution)/shard_map/pallas_call | solution.py:536
  112.4 3.7 %collective-permute-done.18.refs_0_ = bf16[256,1024]{1,0:T(8,128)(2,1)S(1)} collective-permute-done((bf16[256,1024]{1,0:T(8,128)(2,1)S(1)}, bf16[256,1024]{1,0:T(8,128)(2,1)S(1)}, u32[]{:S(2)}, u32[]{:S(2)}) %collective-permute-start.18) | collective-permute-done | bytes 524320 | tf_op jit(solution)/shard_map/ppermute | solution.py:193
  116.1 2.5 %shard_map.83 = bf16[256,1024]{1,0:T(8,128)(2,1)} custom-call(bf16[256,1024]{1,0:T(8,128)(2,1)S(1)} %collective-permute-done.18.refs_0_, f32[256,1024]{1,0:T(8,128)S(1)} %shard_map.81.refs_1_, bf16[1024,4096]{1,0:T(8,128)(2,1)S(1)} %bitcast.9, bf16[1024,4096]{1,0:T(8,128)(2,1)S(1)} %collective-permute-done.21.w1.refs_3_, ...), custom_call_target="tpu_custom_call", output_to_operand_aliasing={{}: (4, {})} | custom-call | flops 1073741824 | bytes 8912896 | tf_op jit(solution)/shard_map/pallas_call | solution.py:536
  (63 shorter events, 15.9 us)
Async XLA Ops:
  0.0 35.7 %collective-permute-start.8 = (bf16[1024,4096]{1,0:T(8,128)(2,1)}, bf16[1024,4096]{1,0:T(8,128)(2,1)S(1)}, u32[]{:S(2)}, u32[]{:S(2)}) collective-permute-start(bf16[1024,4096]{1,0:T(8,128)(2,1)} %refs_0_.1), channel_id=1, source_target_pairs={{0,1},{1,0},{2,3},{3,2},{4,5},{5,4},{6,7},{7,6},{8,9},{9,8},{10,11... | collective-permute-start | bytes 25165832 | tf_op jit(solution)/shard_map/ppermute | solution.py:29
  0.5 91.6 %collective-permute-start.21 = (bf16[1024,4096]{1,0:T(8,128)(2,1)}, bf16[1024,4096]{1,0:T(8,128)(2,1)S(1)}, u32[]{:S(2)}, u32[]{:S(2)}) collective-permute-start(bf16[1024,4096]{1,0:T(8,128)(2,1)} %refs_2_.5), channel_id=1, source_target_pairs={{0,1},{1,0},{2,3},{3,2},{4,5},{5,4},{6,7},{7,6},{8,9},{9,8},{10,11... | collective-permute-start | bytes 25165832 | tf_op jit(solution)/shard_map/ppermute | solution.py:29
  1.6 7.5 %collective-permute-start.3 = (bf16[128,1024]{1,0:T(8,128)(2,1)S(1)}, bf16[128,1024]{1,0:T(8,128)(2,1)S(1)}, u32[]{:S(2)}, u32[]{:S(2)}) collective-permute-start(bf16[128,1024]{1,0:T(8,128)(2,1)S(1)} %get-tuple-element.38.a0), channel_id=1, source_target_pairs={{0,4},{1,3},{2,6},{3,1},{4,0},{5,9},{6,2},{7,11},{8,12},{9,5},{10,... | collective-permute-start | bytes 786440 | tf_op jit(solution)/shard_map/ppermute | solution.py:193
  5.9 5.2 %collective-permute-start = (f32[2,128]{1,0:T(2,128)S(1)}, f32[2,128]{1,0:T(2,128)S(1)}, u32[]{:S(2)}, u32[]{:S(2)}) collective-permute-start(f32[2,128]{1,0:T(2,128)S(1)} %bitcast.16), channel_id=1, source_target_pairs={{0,2},{1,5},{2,0},{3,7},{4,6},{5,1},{6,4},{7,3},{8,10},{9,13},{10,... | collective-permute-start | bytes 3080 | tf_op jit(solution)/shard_map/ppermute | solution.py:387
  7.5 15.7 %collective-permute-start.6 = (bf16[128,1024]{1,0:T(8,128)(2,1)S(1)}, bf16[128,1024]{1,0:T(8,128)(2,1)S(1)}, u32[]{:S(2)}, u32[]{:S(2)}) collective-permute-start(bf16[128,1024]{1,0:T(8,128)(2,1)S(1)} %get-tuple-element.37.b0), channel_id=1, source_target_pairs={{0,4},{1,3},{2,6},{3,1},{4,0},{5,9},{6,2},{7,11},{8,12},{9,5},{10,... | collective-permute-start | bytes 786440 | tf_op jit(solution)/shard_map/ppermute | solution.py:193
  9.1 14.6 %collective-permute-start.4 = (bf16[256,1024]{1,0:T(8,128)(2,1)S(1)}, bf16[256,1024]{1,0:T(8,128)(2,1)S(1)}, u32[]{:S(2)}, u32[]{:S(2)}) collective-permute-start(bf16[256,1024]{1,0:T(8,128)(2,1)S(1)} %pad_maximum_fusion), channel_id=1, source_target_pairs={{0,2},{1,5},{2,0},{3,7},{4,8},{5,1},{6,10},{7,3},{8,4},{9,13},{10,... | collective-permute-start | bytes 1572872 | tf_op jit(solution)/shard_map/ppermute | solution.py:193
  11.1 5.5 %collective-permute-start.1 = (f32[2,128]{1,0:T(2,128)S(1)}, f32[2,128]{1,0:T(2,128)S(1)}, u32[]{:S(2)}, u32[]{:S(2)}) collective-permute-start(f32[2,128]{1,0:T(2,128)S(1)} %bitcast_add_fusion), channel_id=1, source_target_pairs={{0,4},{1,3},{2,6},{3,1},{4,0},{5,7},{6,2},{7,5},{8,12},{9,11},{10,... | collective-permute-start | bytes 3080 | tf_op jit(solution)/shard_map/ppermute | solution.py:387
  16.6 6.4 %collective-permute-start.2 = (f32[2,128]{1,0:T(2,128)S(1)}, f32[2,128]{1,0:T(2,128)S(1)}, u32[]{:S(2)}, u32[]{:S(2)}) collective-permute-start(f32[2,128]{1,0:T(2,128)S(1)} %fusion.5), channel_id=1, source_target_pairs={{0,8},{1,9},{2,10},{3,11},{4,12},{5,13},{6,14},{7,15},{8,0},{9,1},... | collective-permute-start | bytes 3080 | tf_op jit(solution)/shard_map/ppermute | solution.py:387
  23.1 10.5 %collective-permute-start.10 = (bf16[128,4096]{1,0:T(8,128)(2,1)S(1)}, bf16[128,4096]{1,0:T(8,128)(2,1)S(1)}, u32[]{:S(2)}, u32[]{:S(2)}) collective-permute-start(bf16[128,4096]{1,0:T(8,128)(2,1)S(1)} %copy-done.3), channel_id=1, source_target_pairs={{0,1},{1,0},{2,3},{3,2},{4,5},{5,4},{6,7},{7,6},{8,9},{9,8},{10,11... | collective-permute-start | bytes 3145736 | tf_op jit(solution)/shard_map/ppermute | solution.py:29
  23.2 12.5 %collective-permute-start.9 = (bf16[128,4096]{1,0:T(8,128)(2,1)S(1)}, bf16[128,4096]{1,0:T(8,128)(2,1)S(1)}, u32[]{:S(2)}, u32[]{:S(2)}) collective-permute-start(bf16[128,4096]{1,0:T(8,128)(2,1)S(1)} %copy-done.4), channel_id=1, source_target_pairs={{0,1},{1,0},{2,3},{3,2},{4,5},{5,4},{6,7},{7,6},{8,9},{9,8},{10,11... | collective-permute-start | bytes 3145736 | tf_op jit(solution)/shard_map/ppermute | solution.py:29
  23.7 9.2 %collective-permute-start.7 = (bf16[256,1024]{1,0:T(8,128)(2,1)S(1)}, bf16[256,1024]{1,0:T(8,128)(2,1)S(1)}, u32[]{:S(2)}, u32[]{:S(2)}) collective-permute-start(bf16[256,1024]{1,0:T(8,128)(2,1)S(1)} %pad_maximum_fusion.1), channel_id=1, source_target_pairs={{0,2},{1,5},{2,0},{3,7},{4,8},{5,1},{6,10},{7,3},{8,4},{9,13},{10,... | collective-permute-start | bytes 1572872 | tf_op jit(solution)/shard_map/ppermute | solution.py:193
  32.9 9.2 %collective-permute-start.5 = (bf16[256,1024]{1,0:T(8,128)(2,1)S(1)}, bf16[256,1024]{1,0:T(8,128)(2,1)S(1)}, u32[]{:S(2)}, u32[]{:S(2)}) collective-permute-start(bf16[256,1024]{1,0:T(8,128)(2,1)S(1)} %collective-permute-done.4.a2), channel_id=1, source_target_pairs={{0,4},{1,3},{2,6},{3,1},{4,0},{5,9},{6,2},{7,11},{8,12},{9,5},{10,... | collective-permute-start | bytes 1572872 | tf_op jit(solution)/shard_map/ppermute | solution.py:193
  33.6 18.8 %collective-permute-start.12 = (bf16[256,1024]{1,0:T(8,128)(2,1)S(1)}, bf16[256,1024]{1,0:T(8,128)(2,1)S(1)}, u32[]{:S(2)}, u32[]{:S(2)}) collective-permute-start(bf16[256,1024]{1,0:T(8,128)(2,1)S(1)} %collective-permute-done.7.b2), channel_id=1, source_target_pairs={{0,4},{1,3},{2,6},{3,1},{4,0},{5,9},{6,2},{7,11},{8,12},{9,5},{10,... | collective-permute-start | bytes 1572872 | tf_op jit(solution)/shard_map/ppermute | solution.py:193
  42.1 12.7 %collective-permute-start.11 = (bf16[256,1024]{1,0:T(8,128)(2,1)S(1)}, bf16[256,1024]{1,0:T(8,128)(2,1)S(1)}, u32[]{:S(2)}, u32[]{:S(2)}) collective-permute-start(bf16[256,1024]{1,0:T(8,128)(2,1)S(1)} %collective-permute-done.5.a3), channel_id=1, source_target_pairs={{0,2},{1,5},{2,0},{3,7},{4,8},{5,1},{6,10},{7,3},{8,4},{9,13},{10,... | collective-permute-start | bytes 1572872 | tf_op jit(solution)/shard_map/ppermute | solution.py:193
  52.4 11.2 %collective-permute-start.14 = (bf16[256,1024]{1,0:T(8,128)(2,1)S(1)}, bf16[256,1024]{1,0:T(8,128)(2,1)S(1)}, u32[]{:S(2)}, u32[]{:S(2)}) collective-permute-start(bf16[256,1024]{1,0:T(8,128)(2,1)S(1)} %collective-permute-done.12.b3), channel_id=1, source_target_pairs={{0,2},{1,5},{2,0},{3,7},{4,8},{5,1},{6,10},{7,3},{8,4},{9,13},{10,... | collective-permute-start | bytes 1572872 | tf_op jit(solution)/shard_map/ppermute | solution.py:193
  58.5 33.6 %slice-start = ((s8[8388608]{0:T(1024)(128)(4,1)}), s8[4194304]{0:T(1024)(128)(4,1)S(1)}, s32[]{:S(2)}) async-start(s8[8388608]{0:T(1024)(128)(4,1)} %bitcast.8), calls=%async_computation | async-start | bytes 8388608
  58.6 7.2 %collective-permute-start.13 = (bf16[128,1024]{1,0:T(8,128)(2,1)S(1)}, bf16[128,1024]{1,0:T(8,128)(2,1)S(1)}, u32[]{:S(2)}, u32[]{:S(2)}) collective-permute-start(bf16[128,1024]{1,0:T(8,128)(2,1)S(1)} %get-tuple-element.29.a0), channel_id=1, source_target_pairs={{0,4},{1,3},{2,6},{3,1},{4,0},{5,9},{6,2},{7,11},{8,12},{9,5},{10,... | collective-permute-start | bytes 786440 | tf_op jit(solution)/shard_map/ppermute | solution.py:193
  67.9 9.2 %collective-permute-start.15 = (bf16[128,1024]{1,0:T(8,128)(2,1)S(1)}, bf16[128,1024]{1,0:T(8,128)(2,1)S(1)}, u32[]{:S(2)}, u32[]{:S(2)}) collective-permute-start(bf16[128,1024]{1,0:T(8,128)(2,1)S(1)} %get-tuple-element.33.b0), channel_id=1, source_target_pairs={{0,4},{1,3},{2,6},{3,1},{4,0},{5,9},{6,2},{7,11},{8,12},{9,5},{10,... | collective-permute-start | bytes 786440 | tf_op jit(solution)/shard_map/ppermute | solution.py:193
  68.1 10.4 %collective-permute-start.19 = (bf16[256,1024]{1,0:T(8,128)(2,1)S(1)}, bf16[256,1024]{1,0:T(8,128)(2,1)S(1)}, u32[]{:S(2)}, u32[]{:S(2)}) collective-permute-start(bf16[256,1024]{1,0:T(8,128)(2,1)S(1)} %pad_maximum_fusion.3), channel_id=1, source_target_pairs={{0,2},{1,5},{2,0},{3,7},{4,8},{5,1},{6,10},{7,3},{8,4},{9,13},{10,... | collective-permute-start | bytes 1572872 | tf_op jit(solution)/shard_map/ppermute | solution.py:193
  77.2 14.9 %collective-permute-start.16 = (bf16[256,1024]{1,0:T(8,128)(2,1)S(1)}, bf16[256,1024]{1,0:T(8,128)(2,1)S(1)}, u32[]{:S(2)}, u32[]{:S(2)}) collective-permute-start(bf16[256,1024]{1,0:T(8,128)(2,1)S(1)} %pad_maximum_fusion.2), channel_id=1, source_target_pairs={{0,2},{1,5},{2,0},{3,7},{4,8},{5,1},{6,10},{7,3},{8,4},{9,13},{10,... | collective-permute-start | bytes 1572872 | tf_op jit(solution)/shard_map/ppermute | solution.py:193
  78.5 17.0 %collective-permute-start.20 = (bf16[256,1024]{1,0:T(8,128)(2,1)S(1)}, bf16[256,1024]{1,0:T(8,128)(2,1)S(1)}, u32[]{:S(2)}, u32[]{:S(2)}) collective-permute-start(bf16[256,1024]{1,0:T(8,128)(2,1)S(1)} %collective-permute-done.19.a2), channel_id=1, source_target_pairs={{0,4},{1,3},{2,6},{3,1},{4,0},{5,9},{6,2},{7,11},{8,12},{9,5},{10,... | collective-permute-start | bytes 1572872 | tf_op jit(solution)/shard_map/ppermute | solution.py:193
  92.1 14.8 %collective-permute-start.17 = (bf16[256,1024]{1,0:T(8,128)(2,1)S(1)}, bf16[256,1024]{1,0:T(8,128)(2,1)S(1)}, u32[]{:S(2)}, u32[]{:S(2)}) collective-permute-start(bf16[256,1024]{1,0:T(8,128)(2,1)S(1)} %collective-permute-done.16.b2), channel_id=1, source_target_pairs={{0,4},{1,3},{2,6},{3,1},{4,0},{5,9},{6,2},{7,11},{8,12},{9,5},{10,... | collective-permute-start | bytes 1572872 | tf_op jit(solution)/shard_map/ppermute | solution.py:193
  95.5 14.3 %collective-permute-start.22 = (bf16[256,1024]{1,0:T(8,128)(2,1)S(1)}, bf16[256,1024]{1,0:T(8,128)(2,1)S(1)}, u32[]{:S(2)}, u32[]{:S(2)}) collective-permute-start(bf16[256,1024]{1,0:T(8,128)(2,1)S(1)} %collective-permute-done.20.a3), channel_id=1, source_target_pairs={{0,2},{1,5},{2,0},{3,7},{4,8},{5,1},{6,10},{7,3},{8,4},{9,13},{10,... | collective-permute-start | bytes 1572872 | tf_op jit(solution)/shard_map/ppermute | solution.py:193
  106.9 9.2 %collective-permute-start.18 = (bf16[256,1024]{1,0:T(8,128)(2,1)S(1)}, bf16[256,1024]{1,0:T(8,128)(2,1)S(1)}, u32[]{:S(2)}, u32[]{:S(2)}) collective-permute-start(bf16[256,1024]{1,0:T(8,128)(2,1)S(1)} %collective-permute-done.17.b3), channel_id=1, source_target_pairs={{0,2},{1,5},{2,0},{3,7},{4,8},{5,1},{6,10},{7,3},{8,4},{9,13},{10,... | collective-permute-start | bytes 1572872 | tf_op jit(solution)/shard_map/ppermute | solution.py:193
  (6 other events, 103.8 us)

commit v3 on v2

--- a/solution.py
+++ b/solution.py
@@ -353,29 +353,27 @@
         attended[:, h * HD : (h + 1) * HD] = out[h * ROWS : (h + 1) * ROWS, :]
 
 
-def out_early_kernel(a0, b0, a1, b1, a2, b2, w0, w1, acc, xs):
-    for s, (own, first, second) in enumerate(((a0, a1, a2), (b0, b1, b2))):
-        rows = stream_rows(s)
-        xs[0, rows, :] = own[...]
-        xs[1, rows, :] = first[...]
-        xs[2, rows, :] = second[:ROWS, :]
-        xs[3, rows, :] = second[ROWS:, :]
+def stream_units(xs, *streams):
+    for s, units in enumerate(streams):
+        for n, unit in enumerate(units):
+            xs[n, stream_rows(s), :] = unit[...]
+
+
+def out_early_kernel(a0, a1, a2, a3, b0, b1, b2, b3, w0, w1, acc, xs):
+    stream_units(xs, (a0, a1, a2, a3), (b0, b1, b2, b3))
     acc[...] = jnp.zeros_like(acc)
     add_units(xs, acc, w0, (w1,), 0, 4)
 
 
-def out_middle_kernel(a3, b3, acc_in, hidden, w0, w1, acc, xs):
-    for s, ref in enumerate((a3, b3)):
-        xs[0, stream_rows(s), :] = ref[:ROWS, :]
-        xs[1, stream_rows(s), :] = ref[ROWS:, :]
+def out_middle_kernel(a4, a5, b4, b5, acc_in, hidden, w0, w1, acc, xs):
+    stream_units(xs, (a4, a5), (b4, b5))
     acc[...] = acc_in[...] + hidden[...].astype(jnp.float32)
     add_units(xs, acc, w0, (w1,), 4, 2)
 
 
-def out_last_kernel(half, new, acc_in, w0, w1, *refs):
+def out_last_kernel(half, new, newer, acc_in, w0, w1, *refs):
     out, xs, acc = refs[-3:]
-    xs[0] = new[:ROWS, :]
-    xs[1] = new[ROWS:, :]
+    stream_units(xs, (new, newer))
     acc[...] = acc_in[stream_rows(half), :]
     add_units(xs, acc, w0, (w1,), 6, 2)
     out[...] = acc[...].astype(jnp.bfloat16)
@@ -500,52 +498,53 @@
         )(lengths, projected, cosine, sine, *early)
 
     a0, key_a, value_a = attend_stream(0, project(0, a4), ())
-    a1 = swapped(a0, 0)
+    a1, a2 = swapped(a0, 0), swapped(a0, 1)
     projected = project(1, b4)
     a1, projected = after(a1, projected)
-    a2 = swapped(jnp.concatenate([a0, a1], axis=0), 1)
+    a3 = swapped(a1, 1)
     b0, _, _ = attend_stream(1, projected, (key_a, value_a))
-    b1 = swapped(b0, 0)
-    b2 = swapped(jnp.concatenate([b0, b1], axis=0), 1)
-    a3, b3 = swapped(a2, 0), swapped(b2, 0)
+    b1, b2 = swapped(b0, 0), swapped(b0, 1)
+    a4, b3 = swapped(a2, 0), swapped(b1, 1)
+    a5, b4 = swapped(a3, 0), swapped(b2, 0)
+    a6, b5 = swapped(a4, 1), swapped(b3, 0)
     width = output_weight.shape[0]
     acc_shape = jax.ShapeDtypeStruct((STRETCH, width), f32)
     acc = kernel_call(
         out_early_kernel,
         out_shape=acc_shape,
-        in_specs=[VM] * 8,
+        in_specs=[VM] * 10,
         out_specs=VM,
         scratch_shapes=[pltpu.VMEM((4, STRETCH, UNIT), bf16)],
         compiler_params=params(12),
         cost_estimate=cost(STRETCH, 4, width),
-    )(a0, b0, a1, b1, a2, b2, output_weight, other_output)
-    a3, acc = after(a3, acc)
-    a4, b4 = swapped(a3, 1), swapped(b3, 1)
+    )(a0, a1, a2, a3, b0, b1, b2, b3, output_weight, other_output)
+    a5, acc = after(a5, acc)
+    a7, b6, b7 = swapped(a5, 1), swapped(b4, 1), swapped(b5, 1)
     acc = kernel_call(
         out_middle_kernel,
         out_shape=acc_shape,
-        in_specs=[VM] * 6,
+        in_specs=[VM] * 8,
         out_specs=VM,
         scratch_shapes=[pltpu.VMEM((2, STRETCH, UNIT), bf16)],
         compiler_params=params(12),
         cost_estimate=cost(STRETCH, 2, width),
-    )(a3, b3, acc, hidden_in, output_weight, other_output)
-
-    def out_last(half, new, *partial):
+    )(a4, a5, b4, b5, acc, hidden_in, output_weight, other_output)
+
+    def out_last(half, new, newer, *partial):
         part = pl.BlockSpec((ROWS, UNIT), lambda i: (half, 0))
         return kernel_call(
             lambda *refs: out_last_kernel(half, *refs),
             grid=(1,),
             out_shape=jax.ShapeDtypeStruct((STRETCH, UNIT), bf16),
-            in_specs=[VM, VM, VM, VM] + [HBM] * half,
+            in_specs=[VM, VM, VM, VM, VM] + [HBM] * half,
             out_specs=part,
             scratch_shapes=[pltpu.VMEM((2, ROWS, UNIT), bf16), pltpu.VMEM((ROWS, width), f32)],
-            input_output_aliases={4: 0} if half else {},
+            input_output_aliases={5: 0} if half else {},
             compiler_params=params(12),
             cost_estimate=cost(ROWS, 4, width),
-        )(new, acc, output_weight, other_output, *partial)
-
-    return out_last(1, b4, out_last(0, a4))
+        )(new, newer, acc, output_weight, other_output, *partial)
+
+    return out_last(1, b6, b7, out_last(0, a6, a7))
 
 
 def fits_ring(mesh):

time: 119 us -> 110 us (0.924)
  waiting for transfers between devices: 64.5 us -> 49.5 us
  starting transfers between devices: 21.3 us -> 27.6 us
    ppermute x16 -> x22, waiting for transfers between devices: 60.7 us -> 45.7 us  [swapped(): return lax.ppermute(shard, ('tp', 'pair'), ring_swap(later))]
    ppermute x16 -> x22, starting transfers between devices: 14.6 us -> 20.8 us  [swapped(): return lax.ppermute(shard, ('tp', 'pair'), ring_swap(later))]
  transfers between devices with their start and end apart: 23 -> 29, of which waited for: 10 -> 13; matrix products, arithmetic and copies ran while one was open for 3% -> 3% of each run, Pallas kernels for 22% -> 24%
where the time goes in v3:
time: 110 us
  waiting for transfers between devices  49.5 us (45%)
  Pallas kernels  29.3 us (27%)
  starting transfers between devices  27.6 us (25%)
  other arithmetic  2.07 us (2%)
  local copies, waits for them, and re-layouts  1.19 us (1%)
    ppermute x22, waiting for transfers between devices, swapped(): return lax.ppermute(shard, ('tp', 'pair'), ring_swap(later))  45.7 us
    ppermute x22, starting transfers between devices, swapped(): return lax.ppermute(shard, ('tp', 'pair'), ring_swap(later))  20.8 us
    ppermute x3, starting transfers between devices, summed_over_tp(): value = value + lax.ppermute(value, ('tp', 'pair'), pairs)  5.7 us
    pallas_call x2, Pallas kernels, out_last(): kernel_call(lambda *refs: out_last_kernel(half, *refs), grid=(1,), out_sh...  5.06 us
    pallas_call x1, Pallas kernels, ring_layer(): kernel_call(early_kernel, out_shape=acc_shape, in_specs=[VM] * 12, out_sp...  4.54 us
    pallas_call x2, Pallas kernels, project(): kernel_call(lambda *refs: project_kernel(half, *refs), out_shape=jax.Shap...  4.42 us
    pallas_call x1, Pallas kernels, load(): kernel_call(load_kernel, out_shape=jax.ShapeDtypeStruct((rows, arrays[0]....  3.93 us
    ppermute x3, waiting for transfers between devices, summed_over_tp(): value = value + lax.ppermute(value, ('tp', 'pair'), pairs)  3.82 us
  transfers between devices with their start and end apart: 29, of which 13 were waited for; matrix products, arithmetic and copies ran while one was open for 3% of the time, Pallas kernels for 24%

profile of v3, /device:TPU:0, one launch (start us, length us, event | category | flops | bytes accessed | tf_op | source)
XLA Modules:
  0.0 110.0 jit_solution(6741138385472719025)
XLA Ops:
  1.6 3.1 %collective-permute-start.3 = (bf16[128,1024]{1,0:T(8,128)(2,1)S(1)}, bf16[128,1024]{1,0:T(8,128)(2,1)S(1)}, u32[]{:S(2)}, u32[]{:S(2)}) collective-permute-start(bf16[128,1024]{1,0:T(8,128)(2,1)S(1)} %get-tuple-element.38.a0), channel_id=1, source_target_pairs={{0,4},{1,3},{2,6},{3,1},{4,0},{5,9},{6,2},{7,11},{8,12},{9,5},{10,... | collective-permute-start | bytes 786440 | tf_op jit(solution)/shard_map/ppermute | solution.py:193
  9.1 2.0 %collective-permute-start.4 = (bf16[256,1024]{1,0:T(8,128)(2,1)S(1)}, bf16[256,1024]{1,0:T(8,128)(2,1)S(1)}, u32[]{:S(2)}, u32[]{:S(2)}) collective-permute-start(bf16[256,1024]{1,0:T(8,128)(2,1)S(1)} %pad_maximum_fusion), channel_id=1, source_target_pairs={{0,2},{1,5},{2,0},{3,7},{4,8},{5,1},{6,10},{7,3},{8,4},{9,13},{10,... | collective-permute-start | bytes 1572872 | tf_op jit(solution)/shard_map/ppermute | solution.py:193
  12.8 3.8 %collective-permute-done.1 = f32[2,128]{1,0:T(2,128)S(1)} collective-permute-done((f32[2,128]{1,0:T(2,128)S(1)}, f32[2,128]{1,0:T(2,128)S(1)}, u32[]{:S(2)}, u32[]{:S(2)}) %collective-permute-start.1) | collective-permute-done | bytes 1056 | tf_op jit(solution)/shard_map/ppermute | solution.py:385
  16.6 2.5 %collective-permute-start.2 = (f32[2,128]{1,0:T(2,128)S(1)}, f32[2,128]{1,0:T(2,128)S(1)}, u32[]{:S(2)}, u32[]{:S(2)}) collective-permute-start(f32[2,128]{1,0:T(2,128)S(1)} %fusion.5), channel_id=1, source_target_pairs={{0,8},{1,9},{2,10},{3,11},{4,12},{5,13},{6,14},{7,15},{8,0},{9,1},... | collective-permute-start | bytes 3080 | tf_op jit(solution)/shard_map/ppermute | solution.py:385
  19.1 3.9 %shard_map.73.refs_0_.refs_4_ = bf16[1280,4096]{1,0:T(8,128)(2,1)S(1)} custom-call(bf16[1024,4096]{1,0:T(8,128)(2,1)} %refs_0_.1, bf16[128,4096]{1,0:T(8,128)(2,1)} %refs_1_.1, bf16[128,4096]{1,0:T(8,128)(2,1)} %refs_2_.1), custom_call_target="tpu_custom_call" | custom-call | bytes 10485760 | tf_op jit(solution)/shard_map/pallas_call | solution.py:399
  24.0 8.9 %collective-permute-done.7.b2 = bf16[256,1024]{1,0:T(8,128)(2,1)S(1)} collective-permute-done((bf16[256,1024]{1,0:T(8,128)(2,1)S(1)}, bf16[256,1024]{1,0:T(8,128)(2,1)S(1)}, u32[]{:S(2)}, u32[]{:S(2)}) %collective-permute-start.7) | collective-permute-done | bytes 524320 | tf_op jit(solution)/shard_map/ppermute | solution.py:193
  33.6 2.1 %collective-permute-start.12 = (bf16[256,1024]{1,0:T(8,128)(2,1)S(1)}, bf16[256,1024]{1,0:T(8,128)(2,1)S(1)}, u32[]{:S(2)}, u32[]{:S(2)}) collective-permute-start(bf16[256,1024]{1,0:T(8,128)(2,1)S(1)} %collective-permute-done.7.b2), channel_id=1, source_target_pairs={{0,4},{1,3},{2,6},{3,1},{4,0},{5,9},{6,2},{7,11},{8,12},{9,5},{10,... | collective-permute-start | bytes 1572872 | tf_op jit(solution)/shard_map/ppermute | solution.py:193
  35.7 4.5 %shard_map.74.acc_in = f32[256,1280]{1,0:T(8,128)S(1)} custom-call(bf16[128,1024]{1,0:T(8,128)(2,1)S(1)} %get-tuple-element.38.a0, bf16[128,1024]{1,0:T(8,128)(2,1)S(1)} %get-tuple-element.37.b0, bf16[128,1024]{1,0:T(8,128)(2,1)S(1)} %collective-permute-done.3.a1, bf16[128,1024]{1,0:T(8,128)(2,1)S(1)} %collective-permute-done.6.b1, ...), custom_call_target="tpu_custom_call" | custom-call | flops 2684354560 | bytes 11796480 | tf_op jit(solution)/shard_map/pallas_call | solution.py:457
  42.1 10.2 %collective-permute-done.12.b3 = bf16[256,1024]{1,0:T(8,128)(2,1)S(1)} collective-permute-done((bf16[256,1024]{1,0:T(8,128)(2,1)S(1)}, bf16[256,1024]{1,0:T(8,128)(2,1)S(1)}, u32[]{:S(2)}, u32[]{:S(2)}) %collective-permute-start.12) | collective-permute-done | bytes 524320 | tf_op jit(solution)/shard_map/ppermute | solution.py:193
  52.4 2.5 %shard_map.75.refs_3_ = f32[256,1280]{1,0:T(8,128)S(1)} custom-call(bf16[256,1024]{1,0:T(8,128)(2,1)S(1)} %collective-permute-done.5.a3, bf16[256,1024]{1,0:T(8,128)(2,1)S(1)} %collective-permute-done.12.b3, f32[64,128]{1,0:T(8,128)S(1)} %bitcast.11, f32[256,128]{1,0:T(8,128)S(1)} %broadcast_in_dim.45.factor.refs_2_, f32[256,1280]{1,0:T(8,128)S(1)} %shard_map.74.acc_in, ...), custom_call_target="tpu_custom_call" | custom-call | flops 1342177280 | bytes 6553600 | tf_op jit(solution)/shard_map/pallas_call | solution.py:468
  54.9 2.2 %shard_map.76.refs_1_ = f32[128,1280]{1,0:T(8,128)S(1)} custom-call(bf16[256,1024]{1,0:T(8,128)(2,1)S(1)} %collective-permute-done.11.refs_0_, f32[64,128]{1,0:T(8,128)S(1)} %bitcast.12, f32[256,128]{1,0:T(8,128)S(1)} %broadcast_in_dim.45.factor.refs_2_, f32[256,1280]{1,0:T(8,128)S(1)} %shard_map.75.refs_3_, ...), custom_call_target="tpu_custom_call" | custom-call | flops 671088640 | bytes 5898240 | tf_op jit(solution)/shard_map/pallas_call | solution.py:479
  59.5 4.1 %collective-permute-done.14.refs_0_ = bf16[256,1024]{1,0:T(8,128)(2,1)S(1)} collective-permute-done((bf16[256,1024]{1,0:T(8,128)(2,1)S(1)}, bf16[256,1024]{1,0:T(8,128)(2,1)S(1)}, u32[]{:S(2)}, u32[]{:S(2)}) %collective-permute-start.14) | collective-permute-done | bytes 524320 | tf_op jit(solution)/shard_map/ppermute | solution.py:193
  63.6 2.2 %shard_map.78.refs_1_ = f32[128,1280]{1,0:T(8,128)S(1)} custom-call(bf16[256,1024]{1,0:T(8,128)(2,1)S(1)} %collective-permute-done.14.refs_0_, f32[64,128]{1,0:T(8,128)S(1)} %bitcast.13, f32[256,128]{1,0:T(8,128)S(1)} %broadcast_in_dim.45.factor.refs_2_, f32[256,1280]{1,0:T(8,128)S(1)} %shard_map.75.refs_3_, ...), custom_call_target="tpu_custom_call" | custom-call | flops 671088640 | bytes 5898240 | tf_op jit(solution)/shard_map/pallas_call | solution.py:479
  66.0 2.1 %shard_map.79 = (bf16[128,1024]{1,0:T(8,128)(2,1)S(1)}, bf16[128,128]{1,0:T(8,128)(2,1)}, bf16[128,128]{1,0:T(8,128)(2,1)}) custom-call(s32[1,4]{1,0:T(1,128)S(1)} %copy-done.2, f32[128,1280]{1,0:T(8,128)S(1)} %shard_map.78.refs_1_, f32[256,128]{1,0:T(8,128)S(1)} %get-tuple-element.27.refs_2_, f32[256,128]{1,0:T(8,128)S(1)} %get-tuple-element.28.refs_3_, ...), custom_call_target="tpu_custom_call" | custom-call | flops 671088640 | bytes 5898240 | tf_op jit(solution)/shard_map/pallas_call | solution.py:491
  69.6 2.3 %collective-permute-start.24 = (bf16[128,1024]{1,0:T(8,128)(2,1)S(1)}, bf16[128,1024]{1,0:T(8,128)(2,1)S(1)}, u32[]{:S(2)}, u32[]{:S(2)}) collective-permute-start(bf16[128,1024]{1,0:T(8,128)(2,1)S(1)} %collective-permute-done.13.a1), channel_id=1, source_target_pairs={{0,2},{1,5},{2,0},{3,7},{4,8},{5,1},{6,10},{7,3},{8,4},{9,13},{10,... | collective-permute-start | bytes 786440 | tf_op jit(solution)/shard_map/ppermute | solution.py:193
  72.0 3.1 %collective-permute-done.22.a2 = bf16[128,1024]{1,0:T(8,128)(2,1)S(1)} collective-permute-done((bf16[128,1024]{1,0:T(8,128)(2,1)S(1)}, bf16[128,1024]{1,0:T(8,128)(2,1)S(1)}, u32[]{:S(2)}, u32[]{:S(2)}) %collective-permute-start.22) | collective-permute-done | bytes 262176 | tf_op jit(solution)/shard_map/ppermute | solution.py:193
  75.0 2.3 %collective-permute-done.18.b1 = bf16[128,1024]{1,0:T(8,128)(2,1)S(1)} collective-permute-done((bf16[128,1024]{1,0:T(8,128)(2,1)S(1)}, bf16[128,1024]{1,0:T(8,128)(2,1)S(1)}, u32[]{:S(2)}, u32[]{:S(2)}) %collective-permute-start.18) | collective-permute-done | bytes 262176 | tf_op jit(solution)/shard_map/ppermute | solution.py:193
  77.4 3.7 %collective-permute-start.19 = (bf16[128,1024]{1,0:T(8,128)(2,1)S(1)}, bf16[128,1024]{1,0:T(8,128)(2,1)S(1)}, u32[]{:S(2)}, u32[]{:S(2)}) collective-permute-start(bf16[128,1024]{1,0:T(8,128)(2,1)S(1)} %collective-permute-done.18.b1), channel_id=1, source_target_pairs={{0,2},{1,5},{2,0},{3,7},{4,8},{5,1},{6,10},{7,3},{8,4},{9,13},{10,... | collective-permute-start | bytes 786440 | tf_op jit(solution)/shard_map/ppermute | solution.py:193
  81.0 5.3 %collective-permute-done.15.b2 = bf16[128,1024]{1,0:T(8,128)(2,1)S(1)} collective-permute-done((bf16[128,1024]{1,0:T(8,128)(2,1)S(1)}, bf16[128,1024]{1,0:T(8,128)(2,1)S(1)}, u32[]{:S(2)}, u32[]{:S(2)}) %collective-permute-start.15) | collective-permute-done | bytes 262176 | tf_op jit(solution)/shard_map/ppermute | solution.py:193
  87.7 4.2 %collective-permute-done.19.b3 = bf16[128,1024]{1,0:T(8,128)(2,1)S(1)} collective-permute-done((bf16[128,1024]{1,0:T(8,128)(2,1)S(1)}, bf16[128,1024]{1,0:T(8,128)(2,1)S(1)}, u32[]{:S(2)}, u32[]{:S(2)}) %collective-permute-start.19) | collective-permute-done | bytes 262176 | tf_op jit(solution)/shard_map/ppermute | solution.py:193
  91.9 3.4 %shard_map.80.acc_in = f32[256,1024]{1,0:T(8,128)S(1)} custom-call(bf16[128,1024]{1,0:T(8,128)(2,1)S(1)} %get-tuple-element.29.a0, bf16[128,1024]{1,0:T(8,128)(2,1)S(1)} %collective-permute-done.13.a1, bf16[128,1024]{1,0:T(8,128)(2,1)S(1)} %collective-permute-done.22.a2, bf16[128,1024]{1,0:T(8,128)(2,1)S(1)} %collective-permute-done.24.a3, ...), custom_call_target="tpu_custom_call" | custom-call | flops 2147483648 | bytes 9437184 | tf_op jit(solution)/shard_map/pallas_call | solution.py:512
  97.4 3.7 %collective-permute-done.20.b5 = bf16[128,1024]{1,0:T(8,128)(2,1)S(1)} collective-permute-done((bf16[128,1024]{1,0:T(8,128)(2,1)S(1)}, bf16[128,1024]{1,0:T(8,128)(2,1)S(1)}, u32[]{:S(2)}, u32[]{:S(2)}) %collective-permute-start.20) | collective-permute-done | bytes 262176 | tf_op jit(solution)/shard_map/ppermute | solution.py:193
  104.1 2.5 %shard_map.82.refs_5_ = bf16[256,1024]{1,0:T(8,128)(2,1)} custom-call(bf16[128,1024]{1,0:T(8,128)(2,1)S(1)} %collective-permute-done.27.refs_0_, bf16[128,1024]{1,0:T(8,128)(2,1)S(1)} %collective-permute-done.28.refs_1_, f32[256,1024]{1,0:T(8,128)S(1)} %shard_map.81.refs_2_, bf16[1024,4096]{1,0:T(8,128)(2,1)S(1)} %bitcast.9, ...), custom_call_target="tpu_custom_call" | custom-call | flops 1073741824 | bytes 8912896 | tf_op jit(solution)/shard_map/pallas_call | solution.py:535
  107.4 2.5 %shard_map.83 = bf16[256,1024]{1,0:T(8,128)(2,1)} custom-call(bf16[128,1024]{1,0:T(8,128)(2,1)S(1)} %collective-permute-done.17.refs_0_, bf16[128,1024]{1,0:T(8,128)(2,1)S(1)} %collective-permute-done.21.refs_1_, f32[256,1024]{1,0:T(8,128)S(1)} %shard_map.81.refs_2_, bf16[1024,4096]{1,0:T(8,128)(2,1)S(1)} %bitcast.9, ...), custom_call_target="tpu_custom_call", output_to_operand_aliasing={{}: (5, {})} | custom-call | flops 1073741824 | bytes 8912896 | tf_op jit(solution)/shard_map/pallas_call | solution.py:535
  (73 shorter events, 22.5 us)
Async XLA Ops:
  0.0 35.7 %collective-permute-start.8 = (bf16[1024,4096]{1,0:T(8,128)(2,1)}, bf16[1024,4096]{1,0:T(8,128)(2,1)S(1)}, u32[]{:S(2)}, u32[]{:S(2)}) collective-permute-start(bf16[1024,4096]{1,0:T(8,128)(2,1)} %refs_0_.1), channel_id=1, source_target_pairs={{0,1},{1,0},{2,3},{3,2},{4,5},{5,4},{6,7},{7,6},{8,9},{9,8},{10,11... | collective-permute-start | bytes 25165832 | tf_op jit(solution)/shard_map/ppermute | solution.py:29
  0.5 91.4 %collective-permute-start.26 = (bf16[1024,4096]{1,0:T(8,128)(2,1)}, bf16[1024,4096]{1,0:T(8,128)(2,1)S(1)}, u32[]{:S(2)}, u32[]{:S(2)}) collective-permute-start(bf16[1024,4096]{1,0:T(8,128)(2,1)} %refs_3_.3), channel_id=1, source_target_pairs={{0,1},{1,0},{2,3},{3,2},{4,5},{5,4},{6,7},{7,6},{8,9},{9,8},{10,11... | collective-permute-start | bytes 25165832 | tf_op jit(solution)/shard_map/ppermute | solution.py:29
  1.6 7.5 %collective-permute-start.3 = (bf16[128,1024]{1,0:T(8,128)(2,1)S(1)}, bf16[128,1024]{1,0:T(8,128)(2,1)S(1)}, u32[]{:S(2)}, u32[]{:S(2)}) collective-permute-start(bf16[128,1024]{1,0:T(8,128)(2,1)S(1)} %get-tuple-element.38.a0), channel_id=1, source_target_pairs={{0,4},{1,3},{2,6},{3,1},{4,0},{5,9},{6,2},{7,11},{8,12},{9,5},{10,... | collective-permute-start | bytes 786440 | tf_op jit(solution)/shard_map/ppermute | solution.py:193
  7.5 15.7 %collective-permute-start.6 = (bf16[128,1024]{1,0:T(8,128)(2,1)S(1)}, bf16[128,1024]{1,0:T(8,128)(2,1)S(1)}, u32[]{:S(2)}, u32[]{:S(2)}) collective-permute-start(bf16[128,1024]{1,0:T(8,128)(2,1)S(1)} %get-tuple-element.37.b0), channel_id=1, source_target_pairs={{0,4},{1,3},{2,6},{3,1},{4,0},{5,9},{6,2},{7,11},{8,12},{9,5},{10,... | collective-permute-start | bytes 786440 | tf_op jit(solution)/shard_map/ppermute | solution.py:193
  9.1 14.6 %collective-permute-start.4 = (bf16[256,1024]{1,0:T(8,128)(2,1)S(1)}, bf16[256,1024]{1,0:T(8,128)(2,1)S(1)}, u32[]{:S(2)}, u32[]{:S(2)}) collective-permute-start(bf16[256,1024]{1,0:T(8,128)(2,1)S(1)} %pad_maximum_fusion), channel_id=1, source_target_pairs={{0,2},{1,5},{2,0},{3,7},{4,8},{5,1},{6,10},{7,3},{8,4},{9,13},{10,... | collective-permute-start | bytes 1572872 | tf_op jit(solution)/shard_map/ppermute | solution.py:193
  23.1 10.5 %collective-permute-start.10 = (bf16[128,4096]{1,0:T(8,128)(2,1)S(1)}, bf16[128,4096]{1,0:T(8,128)(2,1)S(1)}, u32[]{:S(2)}, u32[]{:S(2)}) collective-permute-start(bf16[128,4096]{1,0:T(8,128)(2,1)S(1)} %copy-done.3), channel_id=1, source_target_pairs={{0,1},{1,0},{2,3},{3,2},{4,5},{5,4},{6,7},{7,6},{8,9},{9,8},{10,11... | collective-permute-start | bytes 3145736 | tf_op jit(solution)/shard_map/ppermute | solution.py:29
  23.2 12.5 %collective-permute-start.9 = (bf16[128,4096]{1,0:T(8,128)(2,1)S(1)}, bf16[128,4096]{1,0:T(8,128)(2,1)S(1)}, u32[]{:S(2)}, u32[]{:S(2)}) collective-permute-start(bf16[128,4096]{1,0:T(8,128)(2,1)S(1)} %copy-done.4), channel_id=1, source_target_pairs={{0,1},{1,0},{2,3},{3,2},{4,5},{5,4},{6,7},{7,6},{8,9},{9,8},{10,11... | collective-permute-start | bytes 3145736 | tf_op jit(solution)/shard_map/ppermute | solution.py:29
  23.7 9.2 %collective-permute-start.7 = (bf16[256,1024]{1,0:T(8,128)(2,1)S(1)}, bf16[256,1024]{1,0:T(8,128)(2,1)S(1)}, u32[]{:S(2)}, u32[]{:S(2)}) collective-permute-start(bf16[256,1024]{1,0:T(8,128)(2,1)S(1)} %pad_maximum_fusion.1), channel_id=1, source_target_pairs={{0,2},{1,5},{2,0},{3,7},{4,8},{5,1},{6,10},{7,3},{8,4},{9,13},{10,... | collective-permute-start | bytes 1572872 | tf_op jit(solution)/shard_map/ppermute | solution.py:193
  32.9 9.2 %collective-permute-start.5 = (bf16[256,1024]{1,0:T(8,128)(2,1)S(1)}, bf16[256,1024]{1,0:T(8,128)(2,1)S(1)}, u32[]{:S(2)}, u32[]{:S(2)}) collective-permute-start(bf16[256,1024]{1,0:T(8,128)(2,1)S(1)} %collective-permute-done.4.a2), channel_id=1, source_target_pairs={{0,4},{1,3},{2,6},{3,1},{4,0},{5,9},{6,2},{7,11},{8,12},{9,5},{10,... | collective-permute-start | bytes 1572872 | tf_op jit(solution)/shard_map/ppermute | solution.py:193
  33.6 18.8 %collective-permute-start.12 = (bf16[256,1024]{1,0:T(8,128)(2,1)S(1)}, bf16[256,1024]{1,0:T(8,128)(2,1)S(1)}, u32[]{:S(2)}, u32[]{:S(2)}) collective-permute-start(bf16[256,1024]{1,0:T(8,128)(2,1)S(1)} %collective-permute-done.7.b2), channel_id=1, source_target_pairs={{0,4},{1,3},{2,6},{3,1},{4,0},{5,9},{6,2},{7,11},{8,12},{9,5},{10,... | collective-permute-start | bytes 1572872 | tf_op jit(solution)/shard_map/ppermute | solution.py:193
  42.1 12.7 %collective-permute-start.11 = (bf16[256,1024]{1,0:T(8,128)(2,1)S(1)}, bf16[256,1024]{1,0:T(8,128)(2,1)S(1)}, u32[]{:S(2)}, u32[]{:S(2)}) collective-permute-start(bf16[256,1024]{1,0:T(8,128)(2,1)S(1)} %collective-permute-done.5.a3), channel_id=1, source_target_pairs={{0,2},{1,5},{2,0},{3,7},{4,8},{5,1},{6,10},{7,3},{8,4},{9,13},{10,... | collective-permute-start | bytes 1572872 | tf_op jit(solution)/shard_map/ppermute | solution.py:193
  52.4 11.2 %collective-permute-start.14 = (bf16[256,1024]{1,0:T(8,128)(2,1)S(1)}, bf16[256,1024]{1,0:T(8,128)(2,1)S(1)}, u32[]{:S(2)}, u32[]{:S(2)}) collective-permute-start(bf16[256,1024]{1,0:T(8,128)(2,1)S(1)} %collective-permute-done.12.b3), channel_id=1, source_target_pairs={{0,2},{1,5},{2,0},{3,7},{4,8},{5,1},{6,10},{7,3},{8,4},{9,13},{10,... | collective-permute-start | bytes 1572872 | tf_op jit(solution)/shard_map/ppermute | solution.py:193
  65.8 9.2 %collective-permute-start.22 = (bf16[128,1024]{1,0:T(8,128)(2,1)S(1)}, bf16[128,1024]{1,0:T(8,128)(2,1)S(1)}, u32[]{:S(2)}, u32[]{:S(2)}) collective-permute-start(bf16[128,1024]{1,0:T(8,128)(2,1)S(1)} %get-tuple-element.29.a0), channel_id=1, source_target_pairs={{0,2},{1,5},{2,0},{3,7},{4,8},{5,1},{6,10},{7,3},{8,4},{9,13},{10,... | collective-permute-start | bytes 786440 | tf_op jit(solution)/shard_map/ppermute | solution.py:193
  68.1 9.2 %collective-permute-start.18 = (bf16[128,1024]{1,0:T(8,128)(2,1)S(1)}, bf16[128,1024]{1,0:T(8,128)(2,1)S(1)}, u32[]{:S(2)}, u32[]{:S(2)}) collective-permute-start(bf16[128,1024]{1,0:T(8,128)(2,1)S(1)} %get-tuple-element.33.b0), channel_id=1, source_target_pairs={{0,4},{1,3},{2,6},{3,1},{4,0},{5,9},{6,2},{7,11},{8,12},{9,5},{10,... | collective-permute-start | bytes 786440 | tf_op jit(solution)/shard_map/ppermute | solution.py:193
  69.6 11.4 %collective-permute-start.24 = (bf16[128,1024]{1,0:T(8,128)(2,1)S(1)}, bf16[128,1024]{1,0:T(8,128)(2,1)S(1)}, u32[]{:S(2)}, u32[]{:S(2)}) collective-permute-start(bf16[128,1024]{1,0:T(8,128)(2,1)S(1)} %collective-permute-done.13.a1), channel_id=1, source_target_pairs={{0,2},{1,5},{2,0},{3,7},{4,8},{5,1},{6,10},{7,3},{8,4},{9,13},{10,... | collective-permute-start | bytes 786440 | tf_op jit(solution)/shard_map/ppermute | solution.py:193
  71.9 14.4 %collective-permute-start.15 = (bf16[128,1024]{1,0:T(8,128)(2,1)S(1)}, bf16[128,1024]{1,0:T(8,128)(2,1)S(1)}, u32[]{:S(2)}, u32[]{:S(2)}) collective-permute-start(bf16[128,1024]{1,0:T(8,128)(2,1)S(1)} %get-tuple-element.33.b0), channel_id=1, source_target_pairs={{0,2},{1,5},{2,0},{3,7},{4,8},{5,1},{6,10},{7,3},{8,4},{9,13},{10,... | collective-permute-start | bytes 786440 | tf_op jit(solution)/shard_map/ppermute | solution.py:193
  75.0 11.2 %collective-permute-start.23 = (bf16[128,1024]{1,0:T(8,128)(2,1)S(1)}, bf16[128,1024]{1,0:T(8,128)(2,1)S(1)}, u32[]{:S(2)}, u32[]{:S(2)}) collective-permute-start(bf16[128,1024]{1,0:T(8,128)(2,1)S(1)} %collective-permute-done.22.a2), channel_id=1, source_target_pairs={{0,4},{1,3},{2,6},{3,1},{4,0},{5,9},{6,2},{7,11},{8,12},{9,5},{10,... | collective-permute-start | bytes 786440 | tf_op jit(solution)/shard_map/ppermute | solution.py:193
  77.4 14.5 %collective-permute-start.19 = (bf16[128,1024]{1,0:T(8,128)(2,1)S(1)}, bf16[128,1024]{1,0:T(8,128)(2,1)S(1)}, u32[]{:S(2)}, u32[]{:S(2)}) collective-permute-start(bf16[128,1024]{1,0:T(8,128)(2,1)S(1)} %collective-permute-done.18.b1), channel_id=1, source_target_pairs={{0,2},{1,5},{2,0},{3,7},{4,8},{5,1},{6,10},{7,3},{8,4},{9,13},{10,... | collective-permute-start | bytes 786440 | tf_op jit(solution)/shard_map/ppermute | solution.py:193
  81.0 14.3 %collective-permute-start.25 = (bf16[128,1024]{1,0:T(8,128)(2,1)S(1)}, bf16[128,1024]{1,0:T(8,128)(2,1)S(1)}, u32[]{:S(2)}, u32[]{:S(2)}) collective-permute-start(bf16[128,1024]{1,0:T(8,128)(2,1)S(1)} %collective-permute-done.24.a3), channel_id=1, source_target_pairs={{0,4},{1,3},{2,6},{3,1},{4,0},{5,9},{6,2},{7,11},{8,12},{9,5},{10,... | collective-permute-start | bytes 786440 | tf_op jit(solution)/shard_map/ppermute | solution.py:193
  86.3 10.5 %collective-permute-start.16 = (bf16[128,1024]{1,0:T(8,128)(2,1)S(1)}, bf16[128,1024]{1,0:T(8,128)(2,1)S(1)}, u32[]{:S(2)}, u32[]{:S(2)}) collective-permute-start(bf16[128,1024]{1,0:T(8,128)(2,1)S(1)} %collective-permute-done.15.b2), channel_id=1, source_target_pairs={{0,4},{1,3},{2,6},{3,1},{4,0},{5,9},{6,2},{7,11},{8,12},{9,5},{10,... | collective-permute-start | bytes 786440 | tf_op jit(solution)/shard_map/ppermute | solution.py:193
  86.3 17.8 %collective-permute-start.27 = (bf16[128,1024]{1,0:T(8,128)(2,1)S(1)}, bf16[128,1024]{1,0:T(8,128)(2,1)S(1)}, u32[]{:S(2)}, u32[]{:S(2)}) collective-permute-start(bf16[128,1024]{1,0:T(8,128)(2,1)S(1)} %collective-permute-done.23.a4), channel_id=1, source_target_pairs={{0,2},{1,5},{2,0},{3,7},{4,8},{5,1},{6,10},{7,3},{8,4},{9,13},{10,... | collective-permute-start | bytes 786440 | tf_op jit(solution)/shard_map/ppermute | solution.py:193
  91.9 9.2 %collective-permute-start.20 = (bf16[128,1024]{1,0:T(8,128)(2,1)S(1)}, bf16[128,1024]{1,0:T(8,128)(2,1)S(1)}, u32[]{:S(2)}, u32[]{:S(2)}) collective-permute-start(bf16[128,1024]{1,0:T(8,128)(2,1)S(1)} %collective-permute-done.19.b3), channel_id=1, source_target_pairs={{0,4},{1,3},{2,6},{3,1},{4,0},{5,9},{6,2},{7,11},{8,12},{9,5},{10,... | collective-permute-start | bytes 786440 | tf_op jit(solution)/shard_map/ppermute | solution.py:193
  95.3 8.8 %collective-permute-start.28 = (bf16[128,1024]{1,0:T(8,128)(2,1)S(1)}, bf16[128,1024]{1,0:T(8,128)(2,1)S(1)}, u32[]{:S(2)}, u32[]{:S(2)}) collective-permute-start(bf16[128,1024]{1,0:T(8,128)(2,1)S(1)} %collective-permute-done.25.a5), channel_id=1, source_target_pairs={{0,2},{1,5},{2,0},{3,7},{4,8},{5,1},{6,10},{7,3},{8,4},{9,13},{10,... | collective-permute-start | bytes 786440 | tf_op jit(solution)/shard_map/ppermute | solution.py:193
  96.8 9.9 %collective-permute-start.17 = (bf16[128,1024]{1,0:T(8,128)(2,1)S(1)}, bf16[128,1024]{1,0:T(8,128)(2,1)S(1)}, u32[]{:S(2)}, u32[]{:S(2)}) collective-permute-start(bf16[128,1024]{1,0:T(8,128)(2,1)S(1)} %collective-permute-done.16.b4), channel_id=1, source_target_pairs={{0,2},{1,5},{2,0},{3,7},{4,8},{5,1},{6,10},{7,3},{8,4},{9,13},{10,... | collective-permute-start | bytes 786440 | tf_op jit(solution)/shard_map/ppermute | solution.py:193
  (12 other events, 171.0 us)

commit v4 on v3

--- a/solution.py
+++ b/solution.py
@@ -213,7 +213,7 @@
 def add_units(xs, acc, own, others, first, count):
     def unit_step(u, carry):
         mine, cols = columns_of(first + u)
-        for here, parts in ((mine, (own,)), (jnp.logical_not(mine), others)):
+        for here, parts in ((mine, own), (jnp.logical_not(mine), others)):
 
             @pl.when(here)
             def _(parts=parts):
@@ -228,13 +228,13 @@
     lax.fori_loop(0, count, unit_step, 0)
 
 
-def load_kernel(*refs):
+def load_kernel(spans, *refs):
     *sources, target, sems = refs
     copies = []
     at = 0
-    for n, source in enumerate(sources):
-        rows = source.shape[0]
-        copies.append(pltpu.make_async_copy(source, target.at[pl.ds(at, rows), :], sems.at[n]))
+    for n, (source, (start, rows)) in enumerate(zip(sources, spans)):
+        where = target.at[pl.ds(at, rows), :]
+        copies.append(pltpu.make_async_copy(source.at[pl.ds(start, rows), :], where, sems.at[n]))
         at += rows
     for copy in copies:
         copy.start()
@@ -278,43 +278,48 @@
     return slice(s * ROWS, (s + 1) * ROWS)
 
 
-def early_kernel(a0, b0, a1, b1, a2, b2, gain, factor, *refs):
+def normed_units(xs, gain, factor, first, *streams):
+    for s, units in enumerate(streams):
+        for n, unit in enumerate(units):
+            place_unit(xs, stream_rows(s), n, unit[...], factor[stream_rows(s), :], gain, first + n)
+
+
+def early_kernel(a0, a1, a2, a3, b0, b1, b2, b3, gain, factor, *refs):
     *weights, acc, xs = refs
-    for s, (own, first, second) in enumerate(((a0, a1, a2), (b0, b1, b2))):
-        rows = stream_rows(s)
-        scale = factor[rows, :]
-        place_unit(xs, rows, 0, own[...], scale, gain, 0)
-        place_unit(xs, rows, 1, first[...], scale, gain, 1)
-        place_unit(xs, rows, 2, second[:ROWS, :], scale, gain, 2)
-        place_unit(xs, rows, 3, second[ROWS:, :], scale, gain, 3)
+    normed_units(xs, gain, factor, 0, (a0, a1, a2, a3), (b0, b1, b2, b3))
     acc[...] = jnp.zeros_like(acc)
-    add_units(xs, acc, weights[0], weights[1:], 0, 4)
-
-
-def middle_kernel(a3, b3, gain, factor, acc_in, *refs):
+    add_units(xs, acc, weights[:2], weights[2:], 0, 4)
+
+
+def middle_kernel(a4, a5, b4, b5, gain, factor, acc_in, *refs):
     *weights, acc, xs = refs
-    for s, ref in enumerate((a3, b3)):
-        for n in range(2):
-            part = ref[n * ROWS : (n + 1) * ROWS, :]
-            place_unit(xs, stream_rows(s), n, part, factor[stream_rows(s), :], gain, 4 + n)
+    normed_units(xs, gain, factor, 4, (a4, a5), (b4, b5))
     acc[...] = acc_in[...]
-    add_units(xs, acc, weights[0], weights[1:], 4, 2)
+    add_units(xs, acc, weights[:2], weights[2:], 4, 2)
+
+
+def project_first_kernel(a6, a7, b6, gain, factor, acc_in, *refs):
+    *weights, first, second, acc, xs, late = refs
+    normed_units(xs, gain, factor, 6, (a6,), (b6,))
+    normed_units(late, gain, factor, 7, (a7,))
+    acc[...] = acc_in[...]
+    add_units(xs, acc, weights[:2], weights[2:], 6, 1)
+    first[...] = acc[:ROWS, :]
+    second[...] = acc[ROWS:, :]
+    add_units(late, first, weights[:2], weights[2:], 7, 1)
+
+
+def project_second_kernel(b7, gain, factor, acc_in, *refs):
+    *weights, acc, late = refs
+    place_unit(late, slice(0, ROWS), 0, b7[...], factor[ROWS:, :], gain, 7)
+    acc[...] = acc_in[...]
+    add_units(late, acc, weights[:2], weights[2:], 7, 1)
 
 
 def turned_heads(part, cosine, sine):
     lane = lax.broadcasted_iota(jnp.int32, part.shape, 1)
     other = jnp.where(lane % 2 == 0, pltpu.roll(part, HD - 1, 1), pltpu.roll(part, 1, 1))
     return (part * cosine + other * sine).astype(jnp.bfloat16)
-
-
-def project_kernel(half, new, gain, factor, acc_in, *refs):
-    *weights, acc, xs = refs
-    rows = stream_rows(half)
-    for n in range(2):
-        part = new[n * ROWS : (n + 1) * ROWS, :]
-        place_unit(xs, slice(0, ROWS), n, part, factor[rows, :], gain, 6 + n)
-    acc[...] = acc_in[rows, :]
-    add_units(xs, acc, weights[0], weights[1:], 6, 2)
 
 
 def attend_kernel(half, lens, acc, cosine, sine, *refs):
@@ -362,20 +367,30 @@
 def out_early_kernel(a0, a1, a2, a3, b0, b1, b2, b3, w0, w1, acc, xs):
     stream_units(xs, (a0, a1, a2, a3), (b0, b1, b2, b3))
     acc[...] = jnp.zeros_like(acc)
-    add_units(xs, acc, w0, (w1,), 0, 4)
+    add_units(xs, acc, (w0,), (w1,), 0, 4)
 
 
 def out_middle_kernel(a4, a5, b4, b5, acc_in, hidden, w0, w1, acc, xs):
     stream_units(xs, (a4, a5), (b4, b5))
     acc[...] = acc_in[...] + hidden[...].astype(jnp.float32)
-    add_units(xs, acc, w0, (w1,), 4, 2)
-
-
-def out_last_kernel(half, new, newer, acc_in, w0, w1, *refs):
-    out, xs, acc = refs[-3:]
-    stream_units(xs, (new, newer))
-    acc[...] = acc_in[stream_rows(half), :]
-    add_units(xs, acc, w0, (w1,), 6, 2)
+    add_units(xs, acc, (w0,), (w1,), 4, 2)
+
+
+def out_first_kernel(a6, a7, b6, acc_in, w0, w1, out, second, acc, first, xs, late):
+    stream_units(xs, (a6,), (b6,))
+    stream_units(late, (a7,))
+    acc[...] = acc_in[...]
+    add_units(xs, acc, (w0,), (w1,), 6, 1)
+    first[...] = acc[:ROWS, :]
+    second[...] = acc[ROWS:, :]
+    add_units(late, first, (w0,), (w1,), 7, 1)
+    out[...] = first[...].astype(jnp.bfloat16)
+
+
+def out_second_kernel(b7, acc_in, w0, w1, partial, out, acc, late):
+    stream_units(late, (b7,))
+    acc[...] = acc_in[...]
+    add_units(late, acc, (w0,), (w1,), 7, 1)
     out[...] = acc[...].astype(jnp.bfloat16)
 
 
@@ -394,10 +409,10 @@
     return pltpu.with_memory_space_constraint(value, pltpu.VMEM)
 
 
-def load(arrays):
-    rows = sum(w.shape[0] for w in arrays)
+def load(arrays, spans):
+    rows = sum(span for _, span in spans)
     return kernel_call(
-        load_kernel,
+        lambda *refs: load_kernel(spans, *refs),
         out_shape=jax.ShapeDtypeStruct((rows, arrays[0].shape[1]), arrays[0].dtype),
         in_specs=[HBM] * len(arrays),
         out_specs=VM,
@@ -428,6 +443,7 @@
     f32, bf16 = jnp.float32, jnp.bfloat16
     a0, b0 = hidden_in[:ROWS], hidden_in[ROWS:]
     a1, b1 = swapped(a0, 0), swapped(b0, 0)
+    a2, b2 = swapped(a0, 1), swapped(b0, 1)
     projections = (query_weight, key_weight, value_weight)
     others = []
     for w in projections:
@@ -438,53 +454,62 @@
     squares = summed_over_tp(squares)
     factor = lax.rsqrt(squares / (RING * UNIT) + 1e-05)
     factor = jnp.broadcast_to(factor.reshape(STRETCH, 1), (STRETCH, 128))
-    a2 = swapped(jnp.concatenate([a0, a1], axis=0), 1)
-    b2 = swapped(jnp.concatenate([b0, b1], axis=0), 1)
     gain = norm_gain.reshape(RING * UNIT // 128, 128)
     position = token_position(lengths[0])
     lane = jnp.arange(HD, dtype=jnp.int32)
     angle = position.astype(f32)[:, None] * scaled_freq(lane - lane % 2)[None, :]
     cosine = jnp.cos(angle)
     sine = jnp.sin(angle) * jnp.where(lane % 2 == 0, -1.0, 1.0)[None, :]
+    a3, b3 = swapped(a1, 1), swapped(b1, 1)
+    a4, b4 = swapped(a2, 0), swapped(b2, 0)
     other_output = in_vmem(partner(output_weight, "pair", 0))
-    own = load(projections)
-    a2, own = after(a2, own)
-    weights = (own, *others)
-    a3, b3 = swapped(a2, 0), swapped(b2, 0)
-
+    cut = query_weight.shape[0] // 2
+    own_first = load((query_weight,), ((0, cut),))
+    own_second = load(
+        projections,
+        ((cut, query_weight.shape[0] - cut), (0, key_weight.shape[0]), (0, value_weight.shape[0])),
+    )
+    a3, own_first = after(a3, own_first)
+    a4, own_second = after(a4, own_second)
+    weights = (own_first, own_second, *others)
+    a5, b5 = swapped(a3, 0), swapped(b3, 0)
+    a6, b6 = swapped(a4, 1), swapped(b4, 1)
     factor, cosine, sine, lengths = after(factor, cosine, sine, lengths)
     acc_shape = jax.ShapeDtypeStruct((STRETCH, qkv), f32)
     acc = kernel_call(
         early_kernel,
         out_shape=acc_shape,
-        in_specs=[VM] * 12,
+        in_specs=[VM] * 15,
         out_specs=VM,
         scratch_shapes=[pltpu.VMEM((4, STRETCH, UNIT), bf16)],
-        compiler_params=params(12),
+        compiler_params=params(10),
         cost_estimate=cost(STRETCH, 4, qkv),
-    )(a0, b0, a1, b1, a2, b2, gain, factor, *weights)
-    a3, acc = after(a3, acc)
-    a4, b4 = swapped(a3, 1), swapped(b3, 1)
+    )(a0, a1, a2, a3, b0, b1, b2, b3, gain, factor, *weights)
+    a5, acc = after(a5, acc)
+    a7, b7 = swapped(a5, 1), swapped(b5, 1)
     acc = kernel_call(
         middle_kernel,
         out_shape=acc_shape,
-        in_specs=[VM] * 9,
+        in_specs=[VM] * 12,
         out_specs=VM,
         scratch_shapes=[pltpu.VMEM((2, STRETCH, UNIT), bf16)],
-        compiler_params=params(12),
+        compiler_params=params(8),
         cost_estimate=cost(STRETCH, 2, qkv),
-    )(a3, b3, gain, factor, acc, *weights)
-
-    def project(half, new):
-        return kernel_call(
-            lambda *refs: project_kernel(half, *refs),
-            out_shape=jax.ShapeDtypeStruct((ROWS, qkv), f32),
-            in_specs=[VM] * 8,
-            out_specs=VM,
-            scratch_shapes=[pltpu.VMEM((2, ROWS, UNIT), bf16)],
-            compiler_params=params(12),
-            cost_estimate=cost(ROWS, 2, qkv),
-        )(new, gain, factor, acc, *weights)
+    )(a4, a5, b4, b5, gain, factor, acc, *weights)
+    half_shape = jax.ShapeDtypeStruct((ROWS, qkv), f32)
+    first, second = kernel_call(
+        project_first_kernel,
+        out_shape=(half_shape, half_shape),
+        in_specs=[VM] * 11,
+        out_specs=(VM, VM),
+        scratch_shapes=[
+            pltpu.VMEM((STRETCH, qkv), f32),
+            pltpu.VMEM((1, STRETCH, UNIT), bf16),
+            pltpu.VMEM((1, ROWS, UNIT), bf16),
+        ],
+        compiler_params=params(8),
+        cost_estimate=cost(STRETCH, 2, qkv),
+    )(a6, a7, b6, gain, factor, acc, *weights)
 
     def attend_stream(half, projected, early):
         kv = jax.ShapeDtypeStruct((ROWS, HD), bf16)
@@ -493,13 +518,21 @@
             out_shape=(jax.ShapeDtypeStruct((ROWS, UNIT), bf16), kv, kv),
             in_specs=[SM] + [VM] * (3 + len(early)),
             out_specs=(VM, VM, VM),
-            compiler_params=params(12),
+            compiler_params=params(8),
             cost_estimate=cost(ROWS, 2, qkv),
         )(lengths, projected, cosine, sine, *early)
 
-    a0, key_a, value_a = attend_stream(0, project(0, a4), ())
+    a0, key_a, value_a = attend_stream(0, first, ())
     a1, a2 = swapped(a0, 0), swapped(a0, 1)
-    projected = project(1, b4)
+    projected = kernel_call(
+        project_second_kernel,
+        out_shape=half_shape,
+        in_specs=[VM] * 9,
+        out_specs=VM,
+        scratch_shapes=[pltpu.VMEM((1, ROWS, UNIT), bf16)],
+        compiler_params=params(10),
+        cost_estimate=cost(ROWS, 1, qkv),
+    )(b7, gain, factor, second, *weights)
     a1, projected = after(a1, projected)
     a3 = swapped(a1, 1)
     b0, _, _ = attend_stream(1, projected, (key_a, value_a))
@@ -515,7 +548,7 @@
         in_specs=[VM] * 10,
         out_specs=VM,
         scratch_shapes=[pltpu.VMEM((4, STRETCH, UNIT), bf16)],
-        compiler_params=params(12),
+        compiler_params=params(10),
         cost_estimate=cost(STRETCH, 4, width),
     )(a0, a1, a2, a3, b0, b1, b2, b3, output_weight, other_output)
     a5, acc = after(a5, acc)
@@ -526,25 +559,40 @@
         in_specs=[VM] * 8,
         out_specs=VM,
         scratch_shapes=[pltpu.VMEM((2, STRETCH, UNIT), bf16)],
-        compiler_params=params(12),
+        compiler_params=params(8),
         cost_estimate=cost(STRETCH, 2, width),
     )(a4, a5, b4, b5, acc, hidden_in, output_weight, other_output)
 
-    def out_last(half, new, newer, *partial):
-        part = pl.BlockSpec((ROWS, UNIT), lambda i: (half, 0))
-        return kernel_call(
-            lambda *refs: out_last_kernel(half, *refs),
-            grid=(1,),
-            out_shape=jax.ShapeDtypeStruct((STRETCH, UNIT), bf16),
-            in_specs=[VM, VM, VM, VM, VM] + [HBM] * half,
-            out_specs=part,
-            scratch_shapes=[pltpu.VMEM((2, ROWS, UNIT), bf16), pltpu.VMEM((ROWS, width), f32)],
-            input_output_aliases={5: 0} if half else {},
-            compiler_params=params(12),
-            cost_estimate=cost(ROWS, 4, width),
-        )(new, newer, acc, output_weight, other_output, *partial)
-
-    return out_last(1, b6, b7, out_last(0, a6, a7))
+    out_shape = jax.ShapeDtypeStruct((STRETCH, UNIT), bf16)
+    half_shape = jax.ShapeDtypeStruct((ROWS, width), f32)
+    half = pltpu.VMEM((ROWS, width), f32)
+    late = pltpu.VMEM((1, ROWS, UNIT), bf16)
+    out, acc = kernel_call(
+        out_first_kernel,
+        grid=(1,),
+        out_shape=(out_shape, half_shape),
+        in_specs=[VM] * 6,
+        out_specs=(pl.BlockSpec((ROWS, UNIT), lambda i: (0, 0)), VM),
+        scratch_shapes=[
+            pltpu.VMEM((STRETCH, width), f32),
+            half,
+            pltpu.VMEM((1, STRETCH, UNIT), bf16),
+            late,
+        ],
+        compiler_params=params(8),
+        cost_estimate=cost(STRETCH, 2, width),
+    )(a6, a7, b6, acc, output_weight, other_output)
+    return kernel_call(
+        out_second_kernel,
+        grid=(1,),
+        out_shape=out_shape,
+        in_specs=[VM] * 4 + [HBM],
+        out_specs=pl.BlockSpec((ROWS, UNIT), lambda i: (1, 0)),
+        scratch_shapes=[half, late],
+        input_output_aliases={4: 0},
+        compiler_params=params(8),
+        cost_estimate=cost(ROWS, 1, width),
+    )(b7, acc, output_weight, other_output, out)
 
 
 def fits_ring(mesh):

time: 110 us -> 117 us (1.064)
  starting transfers between devices: 27.6 us -> 44.9 us
  waiting for transfers between devices: 49.5 us -> 38.8 us
  other arithmetic: 2.07 us -> 3.31 us
    ppermute x22 -> x28, starting transfers between devices: 20.8 us -> 37.9 us  [swapped(): return lax.ppermute(shard, ('tp', 'pair'), ring_swap(later))]
    ppermute x22 -> x28, waiting for transfers between devices: 45.7 us -> 32.8 us  [swapped(): return lax.ppermute(shard, ('tp', 'pair'), ring_swap(later))]
    ppermute x3, waiting for transfers between devices: 3.82 us -> 5.9 us  [summed_over_tp(): value = value + lax.ppermute(value, ('tp', 'pair'), pairs)]
    pallas_call x7 -> x8, Pallas kernels: 20.4 us -> 19.7 us  [the longest x2 5.03 us: load(): kernel_call(lambda *refs: load_kernel(spans, *refs), out_shape=jax.ShapeD...]
  transfers between devices with their start and end apart: 29 -> 35, of which waited for: 13 -> 15; matrix products, arithmetic and copies ran while one was open for 3% -> 4% of each run, Pallas kernels for 24% -> 23%
where the time goes in v4:
time: 117 us
  starting transfers between devices  44.9 us (38%)
  waiting for transfers between devices  38.8 us (33%)
  Pallas kernels  28.3 us (24%)
  other arithmetic  3.31 us (3%)
  local copies, waits for them, and re-layouts  1.19 us (1%)
    ppermute x28, starting transfers between devices, swapped(): return lax.ppermute(shard, ('tp', 'pair'), ring_swap(later))  37.9 us
    ppermute x28, waiting for transfers between devices, swapped(): return lax.ppermute(shard, ('tp', 'pair'), ring_swap(later))  32.8 us
    ppermute x3, starting transfers between devices, summed_over_tp(): value = value + lax.ppermute(value, ('tp', 'pair'), pairs)  6.51 us
    ppermute x3, waiting for transfers between devices, summed_over_tp(): value = value + lax.ppermute(value, ('tp', 'pair'), pairs)  5.9 us
    pallas_call x2, Pallas kernels, load(): kernel_call(lambda *refs: load_kernel(spans, *refs), out_shape=jax.ShapeD...  5.03 us
    pallas_call x1, Pallas kernels, ring_layer(): kernel_call(early_kernel, out_shape=acc_shape, in_specs=[VM] * 15, out_sp...  4.37 us
    pallas_call x2, Pallas kernels, attend_stream(): kernel_call(lambda *refs: attend_kernel(half, *refs), out_shape=(jax.Shap...  3.56 us
    pallas_call x1, Pallas kernels, ring_layer(): kernel_call(out_early_kernel, out_shape=acc_shape, in_specs=[VM] * 10, ou...  3.37 us
  transfers between devices with their start and end apart: 35, of which 15 were waited for; matrix products, arithmetic and copies ran while one was open for 4% of the time, Pallas kernels for 23%

profile of v4, /device:TPU:0, one launch (start us, length us, event | category | flops | bytes accessed | tf_op | source)
XLA Modules:
  0.0 116.7 jit_solution(7512197995655153946)
XLA Ops:
  1.7 3.0 %collective-permute-start = (f32[2,128]{1,0:T(2,128)S(1)}, f32[2,128]{1,0:T(2,128)S(1)}, u32[]{:S(2)}, u32[]{:S(2)}) collective-permute-start(f32[2,128]{1,0:T(2,128)S(1)} %bitcast.16), channel_id=1, source_target_pairs={{0,2},{1,5},{2,0},{3,7},{4,6},{5,1},{6,4},{7,3},{8,10},{9,13},{10,... | collective-permute-start | bytes 3080 | tf_op jit(solution)/shard_map/ppermute | solution.py:400
  6.3 2.1 %collective-permute-start.1 = (f32[2,128]{1,0:T(2,128)S(1)}, f32[2,128]{1,0:T(2,128)S(1)}, u32[]{:S(2)}, u32[]{:S(2)}) collective-permute-start(f32[2,128]{1,0:T(2,128)S(1)} %bitcast_add_fusion), channel_id=1, source_target_pairs={{0,4},{1,3},{2,6},{3,1},{4,0},{5,7},{6,2},{7,5},{8,12},{9,11},{10,... | collective-permute-start | bytes 3080 | tf_op jit(solution)/shard_map/ppermute | solution.py:400
  14.1 4.3 %collective-permute-done.2 = f32[2,128]{1,0:T(2,128)S(1)} collective-permute-done((f32[2,128]{1,0:T(2,128)S(1)}, f32[2,128]{1,0:T(2,128)S(1)}, u32[]{:S(2)}, u32[]{:S(2)}) %collective-permute-start.2) | collective-permute-done | bytes 1056 | tf_op jit(solution)/shard_map/ppermute | solution.py:400
  20.1 2.5 %collective-permute-start.4 = (bf16[128,1024]{1,0:T(8,128)(2,1)S(1)}, bf16[128,1024]{1,0:T(8,128)(2,1)S(1)}, u32[]{:S(2)}, u32[]{:S(2)}) collective-permute-start(bf16[128,1024]{1,0:T(8,128)(2,1)S(1)} %collective-permute-done.3.a2), channel_id=1, source_target_pairs={{0,4},{1,3},{2,6},{3,1},{4,0},{5,9},{6,2},{7,11},{8,12},{9,5},{10,... | collective-permute-start | bytes 786440 | tf_op jit(solution)/shard_map/ppermute | solution.py:193
  22.6 2.9 %collective-permute-done.9.b1 = bf16[128,1024]{1,0:T(8,128)(2,1)S(1)} collective-permute-done((bf16[128,1024]{1,0:T(8,128)(2,1)S(1)}, bf16[128,1024]{1,0:T(8,128)(2,1)S(1)}, u32[]{:S(2)}, u32[]{:S(2)}) %collective-permute-start.9) | collective-permute-done | bytes 262176 | tf_op jit(solution)/shard_map/ppermute | solution.py:193
  25.6 2.7 %collective-permute-start.7 = (bf16[128,1024]{1,0:T(8,128)(2,1)S(1)}, bf16[128,1024]{1,0:T(8,128)(2,1)S(1)}, u32[]{:S(2)}, u32[]{:S(2)}) collective-permute-start(bf16[128,1024]{1,0:T(8,128)(2,1)S(1)} %collective-permute-done.6.a1), channel_id=1, source_target_pairs={{0,2},{1,5},{2,0},{3,7},{4,8},{5,1},{6,10},{7,3},{8,4},{9,13},{10,... | collective-permute-start | bytes 786440 | tf_op jit(solution)/shard_map/ppermute | solution.py:193
  28.3 2.7 %collective-permute-done.4.a4 = bf16[128,1024]{1,0:T(8,128)(2,1)S(1)} collective-permute-done((bf16[128,1024]{1,0:T(8,128)(2,1)S(1)}, bf16[128,1024]{1,0:T(8,128)(2,1)S(1)}, u32[]{:S(2)}, u32[]{:S(2)}) %collective-permute-start.4) | collective-permute-done | bytes 262176 | tf_op jit(solution)/shard_map/ppermute | solution.py:193
  35.4 3.6 %collective-permute-done.11.b3 = bf16[128,1024]{1,0:T(8,128)(2,1)S(1)} collective-permute-done((bf16[128,1024]{1,0:T(8,128)(2,1)S(1)}, bf16[128,1024]{1,0:T(8,128)(2,1)S(1)}, u32[]{:S(2)}, u32[]{:S(2)}) %collective-permute-start.11) | collective-permute-done | bytes 262176 | tf_op jit(solution)/shard_map/ppermute | solution.py:193
  39.1 2.8 %shard_map.73.refs_1_ = bf16[768,4096]{1,0:T(8,128)(2,1)S(1)} custom-call(bf16[1024,4096]{1,0:T(8,128)(2,1)} %refs_0_.3, bf16[128,4096]{1,0:T(8,128)(2,1)} %refs_1_.1, bf16[128,4096]{1,0:T(8,128)(2,1)} %refs_2_.1), custom_call_target="tpu_custom_call" | custom-call | bytes 6291456 | tf_op jit(solution)/shard_map/pallas_call | solution.py:414
  41.9 2.2 %shard_map.74.refs_0_ = bf16[512,4096]{1,0:T(8,128)(2,1)S(1)} custom-call(bf16[1024,4096]{1,0:T(8,128)(2,1)} %refs_0_.3), custom_call_target="tpu_custom_call" | custom-call | bytes 4194304 | tf_op jit(solution)/shard_map/pallas_call | solution.py:414
  46.9 2.1 %collective-permute-start.5 = (bf16[128,1024]{1,0:T(8,128)(2,1)S(1)}, bf16[128,1024]{1,0:T(8,128)(2,1)S(1)}, u32[]{:S(2)}, u32[]{:S(2)}) collective-permute-start(bf16[128,1024]{1,0:T(8,128)(2,1)S(1)} %collective-permute-done.4.a4), channel_id=1, source_target_pairs={{0,2},{1,5},{2,0},{3,7},{4,8},{5,1},{6,10},{7,3},{8,4},{9,13},{10,... | collective-permute-start | bytes 786440 | tf_op jit(solution)/shard_map/ppermute | solution.py:193
  52.0 4.4 %shard_map.75.acc_in = f32[256,1280]{1,0:T(8,128)S(1)} custom-call(bf16[128,1024]{1,0:T(8,128)(2,1)S(1)} %get-tuple-element.50.a0, bf16[128,1024]{1,0:T(8,128)(2,1)S(1)} %collective-permute-done.6.a1, bf16[128,1024]{1,0:T(8,128)(2,1)S(1)} %collective-permute-done.3.a2, bf16[128,1024]{1,0:T(8,128)(2,1)S(1)} %collective-permute-done.7.a3, ...), custom_call_target="tpu_custom_call" | custom-call | flops 2684354560 | bytes 11796480 | tf_op jit(solution)/shard_map/pallas_call | solution.py:479
  56.8 3.4 %collective-permute-done.18.b5 = bf16[128,1024]{1,0:T(8,128)(2,1)S(1)} collective-permute-done((bf16[128,1024]{1,0:T(8,128)(2,1)S(1)}, bf16[128,1024]{1,0:T(8,128)(2,1)S(1)}, u32[]{:S(2)}, u32[]{:S(2)}) %collective-permute-start.18) | collective-permute-done | bytes 262176 | tf_op jit(solution)/shard_map/ppermute | solution.py:193
  60.2 2.2 %collective-permute-start.20 = (bf16[128,1024]{1,0:T(8,128)(2,1)S(1)}, bf16[128,1024]{1,0:T(8,128)(2,1)S(1)}, u32[]{:S(2)}, u32[]{:S(2)}) collective-permute-start(bf16[128,1024]{1,0:T(8,128)(2,1)S(1)} %collective-permute-done.18.b5), channel_id=1, source_target_pairs={{0,2},{1,5},{2,0},{3,7},{4,8},{5,1},{6,10},{7,3},{8,4},{9,13},{10,... | collective-permute-start | bytes 786440 | tf_op jit(solution)/shard_map/ppermute | solution.py:193
  62.4 2.5 %shard_map.76.acc_in = f32[256,1280]{1,0:T(8,128)S(1)} custom-call(bf16[128,1024]{1,0:T(8,128)(2,1)S(1)} %collective-permute-done.4.a4, bf16[128,1024]{1,0:T(8,128)(2,1)S(1)} %collective-permute-done.8.a5, bf16[128,1024]{1,0:T(8,128)(2,1)S(1)} %collective-permute-done.16.b4, bf16[128,1024]{1,0:T(8,128)(2,1)S(1)} %collective-permute-done.18.b5, ...), custom_call_target="tpu_custom_call" | custom-call | flops 1342177280 | bytes 6553600 | tf_op jit(solution)/shard_map/pallas_call | solution.py:490
  65.0 2.4 %shard_map.77 = (f32[128,1280]{1,0:T(8,128)S(1)}, f32[128,1280]{1,0:T(8,128)S(1)}) custom-call(bf16[128,1024]{1,0:T(8,128)(2,1)S(1)} %collective-permute-done.5.a6, bf16[128,1024]{1,0:T(8,128)(2,1)S(1)} %collective-permute-done.15.a7, bf16[128,1024]{1,0:T(8,128)(2,1)S(1)} %collective-permute-done.17.b6, f32[64,128]{1,0:T(8,128)S(1)} %bitcast.12, ...), custom_call_target="tpu_custom_call" | custom-call | flops 1342177280 | bytes 6553600 | tf_op jit(solution)/shard_map/pallas_call | solution.py:500
  75.3 2.1 %shard_map.80 = (bf16[128,1024]{1,0:T(8,128)(2,1)S(1)}, bf16[128,128]{1,0:T(8,128)(2,1)}, bf16[128,128]{1,0:T(8,128)(2,1)}) custom-call(s32[1,4]{1,0:T(1,128)S(1)} %copy-done.2, f32[128,1280]{1,0:T(8,128)S(1)} %shard_map.79.refs_1_, f32[256,128]{1,0:T(8,128)S(1)} %get-tuple-element.36.refs_2_, f32[256,128]{1,0:T(8,128)S(1)} %get-tuple-element.37.refs_3_, ...), custom_call_target="tpu_custom_call" | custom-call | flops 671088640 | bytes 5898240 | tf_op jit(solution)/shard_map/pallas_call | solution.py:516
  81.6 5.1 %collective-permute-done.21.b1 = bf16[128,1024]{1,0:T(8,128)(2,1)S(1)} collective-permute-done((bf16[128,1024]{1,0:T(8,128)(2,1)S(1)}, bf16[128,1024]{1,0:T(8,128)(2,1)S(1)}, u32[]{:S(2)}, u32[]{:S(2)}) %collective-permute-start.21) | collective-permute-done | bytes 262176 | tf_op jit(solution)/shard_map/ppermute | solution.py:193
  88.9 4.4 %collective-permute-done.30.b2 = bf16[128,1024]{1,0:T(8,128)(2,1)S(1)} collective-permute-done((bf16[128,1024]{1,0:T(8,128)(2,1)S(1)}, bf16[128,1024]{1,0:T(8,128)(2,1)S(1)}, u32[]{:S(2)}, u32[]{:S(2)}) %collective-permute-start.30) | collective-permute-done | bytes 262176 | tf_op jit(solution)/shard_map/ppermute | solution.py:193
  95.5 3.5 %collective-permute-done.22.b3 = bf16[128,1024]{1,0:T(8,128)(2,1)S(1)} collective-permute-done((bf16[128,1024]{1,0:T(8,128)(2,1)S(1)}, bf16[128,1024]{1,0:T(8,128)(2,1)S(1)}, u32[]{:S(2)}, u32[]{:S(2)}) %collective-permute-start.22) | collective-permute-done | bytes 262176 | tf_op jit(solution)/shard_map/ppermute | solution.py:193
  99.7 3.4 %shard_map.81.acc_in = f32[256,1024]{1,0:T(8,128)S(1)} custom-call(bf16[128,1024]{1,0:T(8,128)(2,1)S(1)} %get-tuple-element.38.a0, bf16[128,1024]{1,0:T(8,128)(2,1)S(1)} %collective-permute-done.19.a1, bf16[128,1024]{1,0:T(8,128)(2,1)S(1)} %collective-permute-done.25.a2, bf16[128,1024]{1,0:T(8,128)(2,1)S(1)} %collective-permute-done.28.a3, ...), custom_call_target="tpu_custom_call" | custom-call | flops 2147483648 | bytes 9437184 | tf_op jit(solution)/shard_map/pallas_call | solution.py:545
  105.2 3.0 %collective-permute-done.23.b5 = bf16[128,1024]{1,0:T(8,128)(2,1)S(1)} collective-permute-done((bf16[128,1024]{1,0:T(8,128)(2,1)S(1)}, bf16[128,1024]{1,0:T(8,128)(2,1)S(1)}, u32[]{:S(2)}, u32[]{:S(2)}) %collective-permute-start.23) | collective-permute-done | bytes 262176 | tf_op jit(solution)/shard_map/ppermute | solution.py:193
  108.1 2.2 %collective-permute-start.24 = (bf16[128,1024]{1,0:T(8,128)(2,1)S(1)}, bf16[128,1024]{1,0:T(8,128)(2,1)S(1)}, u32[]{:S(2)}, u32[]{:S(2)}) collective-permute-start(bf16[128,1024]{1,0:T(8,128)(2,1)S(1)} %collective-permute-done.23.b5), channel_id=1, source_target_pairs={{0,2},{1,5},{2,0},{3,7},{4,8},{5,1},{6,10},{7,3},{8,4},{9,13},{10,... | collective-permute-start | bytes 786440 | tf_op jit(solution)/shard_map/ppermute | solution.py:193
  112.3 2.5 %shard_map.83 = (bf16[256,1024]{1,0:T(8,128)(2,1)}, f32[128,1024]{1,0:T(8,128)S(1)}) custom-call(bf16[128,1024]{1,0:T(8,128)(2,1)S(1)} %collective-permute-done.27.a6, bf16[128,1024]{1,0:T(8,128)(2,1)S(1)} %collective-permute-done.32.a7, bf16[128,1024]{1,0:T(8,128)(2,1)S(1)} %collective-permute-done.34.b6, f32[256,1024]{1,0:T(8,128)S(1)} %shard_map.82.acc_in, ...), custom_call_target="tpu_custom_call" | custom-call | flops 1073741824 | bytes 5242880 | tf_op jit(solution)/shard_map/pallas_call | solution.py:570
  (80 shorter events, 44.4 us)
Async XLA Ops:
  0.0 50.0 %collective-permute-start.12 = (bf16[1024,4096]{1,0:T(8,128)(2,1)}, bf16[1024,4096]{1,0:T(8,128)(2,1)S(1)}, u32[]{:S(2)}, u32[]{:S(2)}) collective-permute-start(bf16[1024,4096]{1,0:T(8,128)(2,1)} %refs_0_.3), channel_id=1, source_target_pairs={{0,1},{1,0},{2,3},{3,2},{4,5},{5,4},{6,7},{7,6},{8,9},{9,8},{10,11... | collective-permute-start | bytes 25165832 | tf_op jit(solution)/shard_map/ppermute | solution.py:29
  0.5 99.2 %collective-permute-start.31 = (bf16[1024,4096]{1,0:T(8,128)(2,1)}, bf16[1024,4096]{1,0:T(8,128)(2,1)S(1)}, u32[]{:S(2)}, u32[]{:S(2)}) collective-permute-start(bf16[1024,4096]{1,0:T(8,128)(2,1)} %w0.7), channel_id=1, source_target_pairs={{0,1},{1,0},{2,3},{3,2},{4,5},{5,4},{6,7},{7,6},{8,9},{9,8},{10,11... | collective-permute-start | bytes 25165832 | tf_op jit(solution)/shard_map/ppermute | solution.py:29
  9.5 9.4 %collective-permute-start.3 = (bf16[128,1024]{1,0:T(8,128)(2,1)S(1)}, bf16[128,1024]{1,0:T(8,128)(2,1)S(1)}, u32[]{:S(2)}, u32[]{:S(2)}) collective-permute-start(bf16[128,1024]{1,0:T(8,128)(2,1)S(1)} %get-tuple-element.50.a0), channel_id=1, source_target_pairs={{0,2},{1,5},{2,0},{3,7},{4,8},{5,1},{6,10},{7,3},{8,4},{9,13},{10,... | collective-permute-start | bytes 786440 | tf_op jit(solution)/shard_map/ppermute | solution.py:193
  11.1 9.1 %collective-permute-start.6 = (bf16[128,1024]{1,0:T(8,128)(2,1)S(1)}, bf16[128,1024]{1,0:T(8,128)(2,1)S(1)}, u32[]{:S(2)}, u32[]{:S(2)}) collective-permute-start(bf16[128,1024]{1,0:T(8,128)(2,1)S(1)} %get-tuple-element.50.a0), channel_id=1, source_target_pairs={{0,4},{1,3},{2,6},{3,1},{4,0},{5,9},{6,2},{7,11},{8,12},{9,5},{10,... | collective-permute-start | bytes 786440 | tf_op jit(solution)/shard_map/ppermute | solution.py:193
  18.9 9.4 %collective-permute-start.10 = (bf16[128,1024]{1,0:T(8,128)(2,1)S(1)}, bf16[128,1024]{1,0:T(8,128)(2,1)S(1)}, u32[]{:S(2)}, u32[]{:S(2)}) collective-permute-start(bf16[128,1024]{1,0:T(8,128)(2,1)S(1)} %get-tuple-element.49.b0), channel_id=1, source_target_pairs={{0,2},{1,5},{2,0},{3,7},{4,8},{5,1},{6,10},{7,3},{8,4},{9,13},{10,... | collective-permute-start | bytes 786440 | tf_op jit(solution)/shard_map/ppermute | solution.py:193
  20.1 10.9 %collective-permute-start.4 = (bf16[128,1024]{1,0:T(8,128)(2,1)S(1)}, bf16[128,1024]{1,0:T(8,128)(2,1)S(1)}, u32[]{:S(2)}, u32[]{:S(2)}) collective-permute-start(bf16[128,1024]{1,0:T(8,128)(2,1)S(1)} %collective-permute-done.3.a2), channel_id=1, source_target_pairs={{0,4},{1,3},{2,6},{3,1},{4,0},{5,9},{6,2},{7,11},{8,12},{9,5},{10,... | collective-permute-start | bytes 786440 | tf_op jit(solution)/shard_map/ppermute | solution.py:193
  28.3 18.6 %collective-permute-start.13 = (bf16[128,4096]{1,0:T(8,128)(2,1)}, bf16[128,4096]{1,0:T(8,128)(2,1)S(1)}, u32[]{:S(2)}, u32[]{:S(2)}) collective-permute-start(bf16[128,4096]{1,0:T(8,128)(2,1)} %refs_1_.1), channel_id=1, source_target_pairs={{0,1},{1,0},{2,3},{3,2},{4,5},{5,4},{6,7},{7,6},{8,9},{9,8},{10,11... | collective-permute-start | bytes 3145736 | tf_op jit(solution)/shard_map/ppermute | solution.py:29
  31.0 18.0 %collective-permute-start.14 = (bf16[128,4096]{1,0:T(8,128)(2,1)}, bf16[128,4096]{1,0:T(8,128)(2,1)S(1)}, u32[]{:S(2)}, u32[]{:S(2)}) collective-permute-start(bf16[128,4096]{1,0:T(8,128)(2,1)} %refs_2_.1), channel_id=1, source_target_pairs={{0,1},{1,0},{2,3},{3,2},{4,5},{5,4},{6,7},{7,6},{8,9},{9,8},{10,11... | collective-permute-start | bytes 3145736 | tf_op jit(solution)/shard_map/ppermute | solution.py:29
  45.4 11.0 %collective-permute-start.8 = (bf16[128,1024]{1,0:T(8,128)(2,1)S(1)}, bf16[128,1024]{1,0:T(8,128)(2,1)S(1)}, u32[]{:S(2)}, u32[]{:S(2)}) collective-permute-start(bf16[128,1024]{1,0:T(8,128)(2,1)S(1)} %collective-permute-done.7.a3), channel_id=1, source_target_pairs={{0,4},{1,3},{2,6},{3,1},{4,0},{5,9},{6,2},{7,11},{8,12},{9,5},{10,... | collective-permute-start | bytes 786440 | tf_op jit(solution)/shard_map/ppermute | solution.py:193
  46.9 18.1 %collective-permute-start.5 = (bf16[128,1024]{1,0:T(8,128)(2,1)S(1)}, bf16[128,1024]{1,0:T(8,128)(2,1)S(1)}, u32[]{:S(2)}, u32[]{:S(2)}) collective-permute-start(bf16[128,1024]{1,0:T(8,128)(2,1)S(1)} %collective-permute-done.4.a4), channel_id=1, source_target_pairs={{0,2},{1,5},{2,0},{3,7},{4,8},{5,1},{6,10},{7,3},{8,4},{9,13},{10,... | collective-permute-start | bytes 786440 | tf_op jit(solution)/shard_map/ppermute | solution.py:193
  49.0 11.2 %collective-permute-start.18 = (bf16[128,1024]{1,0:T(8,128)(2,1)S(1)}, bf16[128,1024]{1,0:T(8,128)(2,1)S(1)}, u32[]{:S(2)}, u32[]{:S(2)}) collective-permute-start(bf16[128,1024]{1,0:T(8,128)(2,1)S(1)} %collective-permute-done.11.b3), channel_id=1, source_target_pairs={{0,4},{1,3},{2,6},{3,1},{4,0},{5,9},{6,2},{7,11},{8,12},{9,5},{10,... | collective-permute-start | bytes 786440 | tf_op jit(solution)/shard_map/ppermute | solution.py:193
  50.0 15.0 %collective-permute-start.17 = (bf16[128,1024]{1,0:T(8,128)(2,1)S(1)}, bf16[128,1024]{1,0:T(8,128)(2,1)S(1)}, u32[]{:S(2)}, u32[]{:S(2)}) collective-permute-start(bf16[128,1024]{1,0:T(8,128)(2,1)S(1)} %collective-permute-done.16.b4), channel_id=1, source_target_pairs={{0,2},{1,5},{2,0},{3,7},{4,8},{5,1},{6,10},{7,3},{8,4},{9,13},{10,... | collective-permute-start | bytes 786440 | tf_op jit(solution)/shard_map/ppermute | solution.py:193
  60.2 11.9 %collective-permute-start.20 = (bf16[128,1024]{1,0:T(8,128)(2,1)S(1)}, bf16[128,1024]{1,0:T(8,128)(2,1)S(1)}, u32[]{:S(2)}, u32[]{:S(2)}) collective-permute-start(bf16[128,1024]{1,0:T(8,128)(2,1)S(1)} %collective-permute-done.18.b5), channel_id=1, source_target_pairs={{0,2},{1,5},{2,0},{3,7},{4,8},{5,1},{6,10},{7,3},{8,4},{9,13},{10,... | collective-permute-start | bytes 786440 | tf_op jit(solution)/shard_map/ppermute | solution.py:193
  70.1 10.6 %collective-permute-start.25 = (bf16[128,1024]{1,0:T(8,128)(2,1)S(1)}, bf16[128,1024]{1,0:T(8,128)(2,1)S(1)}, u32[]{:S(2)}, u32[]{:S(2)}) collective-permute-start(bf16[128,1024]{1,0:T(8,128)(2,1)S(1)} %get-tuple-element.38.a0), channel_id=1, source_target_pairs={{0,2},{1,5},{2,0},{3,7},{4,8},{5,1},{6,10},{7,3},{8,4},{9,13},{10,... | collective-permute-start | bytes 786440 | tf_op jit(solution)/shard_map/ppermute | solution.py:193
  77.5 9.2 %collective-permute-start.21 = (bf16[128,1024]{1,0:T(8,128)(2,1)S(1)}, bf16[128,1024]{1,0:T(8,128)(2,1)S(1)}, u32[]{:S(2)}, u32[]{:S(2)}) collective-permute-start(bf16[128,1024]{1,0:T(8,128)(2,1)S(1)} %get-tuple-element.43.b0), channel_id=1, source_target_pairs={{0,4},{1,3},{2,6},{3,1},{4,0},{5,9},{6,2},{7,11},{8,12},{9,5},{10,... | collective-permute-start | bytes 786440 | tf_op jit(solution)/shard_map/ppermute | solution.py:193
  78.7 9.2 %collective-permute-start.28 = (bf16[128,1024]{1,0:T(8,128)(2,1)S(1)}, bf16[128,1024]{1,0:T(8,128)(2,1)S(1)}, u32[]{:S(2)}, u32[]{:S(2)}) collective-permute-start(bf16[128,1024]{1,0:T(8,128)(2,1)S(1)} %collective-permute-done.19.a1), channel_id=1, source_target_pairs={{0,2},{1,5},{2,0},{3,7},{4,8},{5,1},{6,10},{7,3},{8,4},{9,13},{10,... | collective-permute-start | bytes 786440 | tf_op jit(solution)/shard_map/ppermute | solution.py:193
  80.7 12.6 %collective-permute-start.30 = (bf16[128,1024]{1,0:T(8,128)(2,1)S(1)}, bf16[128,1024]{1,0:T(8,128)(2,1)S(1)}, u32[]{:S(2)}, u32[]{:S(2)}) collective-permute-start(bf16[128,1024]{1,0:T(8,128)(2,1)S(1)} %get-tuple-element.43.b0), channel_id=1, source_target_pairs={{0,2},{1,5},{2,0},{3,7},{4,8},{5,1},{6,10},{7,3},{8,4},{9,13},{10,... | collective-permute-start | bytes 786440 | tf_op jit(solution)/shard_map/ppermute | solution.py:193
  80.7 13.3 %collective-permute-start.26 = (bf16[128,1024]{1,0:T(8,128)(2,1)S(1)}, bf16[128,1024]{1,0:T(8,128)(2,1)S(1)}, u32[]{:S(2)}, u32[]{:S(2)}) collective-permute-start(bf16[128,1024]{1,0:T(8,128)(2,1)S(1)} %collective-permute-done.25.a2), channel_id=1, source_target_pairs={{0,4},{1,3},{2,6},{3,1},{4,0},{5,9},{6,2},{7,11},{8,12},{9,5},{10,... | collective-permute-start | bytes 786440 | tf_op jit(solution)/shard_map/ppermute | solution.py:193
  86.7 12.2 %collective-permute-start.22 = (bf16[128,1024]{1,0:T(8,128)(2,1)S(1)}, bf16[128,1024]{1,0:T(8,128)(2,1)S(1)}, u32[]{:S(2)}, u32[]{:S(2)}) collective-permute-start(bf16[128,1024]{1,0:T(8,128)(2,1)S(1)} %collective-permute-done.21.b1), channel_id=1, source_target_pairs={{0,2},{1,5},{2,0},{3,7},{4,8},{5,1},{6,10},{7,3},{8,4},{9,13},{10,... | collective-permute-start | bytes 786440 | tf_op jit(solution)/shard_map/ppermute | solution.py:193
  87.9 15.2 %collective-permute-start.29 = (bf16[128,1024]{1,0:T(8,128)(2,1)S(1)}, bf16[128,1024]{1,0:T(8,128)(2,1)S(1)}, u32[]{:S(2)}, u32[]{:S(2)}) collective-permute-start(bf16[128,1024]{1,0:T(8,128)(2,1)S(1)} %collective-permute-done.28.a3), channel_id=1, source_target_pairs={{0,4},{1,3},{2,6},{3,1},{4,0},{5,9},{6,2},{7,11},{8,12},{9,5},{10,... | collective-permute-start | bytes 786440 | tf_op jit(solution)/shard_map/ppermute | solution.py:193
  93.3 11.1 %collective-permute-start.33 = (bf16[128,1024]{1,0:T(8,128)(2,1)S(1)}, bf16[128,1024]{1,0:T(8,128)(2,1)S(1)}, u32[]{:S(2)}, u32[]{:S(2)}) collective-permute-start(bf16[128,1024]{1,0:T(8,128)(2,1)S(1)} %collective-permute-done.30.b2), channel_id=1, source_target_pairs={{0,4},{1,3},{2,6},{3,1},{4,0},{5,9},{6,2},{7,11},{8,12},{9,5},{10,... | collective-permute-start | bytes 786440 | tf_op jit(solution)/shard_map/ppermute | solution.py:193
  94.0 18.0 %collective-permute-start.27 = (bf16[128,1024]{1,0:T(8,128)(2,1)S(1)}, bf16[128,1024]{1,0:T(8,128)(2,1)S(1)}, u32[]{:S(2)}, u32[]{:S(2)}) collective-permute-start(bf16[128,1024]{1,0:T(8,128)(2,1)S(1)} %collective-permute-done.26.a4), channel_id=1, source_target_pairs={{0,2},{1,5},{2,0},{3,7},{4,8},{5,1},{6,10},{7,3},{8,4},{9,13},{10,... | collective-permute-start | bytes 786440 | tf_op jit(solution)/shard_map/ppermute | solution.py:193
  98.9 9.2 %collective-permute-start.23 = (bf16[128,1024]{1,0:T(8,128)(2,1)S(1)}, bf16[128,1024]{1,0:T(8,128)(2,1)S(1)}, u32[]{:S(2)}, u32[]{:S(2)}) collective-permute-start(bf16[128,1024]{1,0:T(8,128)(2,1)S(1)} %collective-permute-done.22.b3), channel_id=1, source_target_pairs={{0,4},{1,3},{2,6},{3,1},{4,0},{5,9},{6,2},{7,11},{8,12},{9,5},{10,... | collective-permute-start | bytes 786440 | tf_op jit(solution)/shard_map/ppermute | solution.py:193
  103.1 9.0 %collective-permute-start.32 = (bf16[128,1024]{1,0:T(8,128)(2,1)S(1)}, bf16[128,1024]{1,0:T(8,128)(2,1)S(1)}, u32[]{:S(2)}, u32[]{:S(2)}) collective-permute-start(bf16[128,1024]{1,0:T(8,128)(2,1)S(1)} %collective-permute-done.29.a5), channel_id=1, source_target_pairs={{0,2},{1,5},{2,0},{3,7},{4,8},{5,1},{6,10},{7,3},{8,4},{9,13},{10,... | collective-permute-start | bytes 786440 | tf_op jit(solution)/shard_map/ppermute | solution.py:193
  (16 other events, 178.8 us)

commit v5 on v4

--- a/solution.py
+++ b/solution.py
@@ -210,13 +210,15 @@
     return mine, pl.ds(pl.multiple_of(t % (RING // 2) * UNIT, UNIT), UNIT)
 
 
-def add_units(xs, acc, own, others, first, count):
+def add_units(xs, acc, own, others, first, count, ready=None):
     def unit_step(u, carry):
         mine, cols = columns_of(first + u)
         for here, parts in ((mine, own), (jnp.logical_not(mine), others)):
 
             @pl.when(here)
             def _(parts=parts):
+                if ready is not None and parts is own:
+                    ready(first + u)
                 at = 0
                 for part in parts:
                     rows = part.shape[0]
@@ -228,18 +230,24 @@
     lax.fori_loop(0, count, unit_step, 0)
 
 
-def load_kernel(spans, *refs):
-    *sources, target, sems = refs
-    copies = []
-    at = 0
-    for n, (source, (start, rows)) in enumerate(zip(sources, spans)):
-        where = target.at[pl.ds(at, rows), :]
-        copies.append(pltpu.make_async_copy(source.at[pl.ds(start, rows), :], where, sems.at[n]))
-        at += rows
-    for copy in copies:
-        copy.start()
-    for copy in copies:
-        copy.wait()
+def fetch_unit(moves, sems, index, go):
+    _, cols = columns_of(index)
+    for n, (source, target) in enumerate(moves):
+        copy = pltpu.make_async_copy(source.at[:, cols], target.at[:, cols], sems.at[n, index])
+        copy.start() if go else copy.wait()
+
+
+def each_own_unit(first, count, action):
+    def unit_step(u, carry):
+        mine, _ = columns_of(u)
+
+        @pl.when(mine)
+        def _():
+            action(u)
+
+        return carry
+
+    lax.fori_loop(first, first + count, unit_step, 0)
 
 
 def normed_unit(part, factor, gain_ref, index):
@@ -285,17 +293,29 @@
 
 
 def early_kernel(a0, a1, a2, a3, b0, b1, b2, b3, gain, factor, *refs):
-    *weights, acc, xs = refs
+    query, key, value = refs[:3]
+    others = refs[3:6]
+    acc, top, bottom, both, xs, sems = refs[6:]
+    rows, kv = top.shape[0], key.shape[0]
+    moves = (
+        (query.at[pl.ds(0, rows), :], top),
+        (query.at[pl.ds(rows, rows), :], bottom),
+        (key, both.at[pl.ds(0, kv), :]),
+        (value, both.at[pl.ds(kv, kv), :]),
+    )
+    each_own_unit(0, RING, lambda u: fetch_unit(moves, sems, u, True))
     normed_units(xs, gain, factor, 0, (a0, a1, a2, a3), (b0, b1, b2, b3))
     acc[...] = jnp.zeros_like(acc)
-    add_units(xs, acc, weights[:2], weights[2:], 0, 4)
+    wait = lambda u: fetch_unit(moves, sems, u, False)
+    add_units(xs, acc, (top, bottom, both), others, 0, 4, wait)
+    each_own_unit(4, 4, wait)
 
 
 def middle_kernel(a4, a5, b4, b5, gain, factor, acc_in, *refs):
     *weights, acc, xs = refs
     normed_units(xs, gain, factor, 4, (a4, a5), (b4, b5))
     acc[...] = acc_in[...]
-    add_units(xs, acc, weights[:2], weights[2:], 4, 2)
+    add_units(xs, acc, weights[:3], weights[3:], 4, 2)
 
 
 def project_first_kernel(a6, a7, b6, gain, factor, acc_in, *refs):
@@ -303,17 +323,17 @@
     normed_units(xs, gain, factor, 6, (a6,), (b6,))
     normed_units(late, gain, factor, 7, (a7,))
     acc[...] = acc_in[...]
-    add_units(xs, acc, weights[:2], weights[2:], 6, 1)
+    add_units(xs, acc, weights[:3], weights[3:], 6, 1)
     first[...] = acc[:ROWS, :]
     second[...] = acc[ROWS:, :]
-    add_units(late, first, weights[:2], weights[2:], 7, 1)
+    add_units(late, first, weights[:3], weights[3:], 7, 1)
 
 
 def project_second_kernel(b7, gain, factor, acc_in, *refs):
     *weights, acc, late = refs
     place_unit(late, slice(0, ROWS), 0, b7[...], factor[ROWS:, :], gain, 7)
     acc[...] = acc_in[...]
-    add_units(late, acc, weights[:2], weights[2:], 7, 1)
+    add_units(late, acc, weights[:3], weights[3:], 7, 1)
 
 
 def turned_heads(part, cosine, sine):
@@ -409,26 +429,18 @@
     return pltpu.with_memory_space_constraint(value, pltpu.VMEM)
 
 
-def load(arrays, spans):
-    rows = sum(span for _, span in spans)
-    return kernel_call(
-        lambda *refs: load_kernel(spans, *refs),
-        out_shape=jax.ShapeDtypeStruct((rows, arrays[0].shape[1]), arrays[0].dtype),
-        in_specs=[HBM] * len(arrays),
-        out_specs=VM,
-        scratch_shapes=[pltpu.SemaphoreType.DMA((len(arrays),))],
-        compiler_params=params(2),
-        cost_estimate=cost(0, rows * arrays[0].shape[1] // UNIT, 1),
-    )(*(pltpu.with_memory_space_constraint(w, pltpu.HBM) for w in arrays))
-
-
-def token_position(lengths):
-    count = lengths.shape[0]
-    upto = jnp.arange(count)[:, None] >= jnp.arange(count)[None, :]
-    ends = jnp.sum(jnp.where(upto, lengths[None, :], 0), axis=1)
-    offsets = jnp.arange(STRETCH, dtype=jnp.int32)
-    finished = ends[None, :] <= offsets[:, None]
-    return offsets - jnp.sum(jnp.where(finished, lengths[None, :], 0), axis=1)
+def in_hbm(value):
+    return pltpu.with_memory_space_constraint(value, pltpu.HBM)
+
+
+def angle_kernel(lens, freq, angle):
+    place = lax.broadcasted_iota(jnp.int32, angle.shape, 0)
+    position = place
+    end = jnp.int32(0)
+    for k in range(lens.shape[1]):
+        end = end + lens[0, k]
+        position = position - jnp.where(end <= place, lens[0, k], 0)
+    angle[...] = position.astype(jnp.float32) * freq[...]
 
 
 def after(value, *others):
@@ -455,42 +467,49 @@
     factor = lax.rsqrt(squares / (RING * UNIT) + 1e-05)
     factor = jnp.broadcast_to(factor.reshape(STRETCH, 1), (STRETCH, 128))
     gain = norm_gain.reshape(RING * UNIT // 128, 128)
-    position = token_position(lengths[0])
     lane = jnp.arange(HD, dtype=jnp.int32)
-    angle = position.astype(f32)[:, None] * scaled_freq(lane - lane % 2)[None, :]
+    angle = kernel_call(
+        angle_kernel,
+        out_shape=jax.ShapeDtypeStruct((STRETCH, HD), f32),
+        in_specs=[SM, VM],
+        out_specs=VM,
+        compiler_params=params(2),
+    )(lengths, scaled_freq(lane - lane % 2)[None, :])
     cosine = jnp.cos(angle)
     sine = jnp.sin(angle) * jnp.where(lane % 2 == 0, -1.0, 1.0)[None, :]
     a3, b3 = swapped(a1, 1), swapped(b1, 1)
     a4, b4 = swapped(a2, 0), swapped(b2, 0)
     other_output = in_vmem(partner(output_weight, "pair", 0))
-    cut = query_weight.shape[0] // 2
-    own_first = load((query_weight,), ((0, cut),))
-    own_second = load(
-        projections,
-        ((cut, query_weight.shape[0] - cut), (0, key_weight.shape[0]), (0, value_weight.shape[0])),
-    )
-    a3, own_first = after(a3, own_first)
-    a4, own_second = after(a4, own_second)
-    weights = (own_first, own_second, *others)
     a5, b5 = swapped(a3, 0), swapped(b3, 0)
     a6, b6 = swapped(a4, 1), swapped(b4, 1)
     factor, cosine, sine, lengths = after(factor, cosine, sine, lengths)
     acc_shape = jax.ShapeDtypeStruct((STRETCH, qkv), f32)
-    acc = kernel_call(
+    columns = query_weight.shape[1]
+    half_query = jax.ShapeDtypeStruct((query_weight.shape[0] // 2, columns), bf16)
+    both = jax.ShapeDtypeStruct((qkv - query_weight.shape[0], columns), bf16)
+    acc, *own = kernel_call(
         early_kernel,
-        out_shape=acc_shape,
-        in_specs=[VM] * 15,
-        out_specs=VM,
-        scratch_shapes=[pltpu.VMEM((4, STRETCH, UNIT), bf16)],
+        out_shape=(acc_shape, half_query, half_query, both),
+        in_specs=[VM] * 10 + [HBM] * 3 + [VM] * 3,
+        out_specs=(VM,) * 4,
+        scratch_shapes=[
+            pltpu.VMEM((4, STRETCH, UNIT), bf16),
+            pltpu.SemaphoreType.DMA((4, RING)),
+        ],
         compiler_params=params(10),
         cost_estimate=cost(STRETCH, 4, qkv),
-    )(a0, a1, a2, a3, b0, b1, b2, b3, gain, factor, *weights)
+    )(
+        *(a0, a1, a2, a3, b0, b1, b2, b3, gain, factor),
+        *(in_hbm(w) for w in projections),
+        *others,
+    )
+    weights = (*own, *others)
     a5, acc = after(a5, acc)
     a7, b7 = swapped(a5, 1), swapped(b5, 1)
     acc = kernel_call(
         middle_kernel,
         out_shape=acc_shape,
-        in_specs=[VM] * 12,
+        in_specs=[VM] * 13,
         out_specs=VM,
         scratch_shapes=[pltpu.VMEM((2, STRETCH, UNIT), bf16)],
         compiler_params=params(8),
@@ -500,7 +519,7 @@
     first, second = kernel_call(
         project_first_kernel,
         out_shape=(half_shape, half_shape),
-        in_specs=[VM] * 11,
+        in_specs=[VM] * 12,
         out_specs=(VM, VM),
         scratch_shapes=[
             pltpu.VMEM((STRETCH, qkv), f32),
@@ -527,7 +546,7 @@
     projected = kernel_call(
         project_second_kernel,
         out_shape=half_shape,
-        in_specs=[VM] * 9,
+        in_specs=[VM] * 10,
         out_specs=VM,
         scratch_shapes=[pltpu.VMEM((1, ROWS, UNIT), bf16)],
         compiler_params=params(10),

time: 117 us -> 119 us (1.017)
  starting transfers between devices: 44.9 us -> 49.9 us
  Pallas kernels: 28.3 us -> 25.2 us
  other arithmetic: 3.31 us -> 1.73 us
  local copies, waits for them, and re-layouts: 1.19 us -> 2.59 us
    ppermute x28, starting transfers between devices: 37.9 us -> 41.7 us  [swapped(): return lax.ppermute(shard, ('tp', 'pair'), ring_swap(later))]
    pallas_call x4 -> x3, Pallas kernels: 11.9 us -> 8.8 us  [the longest x1 5.71 us: ring_layer(): kernel_call(early_kernel, out_shape=(acc_shape, half_query, half_query, b...]
    ppermute x28, waiting for transfers between devices: 32.8 us -> 35.6 us  [swapped(): return lax.ppermute(shard, ('tp', 'pair'), ring_swap(later))]
    ppermute x3, waiting for transfers between devices: 5.9 us -> 3.68 us  [summed_over_tp(): value = value + lax.ppermute(value, ('tp', 'pair'), pairs)]
    reduce_sum x2 -> x0, other arithmetic: 1.51 us -> none  [the longest x1 0.77 us: token_position(): ends = jnp.sum(jnp.where(upto, lengths[None, :], 0), axis=1)]
    unnamed x10 -> x12, local copies, waits for them, and re-layouts: 0.03 us -> 1.43 us
    ppermute x3, starting transfers between devices: 6.51 us -> 7.72 us  [summed_over_tp(): value = value + lax.ppermute(value, ('tp', 'pair'), pairs)]
  transfers between devices with their start and end apart: 35 -> 35, of which waited for: 15 -> 17; matrix products, arithmetic and copies ran while one was open for 4% -> 2% of each run, Pallas kernels for 23% -> 20%
where the time goes in v5:
time: 119 us
  starting transfers between devices  49.9 us (42%)
  waiting for transfers between devices  39.3 us (33%)
  Pallas kernels  25.2 us (21%)
  local copies, waits for them, and re-layouts  2.59 us (2%)
  other arithmetic  1.73 us (1%)
    ppermute x28, starting transfers between devices, swapped(): return lax.ppermute(shard, ('tp', 'pair'), ring_swap(later))  41.7 us
    ppermute x28, waiting for transfers between devices, swapped(): return lax.ppermute(shard, ('tp', 'pair'), ring_swap(later))  35.6 us
    ppermute x3, starting transfers between devices, summed_over_tp(): value = value + lax.ppermute(value, ('tp', 'pair'), pairs)  7.72 us
    pallas_call x1, Pallas kernels, ring_layer(): kernel_call(early_kernel, out_shape=(acc_shape, half_query, half_query, b...  5.71 us
    ppermute x3, waiting for transfers between devices, summed_over_tp(): value = value + lax.ppermute(value, ('tp', 'pair'), pairs)  3.68 us
    pallas_call x2, Pallas kernels, attend_stream(): kernel_call(lambda *refs: attend_kernel(half, *refs), out_shape=(jax.Shap...  3.57 us
    pallas_call x1, Pallas kernels, ring_layer(): kernel_call(out_early_kernel, out_shape=acc_shape, in_specs=[VM] * 10, ou...  3.37 us
    pallas_call x1, Pallas kernels, ring_layer(): kernel_call(out_first_kernel, grid=(1,), out_shape=(out_shape, half_shape...  2.48 us
  transfers between devices with their start and end apart: 35, of which 17 were waited for; matrix products, arithmetic and copies ran while one was open for 2% of the time, Pallas kernels for 20%

profile of v5, /device:TPU:0, one launch (start us, length us, event | category | flops | bytes accessed | tf_op | source)
XLA Modules:
  0.0 119.0 jit_solution(470118623798532776)
XLA Ops:
  1.7 3.0 %collective-permute-start = (f32[2,128]{1,0:T(2,128)S(1)}, f32[2,128]{1,0:T(2,128)S(1)}, u32[]{:S(2)}, u32[]{:S(2)}) collective-permute-start(f32[2,128]{1,0:T(2,128)S(1)} %bitcast.13), channel_id=1, source_target_pairs={{0,2},{1,5},{2,0},{3,7},{4,6},{5,1},{6,4},{7,3},{8,10},{9,13},{10,... | collective-permute-start | bytes 3080 | tf_op jit(solution)/shard_map/ppermute | solution.py:420
  11.6 2.6 %collective-permute-start.2 = (f32[2,128]{1,0:T(2,128)S(1)}, f32[2,128]{1,0:T(2,128)S(1)}, u32[]{:S(2)}, u32[]{:S(2)}) collective-permute-start(f32[2,128]{1,0:T(2,128)S(1)} %fusion.4), channel_id=1, source_target_pairs={{0,8},{1,9},{2,10},{3,11},{4,12},{5,13},{6,14},{7,15},{8,0},{9,1},... | collective-permute-start | bytes 3080 | tf_op jit(solution)/shard_map/ppermute | solution.py:420
  20.4 2.3 %collective-permute-done.10.b2 = bf16[128,1024]{1,0:T(8,128)(2,1)S(1)} collective-permute-done((bf16[128,1024]{1,0:T(8,128)(2,1)S(1)}, bf16[128,1024]{1,0:T(8,128)(2,1)S(1)}, u32[]{:S(2)}, u32[]{:S(2)}) %collective-permute-start.10) | collective-permute-done | bytes 262176 | tf_op jit(solution)/shard_map/ppermute | solution.py:193
  25.5 2.8 %collective-permute-done.11.b3 = bf16[128,1024]{1,0:T(8,128)(2,1)S(1)} collective-permute-done((bf16[128,1024]{1,0:T(8,128)(2,1)S(1)}, bf16[128,1024]{1,0:T(8,128)(2,1)S(1)}, u32[]{:S(2)}, u32[]{:S(2)}) %collective-permute-start.11) | collective-permute-done | bytes 262176 | tf_op jit(solution)/shard_map/ppermute | solution.py:193
  28.3 2.8 %collective-permute-done.7.a3 = bf16[128,1024]{1,0:T(8,128)(2,1)S(1)} collective-permute-done((bf16[128,1024]{1,0:T(8,128)(2,1)S(1)}, bf16[128,1024]{1,0:T(8,128)(2,1)S(1)}, u32[]{:S(2)}, u32[]{:S(2)}) %collective-permute-start.7) | collective-permute-done | bytes 262176 | tf_op jit(solution)/shard_map/ppermute | solution.py:193
  31.1 5.3 %collective-permute-start.16 = (bf16[128,1024]{1,0:T(8,128)(2,1)S(1)}, bf16[128,1024]{1,0:T(8,128)(2,1)S(1)}, u32[]{:S(2)}, u32[]{:S(2)}) collective-permute-start(bf16[128,1024]{1,0:T(8,128)(2,1)S(1)} %collective-permute-done.10.b2), channel_id=1, source_target_pairs={{0,4},{1,3},{2,6},{3,1},{4,0},{5,9},{6,2},{7,11},{8,12},{9,5},{10,... | collective-permute-start | bytes 786440 | tf_op jit(solution)/shard_map/ppermute | solution.py:193
  36.5 4.3 %collective-permute-done.16.b4 = bf16[128,1024]{1,0:T(8,128)(2,1)S(1)} collective-permute-done((bf16[128,1024]{1,0:T(8,128)(2,1)S(1)}, bf16[128,1024]{1,0:T(8,128)(2,1)S(1)}, u32[]{:S(2)}, u32[]{:S(2)}) %collective-permute-start.16) | collective-permute-done | bytes 262176 | tf_op jit(solution)/shard_map/ppermute | solution.py:193
  44.6 2.7 %collective-permute-done.4.a4 = bf16[128,1024]{1,0:T(8,128)(2,1)S(1)} collective-permute-done((bf16[128,1024]{1,0:T(8,128)(2,1)S(1)}, bf16[128,1024]{1,0:T(8,128)(2,1)S(1)}, u32[]{:S(2)}, u32[]{:S(2)}) %collective-permute-start.4) | collective-permute-done | bytes 262176 | tf_op jit(solution)/shard_map/ppermute | solution.py:193
  47.2 2.3 %collective-permute-start.8 = (bf16[128,1024]{1,0:T(8,128)(2,1)S(1)}, bf16[128,1024]{1,0:T(8,128)(2,1)S(1)}, u32[]{:S(2)}, u32[]{:S(2)}) collective-permute-start(bf16[128,1024]{1,0:T(8,128)(2,1)S(1)} %collective-permute-done.7.a3), channel_id=1, source_target_pairs={{0,4},{1,3},{2,6},{3,1},{4,0},{5,9},{6,2},{7,11},{8,12},{9,5},{10,... | collective-permute-start | bytes 786440 | tf_op jit(solution)/shard_map/ppermute | solution.py:193
  49.8 2.5 %collective-permute-start.17 = (bf16[128,1024]{1,0:T(8,128)(2,1)S(1)}, bf16[128,1024]{1,0:T(8,128)(2,1)S(1)}, u32[]{:S(2)}, u32[]{:S(2)}) collective-permute-start(bf16[128,1024]{1,0:T(8,128)(2,1)S(1)} %collective-permute-done.16.b4), channel_id=1, source_target_pairs={{0,2},{1,5},{2,0},{3,7},{4,8},{5,1},{6,10},{7,3},{8,4},{9,13},{10,... | collective-permute-start | bytes 786440 | tf_op jit(solution)/shard_map/ppermute | solution.py:193
  53.1 5.7 %shard_map.74 = (f32[256,1280]{1,0:T(8,128)S(1)}, bf16[512,4096]{1,0:T(8,128)(2,1)S(1)}, bf16[512,4096]{1,0:T(8,128)(2,1)S(1)}, bf16[256,4096]{1,0:T(8,128)(2,1)S(1)}) custom-call(bf16[128,1024]{1,0:T(8,128)(2,1)S(1)} %get-tuple-element.50.a0, bf16[128,1024]{1,0:T(8,128)(2,1)S(1)} %collective-permute-done.6.a1, ...), custom_call_target="tpu_custom_call" | custom-call | flops 2684354560 | bytes 11796480 | tf_op jit(solution)/shard_map/pallas_call | solution.py:490
  62.2 2.4 %collective-permute-start.20 = (bf16[128,1024]{1,0:T(8,128)(2,1)S(1)}, bf16[128,1024]{1,0:T(8,128)(2,1)S(1)}, u32[]{:S(2)}, u32[]{:S(2)}) collective-permute-start(bf16[128,1024]{1,0:T(8,128)(2,1)S(1)} %collective-permute-done.18.b5), channel_id=1, source_target_pairs={{0,2},{1,5},{2,0},{3,7},{4,8},{5,1},{6,10},{7,3},{8,4},{9,13},{10,... | collective-permute-start | bytes 786440 | tf_op jit(solution)/shard_map/ppermute | solution.py:193
  64.6 2.5 %shard_map.75.acc_in = f32[256,1280]{1,0:T(8,128)S(1)} custom-call(bf16[128,1024]{1,0:T(8,128)(2,1)S(1)} %collective-permute-done.4.a4, bf16[128,1024]{1,0:T(8,128)(2,1)S(1)} %collective-permute-done.8.a5, bf16[128,1024]{1,0:T(8,128)(2,1)S(1)} %collective-permute-done.16.b4, bf16[128,1024]{1,0:T(8,128)(2,1)S(1)} %collective-permute-done.18.b5, ...), custom_call_target="tpu_custom_call" | custom-call | flops 1342177280 | bytes 6553600 | tf_op jit(solution)/shard_map/pallas_call | solution.py:509
  67.1 2.4 %shard_map.76 = (f32[128,1280]{1,0:T(8,128)S(1)}, f32[128,1280]{1,0:T(8,128)S(1)}) custom-call(bf16[128,1024]{1,0:T(8,128)(2,1)S(1)} %collective-permute-done.5.a6, bf16[128,1024]{1,0:T(8,128)(2,1)S(1)} %collective-permute-done.15.a7, bf16[128,1024]{1,0:T(8,128)(2,1)S(1)} %collective-permute-done.17.b6, f32[64,128]{1,0:T(8,128)S(1)} %bitcast.11, ...), custom_call_target="tpu_custom_call" | custom-call | flops 1342177280 | bytes 6553600 | tf_op jit(solution)/shard_map/pallas_call | solution.py:519
  71.0 2.2 %collective-permute-start.25 = (bf16[128,1024]{1,0:T(8,128)(2,1)S(1)}, bf16[128,1024]{1,0:T(8,128)(2,1)S(1)}, u32[]{:S(2)}, u32[]{:S(2)}) collective-permute-start(bf16[128,1024]{1,0:T(8,128)(2,1)S(1)} %get-tuple-element.38.a0), channel_id=1, source_target_pairs={{0,2},{1,5},{2,0},{3,7},{4,8},{5,1},{6,10},{7,3},{8,4},{9,13},{10,... | collective-permute-start | bytes 786440 | tf_op jit(solution)/shard_map/ppermute | solution.py:193
  74.6 2.8 %collective-permute-done.19.a1 = bf16[128,1024]{1,0:T(8,128)(2,1)S(1)} collective-permute-done((bf16[128,1024]{1,0:T(8,128)(2,1)S(1)}, bf16[128,1024]{1,0:T(8,128)(2,1)S(1)}, u32[]{:S(2)}, u32[]{:S(2)}) %collective-permute-start.19) | collective-permute-done | bytes 262176 | tf_op jit(solution)/shard_map/ppermute | solution.py:193
  79.6 2.2 %collective-permute-start.28 = (bf16[128,1024]{1,0:T(8,128)(2,1)S(1)}, bf16[128,1024]{1,0:T(8,128)(2,1)S(1)}, u32[]{:S(2)}, u32[]{:S(2)}) collective-permute-start(bf16[128,1024]{1,0:T(8,128)(2,1)S(1)} %collective-permute-done.19.a1), channel_id=1, source_target_pairs={{0,2},{1,5},{2,0},{3,7},{4,8},{5,1},{6,10},{7,3},{8,4},{9,13},{10,... | collective-permute-start | bytes 786440 | tf_op jit(solution)/shard_map/ppermute | solution.py:193
  83.7 5.1 %collective-permute-done.21.b1 = bf16[128,1024]{1,0:T(8,128)(2,1)S(1)} collective-permute-done((bf16[128,1024]{1,0:T(8,128)(2,1)S(1)}, bf16[128,1024]{1,0:T(8,128)(2,1)S(1)}, u32[]{:S(2)}, u32[]{:S(2)}) %collective-permute-start.21) | collective-permute-done | bytes 262176 | tf_op jit(solution)/shard_map/ppermute | solution.py:193
  90.8 3.3 %collective-permute-done.30.b2 = bf16[128,1024]{1,0:T(8,128)(2,1)S(1)} collective-permute-done((bf16[128,1024]{1,0:T(8,128)(2,1)S(1)}, bf16[128,1024]{1,0:T(8,128)(2,1)S(1)}, u32[]{:S(2)}, u32[]{:S(2)}) %collective-permute-start.30) | collective-permute-done | bytes 262176 | tf_op jit(solution)/shard_map/ppermute | solution.py:193
  94.1 2.3 %collective-permute-start.33 = (bf16[128,1024]{1,0:T(8,128)(2,1)S(1)}, bf16[128,1024]{1,0:T(8,128)(2,1)S(1)}, u32[]{:S(2)}, u32[]{:S(2)}) collective-permute-start(bf16[128,1024]{1,0:T(8,128)(2,1)S(1)} %collective-permute-done.30.b2), channel_id=1, source_target_pairs={{0,4},{1,3},{2,6},{3,1},{4,0},{5,9},{6,2},{7,11},{8,12},{9,5},{10,... | collective-permute-start | bytes 786440 | tf_op jit(solution)/shard_map/ppermute | solution.py:193
  96.7 3.0 %collective-permute-done.22.b3 = bf16[128,1024]{1,0:T(8,128)(2,1)S(1)} collective-permute-done((bf16[128,1024]{1,0:T(8,128)(2,1)S(1)}, bf16[128,1024]{1,0:T(8,128)(2,1)S(1)}, u32[]{:S(2)}, u32[]{:S(2)}) %collective-permute-start.22) | collective-permute-done | bytes 262176 | tf_op jit(solution)/shard_map/ppermute | solution.py:193
  101.9 3.4 %shard_map.80.acc_in = f32[256,1024]{1,0:T(8,128)S(1)} custom-call(bf16[128,1024]{1,0:T(8,128)(2,1)S(1)} %get-tuple-element.38.a0, bf16[128,1024]{1,0:T(8,128)(2,1)S(1)} %collective-permute-done.19.a1, bf16[128,1024]{1,0:T(8,128)(2,1)S(1)} %collective-permute-done.25.a2, bf16[128,1024]{1,0:T(8,128)(2,1)S(1)} %collective-permute-done.28.a3, ...), custom_call_target="tpu_custom_call" | custom-call | flops 2147483648 | bytes 9437184 | tf_op jit(solution)/shard_map/pallas_call | solution.py:564
  107.4 2.2 %collective-permute-done.23.b5 = bf16[128,1024]{1,0:T(8,128)(2,1)S(1)} collective-permute-done((bf16[128,1024]{1,0:T(8,128)(2,1)S(1)}, bf16[128,1024]{1,0:T(8,128)(2,1)S(1)}, u32[]{:S(2)}, u32[]{:S(2)}) %collective-permute-start.23) | collective-permute-done | bytes 262176 | tf_op jit(solution)/shard_map/ppermute | solution.py:193
  114.6 2.5 %shard_map.82 = (bf16[256,1024]{1,0:T(8,128)(2,1)}, f32[128,1024]{1,0:T(8,128)S(1)}) custom-call(bf16[128,1024]{1,0:T(8,128)(2,1)S(1)} %collective-permute-done.27.a6, bf16[128,1024]{1,0:T(8,128)(2,1)S(1)} %collective-permute-done.32.a7, bf16[128,1024]{1,0:T(8,128)(2,1)S(1)} %collective-permute-done.34.b6, f32[256,1024]{1,0:T(8,128)S(1)} %shard_map.81.acc_in, ...), custom_call_target="tpu_custom_call" | custom-call | flops 1073741824 | bytes 5242880 | tf_op jit(solution)/shard_map/pallas_call | solution.py:589
  (79 shorter events, 46.0 us)
Async XLA Ops:
  0.0 52.3 %collective-permute-start.12 = (bf16[1024,4096]{1,0:T(8,128)(2,1)}, bf16[1024,4096]{1,0:T(8,128)(2,1)S(1)}, u32[]{:S(2)}, u32[]{:S(2)}) collective-permute-start(bf16[1024,4096]{1,0:T(8,128)(2,1)} %refs_0_.1), channel_id=1, source_target_pairs={{0,1},{1,0},{2,3},{3,2},{4,5},{5,4},{6,7},{7,6},{8,9},{9,8},{10,11... | collective-permute-start | bytes 25165832 | tf_op jit(solution)/shard_map/ppermute | solution.py:29
  0.5 101.4 %collective-permute-start.31 = (bf16[1024,4096]{1,0:T(8,128)(2,1)}, bf16[1024,4096]{1,0:T(8,128)(2,1)S(1)}, u32[]{:S(2)}, u32[]{:S(2)}) collective-permute-start(bf16[1024,4096]{1,0:T(8,128)(2,1)} %w0.7), channel_id=1, source_target_pairs={{0,1},{1,0},{2,3},{3,2},{4,5},{5,4},{6,7},{7,6},{8,9},{9,8},{10,11... | collective-permute-start | bytes 25165832 | tf_op jit(solution)/shard_map/ppermute | solution.py:29
  9.5 8.9 %collective-permute-start.9 = (bf16[128,1024]{1,0:T(8,128)(2,1)S(1)}, bf16[128,1024]{1,0:T(8,128)(2,1)S(1)}, u32[]{:S(2)}, u32[]{:S(2)}) collective-permute-start(bf16[128,1024]{1,0:T(8,128)(2,1)S(1)} %get-tuple-element.49.b0), channel_id=1, source_target_pairs={{0,4},{1,3},{2,6},{3,1},{4,0},{5,9},{6,2},{7,11},{8,12},{9,5},{10,... | collective-permute-start | bytes 786440 | tf_op jit(solution)/shard_map/ppermute | solution.py:193
  9.6 9.2 %collective-permute-start.6 = (bf16[128,1024]{1,0:T(8,128)(2,1)S(1)}, bf16[128,1024]{1,0:T(8,128)(2,1)S(1)}, u32[]{:S(2)}, u32[]{:S(2)}) collective-permute-start(bf16[128,1024]{1,0:T(8,128)(2,1)S(1)} %get-tuple-element.50.a0), channel_id=1, source_target_pairs={{0,4},{1,3},{2,6},{3,1},{4,0},{5,9},{6,2},{7,11},{8,12},{9,5},{10,... | collective-permute-start | bytes 786440 | tf_op jit(solution)/shard_map/ppermute | solution.py:193
  18.8 9.6 %collective-permute-start.11 = (bf16[128,1024]{1,0:T(8,128)(2,1)S(1)}, bf16[128,1024]{1,0:T(8,128)(2,1)S(1)}, u32[]{:S(2)}, u32[]{:S(2)}) collective-permute-start(bf16[128,1024]{1,0:T(8,128)(2,1)S(1)} %collective-permute-done.9.b1), channel_id=1, source_target_pairs={{0,2},{1,5},{2,0},{3,7},{4,8},{5,1},{6,10},{7,3},{8,4},{9,13},{10,... | collective-permute-start | bytes 786440 | tf_op jit(solution)/shard_map/ppermute | solution.py:193
  25.5 24.1 %collective-permute-start.13 = (bf16[128,4096]{1,0:T(8,128)(2,1)}, bf16[128,4096]{1,0:T(8,128)(2,1)S(1)}, u32[]{:S(2)}, u32[]{:S(2)}) collective-permute-start(bf16[128,4096]{1,0:T(8,128)(2,1)} %refs_1_.1), channel_id=1, source_target_pairs={{0,1},{1,0},{2,3},{3,2},{4,5},{5,4},{6,7},{7,6},{8,9},{9,8},{10,11... | collective-permute-start | bytes 3145736 | tf_op jit(solution)/shard_map/ppermute | solution.py:29
  28.3 21.4 %collective-permute-start.14 = (bf16[128,4096]{1,0:T(8,128)(2,1)}, bf16[128,4096]{1,0:T(8,128)(2,1)S(1)}, u32[]{:S(2)}, u32[]{:S(2)}) collective-permute-start(bf16[128,4096]{1,0:T(8,128)(2,1)} %refs_2_.1), channel_id=1, source_target_pairs={{0,1},{1,0},{2,3},{3,2},{4,5},{5,4},{6,7},{7,6},{8,9},{9,8},{10,11... | collective-permute-start | bytes 3145736 | tf_op jit(solution)/shard_map/ppermute | solution.py:29
  31.1 9.7 %collective-permute-start.16 = (bf16[128,1024]{1,0:T(8,128)(2,1)S(1)}, bf16[128,1024]{1,0:T(8,128)(2,1)S(1)}, u32[]{:S(2)}, u32[]{:S(2)}) collective-permute-start(bf16[128,1024]{1,0:T(8,128)(2,1)S(1)} %collective-permute-done.10.b2), channel_id=1, source_target_pairs={{0,4},{1,3},{2,6},{3,1},{4,0},{5,9},{6,2},{7,11},{8,12},{9,5},{10,... | collective-permute-start | bytes 786440 | tf_op jit(solution)/shard_map/ppermute | solution.py:193
  47.2 11.6 %collective-permute-start.8 = (bf16[128,1024]{1,0:T(8,128)(2,1)S(1)}, bf16[128,1024]{1,0:T(8,128)(2,1)S(1)}, u32[]{:S(2)}, u32[]{:S(2)}) collective-permute-start(bf16[128,1024]{1,0:T(8,128)(2,1)S(1)} %collective-permute-done.7.a3), channel_id=1, source_target_pairs={{0,4},{1,3},{2,6},{3,1},{4,0},{5,9},{6,2},{7,11},{8,12},{9,5},{10,... | collective-permute-start | bytes 786440 | tf_op jit(solution)/shard_map/ppermute | solution.py:193
  49.7 12.5 %collective-permute-start.18 = (bf16[128,1024]{1,0:T(8,128)(2,1)S(1)}, bf16[128,1024]{1,0:T(8,128)(2,1)S(1)}, u32[]{:S(2)}, u32[]{:S(2)}) collective-permute-start(bf16[128,1024]{1,0:T(8,128)(2,1)S(1)} %collective-permute-done.11.b3), channel_id=1, source_target_pairs={{0,4},{1,3},{2,6},{3,1},{4,0},{5,9},{6,2},{7,11},{8,12},{9,5},{10,... | collective-permute-start | bytes 786440 | tf_op jit(solution)/shard_map/ppermute | solution.py:193
  49.8 17.3 %collective-permute-start.17 = (bf16[128,1024]{1,0:T(8,128)(2,1)S(1)}, bf16[128,1024]{1,0:T(8,128)(2,1)S(1)}, u32[]{:S(2)}, u32[]{:S(2)}) collective-permute-start(bf16[128,1024]{1,0:T(8,128)(2,1)S(1)} %collective-permute-done.16.b4), channel_id=1, source_target_pairs={{0,2},{1,5},{2,0},{3,7},{4,8},{5,1},{6,10},{7,3},{8,4},{9,13},{10,... | collective-permute-start | bytes 786440 | tf_op jit(solution)/shard_map/ppermute | solution.py:193
  52.3 14.9 %collective-permute-start.5 = (bf16[128,1024]{1,0:T(8,128)(2,1)S(1)}, bf16[128,1024]{1,0:T(8,128)(2,1)S(1)}, u32[]{:S(2)}, u32[]{:S(2)}) collective-permute-start(bf16[128,1024]{1,0:T(8,128)(2,1)S(1)} %collective-permute-done.4.a4), channel_id=1, source_target_pairs={{0,2},{1,5},{2,0},{3,7},{4,8},{5,1},{6,10},{7,3},{8,4},{9,13},{10,... | collective-permute-start | bytes 786440 | tf_op jit(solution)/shard_map/ppermute | solution.py:193
  62.2 11.1 %collective-permute-start.20 = (bf16[128,1024]{1,0:T(8,128)(2,1)S(1)}, bf16[128,1024]{1,0:T(8,128)(2,1)S(1)}, u32[]{:S(2)}, u32[]{:S(2)}) collective-permute-start(bf16[128,1024]{1,0:T(8,128)(2,1)S(1)} %collective-permute-done.18.b5), channel_id=1, source_target_pairs={{0,2},{1,5},{2,0},{3,7},{4,8},{5,1},{6,10},{7,3},{8,4},{9,13},{10,... | collective-permute-start | bytes 786440 | tf_op jit(solution)/shard_map/ppermute | solution.py:193
  71.0 10.8 %collective-permute-start.25 = (bf16[128,1024]{1,0:T(8,128)(2,1)S(1)}, bf16[128,1024]{1,0:T(8,128)(2,1)S(1)}, u32[]{:S(2)}, u32[]{:S(2)}) collective-permute-start(bf16[128,1024]{1,0:T(8,128)(2,1)S(1)} %get-tuple-element.38.a0), channel_id=1, source_target_pairs={{0,2},{1,5},{2,0},{3,7},{4,8},{5,1},{6,10},{7,3},{8,4},{9,13},{10,... | collective-permute-start | bytes 786440 | tf_op jit(solution)/shard_map/ppermute | solution.py:193
  79.5 9.2 %collective-permute-start.21 = (bf16[128,1024]{1,0:T(8,128)(2,1)S(1)}, bf16[128,1024]{1,0:T(8,128)(2,1)S(1)}, u32[]{:S(2)}, u32[]{:S(2)}) collective-permute-start(bf16[128,1024]{1,0:T(8,128)(2,1)S(1)} %get-tuple-element.43.b0), channel_id=1, source_target_pairs={{0,4},{1,3},{2,6},{3,1},{4,0},{5,9},{6,2},{7,11},{8,12},{9,5},{10,... | collective-permute-start | bytes 786440 | tf_op jit(solution)/shard_map/ppermute | solution.py:193
  79.6 9.4 %collective-permute-start.28 = (bf16[128,1024]{1,0:T(8,128)(2,1)S(1)}, bf16[128,1024]{1,0:T(8,128)(2,1)S(1)}, u32[]{:S(2)}, u32[]{:S(2)}) collective-permute-start(bf16[128,1024]{1,0:T(8,128)(2,1)S(1)} %collective-permute-done.19.a1), channel_id=1, source_target_pairs={{0,2},{1,5},{2,0},{3,7},{4,8},{5,1},{6,10},{7,3},{8,4},{9,13},{10,... | collective-permute-start | bytes 786440 | tf_op jit(solution)/shard_map/ppermute | solution.py:193
  81.9 12.2 %collective-permute-start.30 = (bf16[128,1024]{1,0:T(8,128)(2,1)S(1)}, bf16[128,1024]{1,0:T(8,128)(2,1)S(1)}, u32[]{:S(2)}, u32[]{:S(2)}) collective-permute-start(bf16[128,1024]{1,0:T(8,128)(2,1)S(1)} %get-tuple-element.43.b0), channel_id=1, source_target_pairs={{0,2},{1,5},{2,0},{3,7},{4,8},{5,1},{6,10},{7,3},{8,4},{9,13},{10,... | collective-permute-start | bytes 786440 | tf_op jit(solution)/shard_map/ppermute | solution.py:193
  81.9 14.5 %collective-permute-start.26 = (bf16[128,1024]{1,0:T(8,128)(2,1)S(1)}, bf16[128,1024]{1,0:T(8,128)(2,1)S(1)}, u32[]{:S(2)}, u32[]{:S(2)}) collective-permute-start(bf16[128,1024]{1,0:T(8,128)(2,1)S(1)} %collective-permute-done.25.a2), channel_id=1, source_target_pairs={{0,4},{1,3},{2,6},{3,1},{4,0},{5,9},{6,2},{7,11},{8,12},{9,5},{10,... | collective-permute-start | bytes 786440 | tf_op jit(solution)/shard_map/ppermute | solution.py:193
  88.8 10.9 %collective-permute-start.22 = (bf16[128,1024]{1,0:T(8,128)(2,1)S(1)}, bf16[128,1024]{1,0:T(8,128)(2,1)S(1)}, u32[]{:S(2)}, u32[]{:S(2)}) collective-permute-start(bf16[128,1024]{1,0:T(8,128)(2,1)S(1)} %collective-permute-done.21.b1), channel_id=1, source_target_pairs={{0,2},{1,5},{2,0},{3,7},{4,8},{5,1},{6,10},{7,3},{8,4},{9,13},{10,... | collective-permute-start | bytes 786440 | tf_op jit(solution)/shard_map/ppermute | solution.py:193
  89.0 16.3 %collective-permute-start.29 = (bf16[128,1024]{1,0:T(8,128)(2,1)S(1)}, bf16[128,1024]{1,0:T(8,128)(2,1)S(1)}, u32[]{:S(2)}, u32[]{:S(2)}) collective-permute-start(bf16[128,1024]{1,0:T(8,128)(2,1)S(1)} %collective-permute-done.28.a3), channel_id=1, source_target_pairs={{0,4},{1,3},{2,6},{3,1},{4,0},{5,9},{6,2},{7,11},{8,12},{9,5},{10,... | collective-permute-start | bytes 786440 | tf_op jit(solution)/shard_map/ppermute | solution.py:193
  94.1 11.7 %collective-permute-start.33 = (bf16[128,1024]{1,0:T(8,128)(2,1)S(1)}, bf16[128,1024]{1,0:T(8,128)(2,1)S(1)}, u32[]{:S(2)}, u32[]{:S(2)}) collective-permute-start(bf16[128,1024]{1,0:T(8,128)(2,1)S(1)} %collective-permute-done.30.b2), channel_id=1, source_target_pairs={{0,4},{1,3},{2,6},{3,1},{4,0},{5,9},{6,2},{7,11},{8,12},{9,5},{10,... | collective-permute-start | bytes 786440 | tf_op jit(solution)/shard_map/ppermute | solution.py:193
  96.4 16.7 %collective-permute-start.27 = (bf16[128,1024]{1,0:T(8,128)(2,1)S(1)}, bf16[128,1024]{1,0:T(8,128)(2,1)S(1)}, u32[]{:S(2)}, u32[]{:S(2)}) collective-permute-start(bf16[128,1024]{1,0:T(8,128)(2,1)S(1)} %collective-permute-done.26.a4), channel_id=1, source_target_pairs={{0,2},{1,5},{2,0},{3,7},{4,8},{5,1},{6,10},{7,3},{8,4},{9,13},{10,... | collective-permute-start | bytes 786440 | tf_op jit(solution)/shard_map/ppermute | solution.py:193
  99.7 9.9 %collective-permute-start.23 = (bf16[128,1024]{1,0:T(8,128)(2,1)S(1)}, bf16[128,1024]{1,0:T(8,128)(2,1)S(1)}, u32[]{:S(2)}, u32[]{:S(2)}) collective-permute-start(bf16[128,1024]{1,0:T(8,128)(2,1)S(1)} %collective-permute-done.22.b3), channel_id=1, source_target_pairs={{0,4},{1,3},{2,6},{3,1},{4,0},{5,9},{6,2},{7,11},{8,12},{9,5},{10,... | collective-permute-start | bytes 786440 | tf_op jit(solution)/shard_map/ppermute | solution.py:193
  105.8 8.7 %collective-permute-start.34 = (bf16[128,1024]{1,0:T(8,128)(2,1)S(1)}, bf16[128,1024]{1,0:T(8,128)(2,1)S(1)}, u32[]{:S(2)}, u32[]{:S(2)}) collective-permute-start(bf16[128,1024]{1,0:T(8,128)(2,1)S(1)} %collective-permute-done.33.b4), channel_id=1, source_target_pairs={{0,2},{1,5},{2,0},{3,7},{4,8},{5,1},{6,10},{7,3},{8,4},{9,13},{10,... | collective-permute-start | bytes 786440 | tf_op jit(solution)/shard_map/ppermute | solution.py:193
  (17 other events, 166.2 us)

commit v6 on v5

--- a/solution.py
+++ b/solution.py
@@ -433,6 +433,17 @@
     return pltpu.with_memory_space_constraint(value, pltpu.HBM)
 
 
+def split_kernel(hidden, first, second, sems):
+    copies = [
+        pltpu.make_async_copy(hidden.at[pl.ds(s * ROWS, ROWS), :], target, sems.at[s])
+        for s, target in enumerate((first, second))
+    ]
+    for copy in copies:
+        copy.start()
+    for copy in copies:
+        copy.wait()
+
+
 def angle_kernel(lens, freq, angle):
     place = lax.broadcasted_iota(jnp.int32, angle.shape, 0)
     position = place
@@ -453,7 +464,15 @@
 
 def ring_layer(hidden_in, norm_gain, query_weight, key_weight, value_weight, output_weight, lengths):
     f32, bf16 = jnp.float32, jnp.bfloat16
-    a0, b0 = hidden_in[:ROWS], hidden_in[ROWS:]
+    rows_shape = jax.ShapeDtypeStruct((ROWS, UNIT), bf16)
+    a0, b0 = kernel_call(
+        split_kernel,
+        out_shape=(rows_shape, rows_shape),
+        in_specs=[HBM],
+        out_specs=(VM, VM),
+        scratch_shapes=[pltpu.SemaphoreType.DMA((2,))],
+        compiler_params=params(2),
+    )(in_hbm(hidden_in))
     a1, b1 = swapped(a0, 0), swapped(b0, 0)
     a2, b2 = swapped(a0, 1), swapped(b0, 1)
     projections = (query_weight, key_weight, value_weight)
@@ -552,7 +571,6 @@
         compiler_params=params(10),
         cost_estimate=cost(ROWS, 1, qkv),
     )(b7, gain, factor, second, *weights)
-    a1, projected = after(a1, projected)
     a3 = swapped(a1, 1)
     b0, _, _ = attend_stream(1, projected, (key_a, value_a))
     b1, b2 = swapped(b0, 0), swapped(b0, 1)

time: 119 us -> 120 us (level)
  waiting for transfers between devices: 39.3 us -> 44 us
  starting transfers between devices: 49.9 us -> 45.8 us
    ppermute x28, waiting for transfers between devices: 35.6 us -> 40.3 us  [swapped(): return lax.ppermute(shard, ('tp', 'pair'), ring_swap(later))]
    ppermute x28, starting transfers between devices: 41.7 us -> 37.5 us  [swapped(): return lax.ppermute(shard, ('tp', 'pair'), ring_swap(later))]
  transfers between devices with their start and end apart: 35 -> 35, of which waited for: 17 -> 17; matrix products, arithmetic and copies ran while one was open for 2% -> 2% of each run, Pallas kernels for 20% -> 21%
where the time goes in v6:
time: 120 us
  starting transfers between devices  45.8 us (38%)
  waiting for transfers between devices  44 us (37%)
  Pallas kernels  26.3 us (22%)
  other arithmetic  1.73 us (1%)
  local copies, waits for them, and re-layouts  1.53 us (1%)
    ppermute x28, waiting for transfers between devices, swapped(): return lax.ppermute(shard, ('tp', 'pair'), ring_swap(later))  40.3 us
    ppermute x28, starting transfers between devices, swapped(): return lax.ppermute(shard, ('tp', 'pair'), ring_swap(later))  37.5 us
    ppermute x3, starting transfers between devices, summed_over_tp(): value = value + lax.ppermute(value, ('tp', 'pair'), pairs)  7.72 us
    pallas_call x1, Pallas kernels, ring_layer(): kernel_call(early_kernel, out_shape=(acc_shape, half_query, half_query, b...  5.71 us
    ppermute x3, waiting for transfers between devices, summed_over_tp(): value = value + lax.ppermute(value, ('tp', 'pair'), pairs)  3.68 us
    pallas_call x2, Pallas kernels, attend_stream(): kernel_call(lambda *refs: attend_kernel(half, *refs), out_shape=(jax.Shap...  3.57 us
    pallas_call x1, Pallas kernels, ring_layer(): kernel_call(out_early_kernel, out_shape=acc_shape, in_specs=[VM] * 10, ou...  3.37 us
    pallas_call x1, Pallas kernels, ring_layer(): kernel_call(out_first_kernel, grid=(1,), out_shape=(out_shape, half_shape...  2.48 us
  transfers between devices with their start and end apart: 35, of which 17 were waited for; matrix products, arithmetic and copies ran while one was open for 2% of the time, Pallas kernels for 21%

profile of v6, /device:TPU:0, one launch (start us, length us, event | category | flops | bytes accessed | tf_op | source)
XLA Modules:
  0.0 119.5 jit_solution(1627491738741706865)
XLA Ops:
  1.7 3.0 %collective-permute-start = (f32[2,128]{1,0:T(2,128)S(1)}, f32[2,128]{1,0:T(2,128)S(1)}, u32[]{:S(2)}, u32[]{:S(2)}) collective-permute-start(f32[2,128]{1,0:T(2,128)S(1)} %bitcast.13), channel_id=1, source_target_pairs={{0,2},{1,5},{2,0},{3,7},{4,6},{5,1},{6,4},{7,3},{8,10},{9,13},{10,... | collective-permute-start | bytes 3080 | tf_op jit(solution)/shard_map/ppermute | solution.py:420
  11.6 2.6 %collective-permute-start.2 = (f32[2,128]{1,0:T(2,128)S(1)}, f32[2,128]{1,0:T(2,128)S(1)}, u32[]{:S(2)}, u32[]{:S(2)}) collective-permute-start(f32[2,128]{1,0:T(2,128)S(1)} %fusion.3), channel_id=1, source_target_pairs={{0,8},{1,9},{2,10},{3,11},{4,12},{5,13},{6,14},{7,15},{8,0},{9,1},... | collective-permute-start | bytes 3080 | tf_op jit(solution)/shard_map/ppermute | solution.py:420
  14.2 2.1 %collective-permute-done.2 = f32[2,128]{1,0:T(2,128)S(1)} collective-permute-done((f32[2,128]{1,0:T(2,128)S(1)}, f32[2,128]{1,0:T(2,128)S(1)}, u32[]{:S(2)}, u32[]{:S(2)}) %collective-permute-start.2) | collective-permute-done | bytes 1056 | tf_op jit(solution)/shard_map/ppermute | solution.py:420
  20.4 2.3 %collective-permute-done.13.b2 = bf16[128,1024]{1,0:T(8,128)(2,1)S(1)} collective-permute-done((bf16[128,1024]{1,0:T(8,128)(2,1)S(1)}, bf16[128,1024]{1,0:T(8,128)(2,1)S(1)}, u32[]{:S(2)}, u32[]{:S(2)}) %collective-permute-start.13) | collective-permute-done | bytes 262176 | tf_op jit(solution)/shard_map/ppermute | solution.py:193
  25.5 2.8 %collective-permute-done.11.a3 = bf16[128,1024]{1,0:T(8,128)(2,1)S(1)} collective-permute-done((bf16[128,1024]{1,0:T(8,128)(2,1)S(1)}, bf16[128,1024]{1,0:T(8,128)(2,1)S(1)}, u32[]{:S(2)}, u32[]{:S(2)}) %collective-permute-start.11) | collective-permute-done | bytes 262176 | tf_op jit(solution)/shard_map/ppermute | solution.py:193
  28.3 2.8 %collective-permute-done.4.b3 = bf16[128,1024]{1,0:T(8,128)(2,1)S(1)} collective-permute-done((bf16[128,1024]{1,0:T(8,128)(2,1)S(1)}, bf16[128,1024]{1,0:T(8,128)(2,1)S(1)}, u32[]{:S(2)}, u32[]{:S(2)}) %collective-permute-start.4) | collective-permute-done | bytes 262176 | tf_op jit(solution)/shard_map/ppermute | solution.py:193
  31.1 5.3 %collective-permute-start.18 = (bf16[128,1024]{1,0:T(8,128)(2,1)S(1)}, bf16[128,1024]{1,0:T(8,128)(2,1)S(1)}, u32[]{:S(2)}, u32[]{:S(2)}) collective-permute-start(bf16[128,1024]{1,0:T(8,128)(2,1)S(1)} %collective-permute-done.13.b2), channel_id=1, source_target_pairs={{0,4},{1,3},{2,6},{3,1},{4,0},{5,9},{6,2},{7,11},{8,12},{9,5},{10,... | collective-permute-start | bytes 786440 | tf_op jit(solution)/shard_map/ppermute | solution.py:193
  36.5 4.3 %collective-permute-done.18.b4 = bf16[128,1024]{1,0:T(8,128)(2,1)S(1)} collective-permute-done((bf16[128,1024]{1,0:T(8,128)(2,1)S(1)}, bf16[128,1024]{1,0:T(8,128)(2,1)S(1)}, u32[]{:S(2)}, u32[]{:S(2)}) %collective-permute-start.18) | collective-permute-done | bytes 262176 | tf_op jit(solution)/shard_map/ppermute | solution.py:193
  44.6 2.7 %collective-permute-done.8.a4 = bf16[128,1024]{1,0:T(8,128)(2,1)S(1)} collective-permute-done((bf16[128,1024]{1,0:T(8,128)(2,1)S(1)}, bf16[128,1024]{1,0:T(8,128)(2,1)S(1)}, u32[]{:S(2)}, u32[]{:S(2)}) %collective-permute-start.8) | collective-permute-done | bytes 262176 | tf_op jit(solution)/shard_map/ppermute | solution.py:193
  47.2 2.3 %collective-permute-start.12 = (bf16[128,1024]{1,0:T(8,128)(2,1)S(1)}, bf16[128,1024]{1,0:T(8,128)(2,1)S(1)}, u32[]{:S(2)}, u32[]{:S(2)}) collective-permute-start(bf16[128,1024]{1,0:T(8,128)(2,1)S(1)} %collective-permute-done.11.a3), channel_id=1, source_target_pairs={{0,4},{1,3},{2,6},{3,1},{4,0},{5,9},{6,2},{7,11},{8,12},{9,5},{10,... | collective-permute-start | bytes 786440 | tf_op jit(solution)/shard_map/ppermute | solution.py:193
  49.7 2.5 %collective-permute-start.19 = (bf16[128,1024]{1,0:T(8,128)(2,1)S(1)}, bf16[128,1024]{1,0:T(8,128)(2,1)S(1)}, u32[]{:S(2)}, u32[]{:S(2)}) collective-permute-start(bf16[128,1024]{1,0:T(8,128)(2,1)S(1)} %collective-permute-done.18.b4), channel_id=1, source_target_pairs={{0,2},{1,5},{2,0},{3,7},{4,8},{5,1},{6,10},{7,3},{8,4},{9,13},{10,... | collective-permute-start | bytes 786440 | tf_op jit(solution)/shard_map/ppermute | solution.py:193
  53.1 5.7 %shard_map.75 = (f32[256,1280]{1,0:T(8,128)S(1)}, bf16[512,4096]{1,0:T(8,128)(2,1)S(1)}, bf16[512,4096]{1,0:T(8,128)(2,1)S(1)}, bf16[256,4096]{1,0:T(8,128)(2,1)S(1)}) custom-call(bf16[128,1024]{1,0:T(8,128)(2,1)S(1)} %get-tuple-element.30.a0, bf16[128,1024]{1,0:T(8,128)(2,1)S(1)} %collective-permute-done.10.a1, ...), custom_call_target="tpu_custom_call" | custom-call | flops 2684354560 | bytes 11796480 | tf_op jit(solution)/shard_map/pallas_call | solution.py:509
  62.2 2.4 %collective-permute-start.6 = (bf16[128,1024]{1,0:T(8,128)(2,1)S(1)}, bf16[128,1024]{1,0:T(8,128)(2,1)S(1)}, u32[]{:S(2)}, u32[]{:S(2)}) collective-permute-start(bf16[128,1024]{1,0:T(8,128)(2,1)S(1)} %collective-permute-done.5.b5), channel_id=1, source_target_pairs={{0,2},{1,5},{2,0},{3,7},{4,8},{5,1},{6,10},{7,3},{8,4},{9,13},{10,... | collective-permute-start | bytes 786440 | tf_op jit(solution)/shard_map/ppermute | solution.py:193
  64.6 2.5 %shard_map.76.acc_in = f32[256,1280]{1,0:T(8,128)S(1)} custom-call(bf16[128,1024]{1,0:T(8,128)(2,1)S(1)} %collective-permute-done.8.a4, bf16[128,1024]{1,0:T(8,128)(2,1)S(1)} %collective-permute-done.12.a5, bf16[128,1024]{1,0:T(8,128)(2,1)S(1)} %collective-permute-done.18.b4, bf16[128,1024]{1,0:T(8,128)(2,1)S(1)} %collective-permute-done.5.b5, ...), custom_call_target="tpu_custom_call" | custom-call | flops 1342177280 | bytes 6553600 | tf_op jit(solution)/shard_map/pallas_call | solution.py:528
  67.1 2.4 %shard_map.77 = (f32[128,1280]{1,0:T(8,128)S(1)}, f32[128,1280]{1,0:T(8,128)S(1)}) custom-call(bf16[128,1024]{1,0:T(8,128)(2,1)S(1)} %collective-permute-done.9.a6, bf16[128,1024]{1,0:T(8,128)(2,1)S(1)} %collective-permute-done.17.a7, bf16[128,1024]{1,0:T(8,128)(2,1)S(1)} %collective-permute-done.19.b6, f32[64,128]{1,0:T(8,128)S(1)} %bitcast.11, ...), custom_call_target="tpu_custom_call" | custom-call | flops 1342177280 | bytes 6553600 | tf_op jit(solution)/shard_map/pallas_call | solution.py:538
  72.3 2.1 %shard_map.80 = (bf16[128,1024]{1,0:T(8,128)(2,1)S(1)}, bf16[128,128]{1,0:T(8,128)(2,1)}, bf16[128,128]{1,0:T(8,128)(2,1)}) custom-call(s32[1,4]{1,0:T(1,128)S(1)} %copy-done.3, f32[128,1280]{1,0:T(8,128)S(1)} %shard_map.78.refs_1_, f32[256,128]{1,0:T(8,128)S(1)} %get-tuple-element.38.refs_2_, f32[256,128]{1,0:T(8,128)S(1)} %get-tuple-element.39.refs_3_, ...), custom_call_target="tpu_custom_call" | custom-call | flops 671088640 | bytes 5898240 | tf_op jit(solution)/shard_map/pallas_call | solution.py:554
  80.6 5.2 %collective-permute-done.20.b1 = bf16[128,1024]{1,0:T(8,128)(2,1)S(1)} collective-permute-done((bf16[128,1024]{1,0:T(8,128)(2,1)S(1)}, bf16[128,1024]{1,0:T(8,128)(2,1)S(1)}, u32[]{:S(2)}, u32[]{:S(2)}) %collective-permute-start.20) | collective-permute-done | bytes 262176 | tf_op jit(solution)/shard_map/ppermute | solution.py:193
  87.5 3.4 %collective-permute-done.24.a2 = bf16[128,1024]{1,0:T(8,128)(2,1)S(1)} collective-permute-done((bf16[128,1024]{1,0:T(8,128)(2,1)S(1)}, bf16[128,1024]{1,0:T(8,128)(2,1)S(1)}, u32[]{:S(2)}, u32[]{:S(2)}) %collective-permute-start.24) | collective-permute-done | bytes 262176 | tf_op jit(solution)/shard_map/ppermute | solution.py:193
  90.8 5.6 %collective-permute-done.28.a3 = bf16[128,1024]{1,0:T(8,128)(2,1)S(1)} collective-permute-done((bf16[128,1024]{1,0:T(8,128)(2,1)S(1)}, bf16[128,1024]{1,0:T(8,128)(2,1)S(1)}, u32[]{:S(2)}, u32[]{:S(2)}) %collective-permute-start.28) | collective-permute-done | bytes 262176 | tf_op jit(solution)/shard_map/ppermute | solution.py:193
  96.5 5.6 %collective-permute-done.21.b3 = bf16[128,1024]{1,0:T(8,128)(2,1)S(1)} collective-permute-done((bf16[128,1024]{1,0:T(8,128)(2,1)S(1)}, bf16[128,1024]{1,0:T(8,128)(2,1)S(1)}, u32[]{:S(2)}, u32[]{:S(2)}) %collective-permute-start.21) | collective-permute-done | bytes 262176 | tf_op jit(solution)/shard_map/ppermute | solution.py:193
  102.1 2.3 %collective-permute-start.34 = (bf16[128,1024]{1,0:T(8,128)(2,1)S(1)}, bf16[128,1024]{1,0:T(8,128)(2,1)S(1)}, u32[]{:S(2)}, u32[]{:S(2)}) collective-permute-start(bf16[128,1024]{1,0:T(8,128)(2,1)S(1)} %collective-permute-done.33.b4), channel_id=1, source_target_pairs={{0,2},{1,5},{2,0},{3,7},{4,8},{5,1},{6,10},{7,3},{8,4},{9,13},{10,... | collective-permute-start | bytes 786440 | tf_op jit(solution)/shard_map/ppermute | solution.py:193
  104.5 3.4 %shard_map.81.acc_in = f32[256,1024]{1,0:T(8,128)S(1)} custom-call(bf16[128,1024]{1,0:T(8,128)(2,1)S(1)} %get-tuple-element.44.a0, bf16[128,1024]{1,0:T(8,128)(2,1)S(1)} %collective-permute-done.27.a1, bf16[128,1024]{1,0:T(8,128)(2,1)S(1)} %collective-permute-done.24.a2, bf16[128,1024]{1,0:T(8,128)(2,1)S(1)} %collective-permute-done.28.a3, ...), custom_call_target="tpu_custom_call" | custom-call | flops 2147483648 | bytes 9437184 | tf_op jit(solution)/shard_map/pallas_call | solution.py:582
  111.3 2.3 %collective-permute-start.23 = (bf16[128,1024]{1,0:T(8,128)(2,1)S(1)}, bf16[128,1024]{1,0:T(8,128)(2,1)S(1)}, u32[]{:S(2)}, u32[]{:S(2)}) collective-permute-start(bf16[128,1024]{1,0:T(8,128)(2,1)S(1)} %collective-permute-done.22.b5), channel_id=1, source_target_pairs={{0,2},{1,5},{2,0},{3,7},{4,8},{5,1},{6,10},{7,3},{8,4},{9,13},{10,... | collective-permute-start | bytes 786440 | tf_op jit(solution)/shard_map/ppermute | solution.py:193
  115.3 2.5 %shard_map.83 = (bf16[256,1024]{1,0:T(8,128)(2,1)}, f32[128,1024]{1,0:T(8,128)S(1)}) custom-call(bf16[128,1024]{1,0:T(8,128)(2,1)S(1)} %collective-permute-done.26.a6, bf16[128,1024]{1,0:T(8,128)(2,1)S(1)} %collective-permute-done.32.a7, bf16[128,1024]{1,0:T(8,128)(2,1)S(1)} %collective-permute-done.34.b6, f32[256,1024]{1,0:T(8,128)S(1)} %shard_map.82.acc_in, ...), custom_call_target="tpu_custom_call" | custom-call | flops 1073741824 | bytes 5242880 | tf_op jit(solution)/shard_map/pallas_call | solution.py:607
  (79 shorter events, 41.1 us)
Async XLA Ops:
  0.0 52.2 %collective-permute-start.14 = (bf16[1024,4096]{1,0:T(8,128)(2,1)}, bf16[1024,4096]{1,0:T(8,128)(2,1)S(1)}, u32[]{:S(2)}, u32[]{:S(2)}) collective-permute-start(bf16[1024,4096]{1,0:T(8,128)(2,1)} %refs_0_.1), channel_id=1, source_target_pairs={{0,1},{1,0},{2,3},{3,2},{4,5},{5,4},{6,7},{7,6},{8,9},{9,8},{10,11... | collective-permute-start | bytes 25165832 | tf_op jit(solution)/shard_map/ppermute | solution.py:29
  0.5 104.0 %collective-permute-start.31 = (bf16[1024,4096]{1,0:T(8,128)(2,1)}, bf16[1024,4096]{1,0:T(8,128)(2,1)S(1)}, u32[]{:S(2)}, u32[]{:S(2)}) collective-permute-start(bf16[1024,4096]{1,0:T(8,128)(2,1)} %w0.7), channel_id=1, source_target_pairs={{0,1},{1,0},{2,3},{3,2},{4,5},{5,4},{6,7},{7,6},{8,9},{9,8},{10,11... | collective-permute-start | bytes 25165832 | tf_op jit(solution)/shard_map/ppermute | solution.py:29
  9.5 8.9 %collective-permute-start.10 = (bf16[128,1024]{1,0:T(8,128)(2,1)S(1)}, bf16[128,1024]{1,0:T(8,128)(2,1)S(1)}, u32[]{:S(2)}, u32[]{:S(2)}) collective-permute-start(bf16[128,1024]{1,0:T(8,128)(2,1)S(1)} %get-tuple-element.30.a0), channel_id=1, source_target_pairs={{0,4},{1,3},{2,6},{3,1},{4,0},{5,9},{6,2},{7,11},{8,12},{9,5},{10,... | collective-permute-start | bytes 786440 | tf_op jit(solution)/shard_map/ppermute | solution.py:193
  9.6 9.2 %collective-permute-start.3 = (bf16[128,1024]{1,0:T(8,128)(2,1)S(1)}, bf16[128,1024]{1,0:T(8,128)(2,1)S(1)}, u32[]{:S(2)}, u32[]{:S(2)}) collective-permute-start(bf16[128,1024]{1,0:T(8,128)(2,1)S(1)} %get-tuple-element.28.b0), channel_id=1, source_target_pairs={{0,4},{1,3},{2,6},{3,1},{4,0},{5,9},{6,2},{7,11},{8,12},{9,5},{10,... | collective-permute-start | bytes 786440 | tf_op jit(solution)/shard_map/ppermute | solution.py:193
  18.7 9.6 %collective-permute-start.11 = (bf16[128,1024]{1,0:T(8,128)(2,1)S(1)}, bf16[128,1024]{1,0:T(8,128)(2,1)S(1)}, u32[]{:S(2)}, u32[]{:S(2)}) collective-permute-start(bf16[128,1024]{1,0:T(8,128)(2,1)S(1)} %collective-permute-done.10.a1), channel_id=1, source_target_pairs={{0,2},{1,5},{2,0},{3,7},{4,8},{5,1},{6,10},{7,3},{8,4},{9,13},{10,... | collective-permute-start | bytes 786440 | tf_op jit(solution)/shard_map/ppermute | solution.py:193
  25.5 24.1 %collective-permute-start.15 = (bf16[128,4096]{1,0:T(8,128)(2,1)}, bf16[128,4096]{1,0:T(8,128)(2,1)S(1)}, u32[]{:S(2)}, u32[]{:S(2)}) collective-permute-start(bf16[128,4096]{1,0:T(8,128)(2,1)} %refs_1_.1), channel_id=1, source_target_pairs={{0,1},{1,0},{2,3},{3,2},{4,5},{5,4},{6,7},{7,6},{8,9},{9,8},{10,11... | collective-permute-start | bytes 3145736 | tf_op jit(solution)/shard_map/ppermute | solution.py:29
  28.3 21.4 %collective-permute-start.16 = (bf16[128,4096]{1,0:T(8,128)(2,1)}, bf16[128,4096]{1,0:T(8,128)(2,1)S(1)}, u32[]{:S(2)}, u32[]{:S(2)}) collective-permute-start(bf16[128,4096]{1,0:T(8,128)(2,1)} %refs_2_.1), channel_id=1, source_target_pairs={{0,1},{1,0},{2,3},{3,2},{4,5},{5,4},{6,7},{7,6},{8,9},{9,8},{10,11... | collective-permute-start | bytes 3145736 | tf_op jit(solution)/shard_map/ppermute | solution.py:29
  31.1 9.7 %collective-permute-start.18 = (bf16[128,1024]{1,0:T(8,128)(2,1)S(1)}, bf16[128,1024]{1,0:T(8,128)(2,1)S(1)}, u32[]{:S(2)}, u32[]{:S(2)}) collective-permute-start(bf16[128,1024]{1,0:T(8,128)(2,1)S(1)} %collective-permute-done.13.b2), channel_id=1, source_target_pairs={{0,4},{1,3},{2,6},{3,1},{4,0},{5,9},{6,2},{7,11},{8,12},{9,5},{10,... | collective-permute-start | bytes 786440 | tf_op jit(solution)/shard_map/ppermute | solution.py:193
  47.2 11.6 %collective-permute-start.12 = (bf16[128,1024]{1,0:T(8,128)(2,1)S(1)}, bf16[128,1024]{1,0:T(8,128)(2,1)S(1)}, u32[]{:S(2)}, u32[]{:S(2)}) collective-permute-start(bf16[128,1024]{1,0:T(8,128)(2,1)S(1)} %collective-permute-done.11.a3), channel_id=1, source_target_pairs={{0,4},{1,3},{2,6},{3,1},{4,0},{5,9},{6,2},{7,11},{8,12},{9,5},{10,... | collective-permute-start | bytes 786440 | tf_op jit(solution)/shard_map/ppermute | solution.py:193
  49.7 12.5 %collective-permute-start.5 = (bf16[128,1024]{1,0:T(8,128)(2,1)S(1)}, bf16[128,1024]{1,0:T(8,128)(2,1)S(1)}, u32[]{:S(2)}, u32[]{:S(2)}) collective-permute-start(bf16[128,1024]{1,0:T(8,128)(2,1)S(1)} %collective-permute-done.4.b3), channel_id=1, source_target_pairs={{0,4},{1,3},{2,6},{3,1},{4,0},{5,9},{6,2},{7,11},{8,12},{9,5},{10,... | collective-permute-start | bytes 786440 | tf_op jit(solution)/shard_map/ppermute | solution.py:193
  49.7 17.3 %collective-permute-start.19 = (bf16[128,1024]{1,0:T(8,128)(2,1)S(1)}, bf16[128,1024]{1,0:T(8,128)(2,1)S(1)}, u32[]{:S(2)}, u32[]{:S(2)}) collective-permute-start(bf16[128,1024]{1,0:T(8,128)(2,1)S(1)} %collective-permute-done.18.b4), channel_id=1, source_target_pairs={{0,2},{1,5},{2,0},{3,7},{4,8},{5,1},{6,10},{7,3},{8,4},{9,13},{10,... | collective-permute-start | bytes 786440 | tf_op jit(solution)/shard_map/ppermute | solution.py:193
  52.2 14.8 %collective-permute-start.9 = (bf16[128,1024]{1,0:T(8,128)(2,1)S(1)}, bf16[128,1024]{1,0:T(8,128)(2,1)S(1)}, u32[]{:S(2)}, u32[]{:S(2)}) collective-permute-start(bf16[128,1024]{1,0:T(8,128)(2,1)S(1)} %collective-permute-done.8.a4), channel_id=1, source_target_pairs={{0,2},{1,5},{2,0},{3,7},{4,8},{5,1},{6,10},{7,3},{8,4},{9,13},{10,... | collective-permute-start | bytes 786440 | tf_op jit(solution)/shard_map/ppermute | solution.py:193
  70.9 9.2 %collective-permute-start.27 = (bf16[128,1024]{1,0:T(8,128)(2,1)S(1)}, bf16[128,1024]{1,0:T(8,128)(2,1)S(1)}, u32[]{:S(2)}, u32[]{:S(2)}) collective-permute-start(bf16[128,1024]{1,0:T(8,128)(2,1)S(1)} %get-tuple-element.44.a0), channel_id=1, source_target_pairs={{0,4},{1,3},{2,6},{3,1},{4,0},{5,9},{6,2},{7,11},{8,12},{9,5},{10,... | collective-permute-start | bytes 786440 | tf_op jit(solution)/shard_map/ppermute | solution.py:193
  74.5 11.3 %collective-permute-start.20 = (bf16[128,1024]{1,0:T(8,128)(2,1)S(1)}, bf16[128,1024]{1,0:T(8,128)(2,1)S(1)}, u32[]{:S(2)}, u32[]{:S(2)}) collective-permute-start(bf16[128,1024]{1,0:T(8,128)(2,1)S(1)} %get-tuple-element.43.b0), channel_id=1, source_target_pairs={{0,4},{1,3},{2,6},{3,1},{4,0},{5,9},{6,2},{7,11},{8,12},{9,5},{10,... | collective-permute-start | bytes 786440 | tf_op jit(solution)/shard_map/ppermute | solution.py:193
  76.5 9.5 %collective-permute-start.30 = (bf16[128,1024]{1,0:T(8,128)(2,1)S(1)}, bf16[128,1024]{1,0:T(8,128)(2,1)S(1)}, u32[]{:S(2)}, u32[]{:S(2)}) collective-permute-start(bf16[128,1024]{1,0:T(8,128)(2,1)S(1)} %get-tuple-element.43.b0), channel_id=1, source_target_pairs={{0,2},{1,5},{2,0},{3,7},{4,8},{5,1},{6,10},{7,3},{8,4},{9,13},{10,... | collective-permute-start | bytes 786440 | tf_op jit(solution)/shard_map/ppermute | solution.py:193
  78.6 12.3 %collective-permute-start.24 = (bf16[128,1024]{1,0:T(8,128)(2,1)S(1)}, bf16[128,1024]{1,0:T(8,128)(2,1)S(1)}, u32[]{:S(2)}, u32[]{:S(2)}) collective-permute-start(bf16[128,1024]{1,0:T(8,128)(2,1)S(1)} %get-tuple-element.44.a0), channel_id=1, source_target_pairs={{0,2},{1,5},{2,0},{3,7},{4,8},{5,1},{6,10},{7,3},{8,4},{9,13},{10,... | collective-permute-start | bytes 786440 | tf_op jit(solution)/shard_map/ppermute | solution.py:193
  80.2 16.3 %collective-permute-start.28 = (bf16[128,1024]{1,0:T(8,128)(2,1)S(1)}, bf16[128,1024]{1,0:T(8,128)(2,1)S(1)}, u32[]{:S(2)}, u32[]{:S(2)}) collective-permute-start(bf16[128,1024]{1,0:T(8,128)(2,1)S(1)} %collective-permute-done.27.a1), channel_id=1, source_target_pairs={{0,2},{1,5},{2,0},{3,7},{4,8},{5,1},{6,10},{7,3},{8,4},{9,13},{10,... | collective-permute-start | bytes 786440 | tf_op jit(solution)/shard_map/ppermute | solution.py:193
  85.8 16.3 %collective-permute-start.21 = (bf16[128,1024]{1,0:T(8,128)(2,1)S(1)}, bf16[128,1024]{1,0:T(8,128)(2,1)S(1)}, u32[]{:S(2)}, u32[]{:S(2)}) collective-permute-start(bf16[128,1024]{1,0:T(8,128)(2,1)S(1)} %collective-permute-done.20.b1), channel_id=1, source_target_pairs={{0,2},{1,5},{2,0},{3,7},{4,8},{5,1},{6,10},{7,3},{8,4},{9,13},{10,... | collective-permute-start | bytes 786440 | tf_op jit(solution)/shard_map/ppermute | solution.py:193
  86.1 16.0 %collective-permute-start.33 = (bf16[128,1024]{1,0:T(8,128)(2,1)S(1)}, bf16[128,1024]{1,0:T(8,128)(2,1)S(1)}, u32[]{:S(2)}, u32[]{:S(2)}) collective-permute-start(bf16[128,1024]{1,0:T(8,128)(2,1)S(1)} %collective-permute-done.30.b2), channel_id=1, source_target_pairs={{0,4},{1,3},{2,6},{3,1},{4,0},{5,9},{6,2},{7,11},{8,12},{9,5},{10,... | collective-permute-start | bytes 786440 | tf_op jit(solution)/shard_map/ppermute | solution.py:193
  90.8 13.6 %collective-permute-start.25 = (bf16[128,1024]{1,0:T(8,128)(2,1)S(1)}, bf16[128,1024]{1,0:T(8,128)(2,1)S(1)}, u32[]{:S(2)}, u32[]{:S(2)}) collective-permute-start(bf16[128,1024]{1,0:T(8,128)(2,1)S(1)} %collective-permute-done.24.a2), channel_id=1, source_target_pairs={{0,4},{1,3},{2,6},{3,1},{4,0},{5,9},{6,2},{7,11},{8,12},{9,5},{10,... | collective-permute-start | bytes 786440 | tf_op jit(solution)/shard_map/ppermute | solution.py:193
  96.5 11.4 %collective-permute-start.29 = (bf16[128,1024]{1,0:T(8,128)(2,1)S(1)}, bf16[128,1024]{1,0:T(8,128)(2,1)S(1)}, u32[]{:S(2)}, u32[]{:S(2)}) collective-permute-start(bf16[128,1024]{1,0:T(8,128)(2,1)S(1)} %collective-permute-done.28.a3), channel_id=1, source_target_pairs={{0,4},{1,3},{2,6},{3,1},{4,0},{5,9},{6,2},{7,11},{8,12},{9,5},{10,... | collective-permute-start | bytes 786440 | tf_op jit(solution)/shard_map/ppermute | solution.py:193
  102.1 9.2 %collective-permute-start.22 = (bf16[128,1024]{1,0:T(8,128)(2,1)S(1)}, bf16[128,1024]{1,0:T(8,128)(2,1)S(1)}, u32[]{:S(2)}, u32[]{:S(2)}) collective-permute-start(bf16[128,1024]{1,0:T(8,128)(2,1)S(1)} %collective-permute-done.21.b3), channel_id=1, source_target_pairs={{0,4},{1,3},{2,6},{3,1},{4,0},{5,9},{6,2},{7,11},{8,12},{9,5},{10,... | collective-permute-start | bytes 786440 | tf_op jit(solution)/shard_map/ppermute | solution.py:193
  102.1 13.2 %collective-permute-start.34 = (bf16[128,1024]{1,0:T(8,128)(2,1)S(1)}, bf16[128,1024]{1,0:T(8,128)(2,1)S(1)}, u32[]{:S(2)}, u32[]{:S(2)}) collective-permute-start(bf16[128,1024]{1,0:T(8,128)(2,1)S(1)} %collective-permute-done.33.b4), channel_id=1, source_target_pairs={{0,2},{1,5},{2,0},{3,7},{4,8},{5,1},{6,10},{7,3},{8,4},{9,13},{10,... | collective-permute-start | bytes 786440 | tf_op jit(solution)/shard_map/ppermute | solution.py:193
  104.4 10.9 %collective-permute-start.26 = (bf16[128,1024]{1,0:T(8,128)(2,1)S(1)}, bf16[128,1024]{1,0:T(8,128)(2,1)S(1)}, u32[]{:S(2)}, u32[]{:S(2)}) collective-permute-start(bf16[128,1024]{1,0:T(8,128)(2,1)S(1)} %collective-permute-done.25.a4), channel_id=1, source_target_pairs={{0,2},{1,5},{2,0},{3,7},{4,8},{5,1},{6,10},{7,3},{8,4},{9,13},{10,... | collective-permute-start | bytes 786440 | tf_op jit(solution)/shard_map/ppermute | solution.py:193
  (17 other events, 184.1 us)

commit v7 on v6

--- a/solution.py
+++ b/solution.py
@@ -311,27 +311,18 @@
     each_own_unit(4, 4, wait)
 
 
-def middle_kernel(a4, a5, b4, b5, gain, factor, acc_in, *refs):
-    *weights, acc, xs = refs
-    normed_units(xs, gain, factor, 4, (a4, a5), (b4, b5))
+def middle_kernel(a4, a5, a6, b4, b5, b6, gain, factor, acc_in, *refs):
+    *weights, first, second, acc, xs = refs
+    normed_units(xs, gain, factor, 4, (a4, a5, a6), (b4, b5, b6))
     acc[...] = acc_in[...]
-    add_units(xs, acc, weights[:3], weights[3:], 4, 2)
-
-
-def project_first_kernel(a6, a7, b6, gain, factor, acc_in, *refs):
-    *weights, first, second, acc, xs, late = refs
-    normed_units(xs, gain, factor, 6, (a6,), (b6,))
-    normed_units(late, gain, factor, 7, (a7,))
-    acc[...] = acc_in[...]
-    add_units(xs, acc, weights[:3], weights[3:], 6, 1)
+    add_units(xs, acc, weights[:3], weights[3:], 4, 3)
     first[...] = acc[:ROWS, :]
     second[...] = acc[ROWS:, :]
-    add_units(late, first, weights[:3], weights[3:], 7, 1)
-
-
-def project_second_kernel(b7, gain, factor, acc_in, *refs):
+
+
+def project_kernel(half, unit, gain, factor, acc_in, *refs):
     *weights, acc, late = refs
-    place_unit(late, slice(0, ROWS), 0, b7[...], factor[ROWS:, :], gain, 7)
+    place_unit(late, slice(0, ROWS), 0, unit[...], factor[stream_rows(half), :], gain, 7)
     acc[...] = acc_in[...]
     add_units(late, acc, weights[:3], weights[3:], 7, 1)
 
@@ -390,28 +381,23 @@
     add_units(xs, acc, (w0,), (w1,), 0, 4)
 
 
-def out_middle_kernel(a4, a5, b4, b5, acc_in, hidden, w0, w1, acc, xs):
-    stream_units(xs, (a4, a5), (b4, b5))
+def out_middle_kernel(a4, a5, a6, b4, b5, b6, acc_in, hidden, w0, w1, acc, xs):
+    stream_units(xs, (a4, a5, a6), (b4, b5, b6))
     acc[...] = acc_in[...] + hidden[...].astype(jnp.float32)
-    add_units(xs, acc, (w0,), (w1,), 4, 2)
-
-
-def out_first_kernel(a6, a7, b6, acc_in, w0, w1, out, second, acc, first, xs, late):
-    stream_units(xs, (a6,), (b6,))
-    stream_units(late, (a7,))
-    acc[...] = acc_in[...]
-    add_units(xs, acc, (w0,), (w1,), 6, 1)
-    first[...] = acc[:ROWS, :]
-    second[...] = acc[ROWS:, :]
-    add_units(late, first, (w0,), (w1,), 7, 1)
-    out[...] = first[...].astype(jnp.bfloat16)
-
-
-def out_second_kernel(b7, acc_in, w0, w1, partial, out, acc, late):
-    stream_units(late, (b7,))
-    acc[...] = acc_in[...]
-    add_units(late, acc, (w0,), (w1,), 7, 1)
-    out[...] = acc[...].astype(jnp.bfloat16)
+    add_units(xs, acc, (w0,), (w1,), 4, 3)
+
+
+def out_last_kernel(a7, b7, acc, w0, w1, out, xs):
+    width = out.shape[1]
+    block = pl.ds(pl.multiple_of(pl.program_id(0) * width, width), width)
+    stream_units(xs, (a7,), (b7,))
+    mine, cols = columns_of(7)
+    for here, part in ((mine, w0), (jnp.logical_not(mine), w1)):
+
+        @pl.when(here)
+        def _(part=part):
+            total = acc[:, block] + contract(xs[0], part[block, cols])
+            out[...] = total.astype(jnp.bfloat16)
 
 
 def summed_over_tp(value):
@@ -525,29 +511,27 @@
     weights = (*own, *others)
     a5, acc = after(a5, acc)
     a7, b7 = swapped(a5, 1), swapped(b5, 1)
-    acc = kernel_call(
-        middle_kernel,
-        out_shape=acc_shape,
-        in_specs=[VM] * 13,
-        out_specs=VM,
-        scratch_shapes=[pltpu.VMEM((2, STRETCH, UNIT), bf16)],
-        compiler_params=params(8),
-        cost_estimate=cost(STRETCH, 2, qkv),
-    )(a4, a5, b4, b5, gain, factor, acc, *weights)
     half_shape = jax.ShapeDtypeStruct((ROWS, qkv), f32)
     first, second = kernel_call(
-        project_first_kernel,
+        middle_kernel,
         out_shape=(half_shape, half_shape),
-        in_specs=[VM] * 12,
+        in_specs=[VM] * 15,
         out_specs=(VM, VM),
-        scratch_shapes=[
-            pltpu.VMEM((STRETCH, qkv), f32),
-            pltpu.VMEM((1, STRETCH, UNIT), bf16),
-            pltpu.VMEM((1, ROWS, UNIT), bf16),
-        ],
-        compiler_params=params(8),
-        cost_estimate=cost(STRETCH, 2, qkv),
-    )(a6, a7, b6, gain, factor, acc, *weights)
+        scratch_shapes=[pltpu.VMEM((STRETCH, qkv), f32), pltpu.VMEM((3, STRETCH, UNIT), bf16)],
+        compiler_params=params(10),
+        cost_estimate=cost(STRETCH, 3, qkv),
+    )(a4, a5, a6, b4, b5, b6, gain, factor, acc, *weights)
+
+    def project(half, unit, partial):
+        return kernel_call(
+            lambda *refs: project_kernel(half, *refs),
+            out_shape=half_shape,
+            in_specs=[VM] * 10,
+            out_specs=VM,
+            scratch_shapes=[pltpu.VMEM((1, ROWS, UNIT), bf16)],
+            compiler_params=params(8),
+            cost_estimate=cost(ROWS, 1, qkv),
+        )(unit, gain, factor, partial, *weights)
 
     def attend_stream(half, projected, early):
         kv = jax.ShapeDtypeStruct((ROWS, HD), bf16)
@@ -560,17 +544,9 @@
             cost_estimate=cost(ROWS, 2, qkv),
         )(lengths, projected, cosine, sine, *early)
 
-    a0, key_a, value_a = attend_stream(0, first, ())
+    a0, key_a, value_a = attend_stream(0, project(0, a7, first), ())
     a1, a2 = swapped(a0, 0), swapped(a0, 1)
-    projected = kernel_call(
-        project_second_kernel,
-        out_shape=half_shape,
-        in_specs=[VM] * 10,
-        out_specs=VM,
-        scratch_shapes=[pltpu.VMEM((1, ROWS, UNIT), bf16)],
-        compiler_params=params(10),
-        cost_estimate=cost(ROWS, 1, qkv),
-    )(b7, gain, factor, second, *weights)
+    projected = project(1, b7, second)
     a3 = swapped(a1, 1)
     b0, _, _ = attend_stream(1, projected, (key_a, value_a))
     b1, b2 = swapped(b0, 0), swapped(b0, 1)
@@ -593,43 +569,22 @@
     acc = kernel_call(
         out_middle_kernel,
         out_shape=acc_shape,
-        in_specs=[VM] * 8,
+        in_specs=[VM] * 10,
         out_specs=VM,
-        scratch_shapes=[pltpu.VMEM((2, STRETCH, UNIT), bf16)],
+        scratch_shapes=[pltpu.VMEM((3, STRETCH, UNIT), bf16)],
+        compiler_params=params(10),
+        cost_estimate=cost(STRETCH, 3, width),
+    )(a4, a5, a6, b4, b5, b6, acc, hidden_in, output_weight, other_output)
+    return kernel_call(
+        out_last_kernel,
+        grid=(2,),
+        out_shape=jax.ShapeDtypeStruct((STRETCH, width), bf16),
+        in_specs=[VM] * 5,
+        out_specs=pl.BlockSpec((STRETCH, width // 2), lambda n: (0, n)),
+        scratch_shapes=[pltpu.VMEM((1, STRETCH, UNIT), bf16)],
         compiler_params=params(8),
-        cost_estimate=cost(STRETCH, 2, width),
-    )(a4, a5, b4, b5, acc, hidden_in, output_weight, other_output)
-
-    out_shape = jax.ShapeDtypeStruct((STRETCH, UNIT), bf16)
-    half_shape = jax.ShapeDtypeStruct((ROWS, width), f32)
-    half = pltpu.VMEM((ROWS, width), f32)
-    late = pltpu.VMEM((1, ROWS, UNIT), bf16)
-    out, acc = kernel_call(
-        out_first_kernel,
-        grid=(1,),
-        out_shape=(out_shape, half_shape),
-        in_specs=[VM] * 6,
-        out_specs=(pl.BlockSpec((ROWS, UNIT), lambda i: (0, 0)), VM),
-        scratch_shapes=[
-            pltpu.VMEM((STRETCH, width), f32),
-            half,
-            pltpu.VMEM((1, STRETCH, UNIT), bf16),
-            late,
-        ],
-        compiler_params=params(8),
-        cost_estimate=cost(STRETCH, 2, width),
-    )(a6, a7, b6, acc, output_weight, other_output)
-    return kernel_call(
-        out_second_kernel,
-        grid=(1,),
-        out_shape=out_shape,
-        in_specs=[VM] * 4 + [HBM],
-        out_specs=pl.BlockSpec((ROWS, UNIT), lambda i: (1, 0)),
-        scratch_shapes=[half, late],
-        input_output_aliases={4: 0},
-        compiler_params=params(8),
-        cost_estimate=cost(ROWS, 1, width),
-    )(b7, acc, output_weight, other_output, out)
+        cost_estimate=cost(STRETCH, 1, width),
+    )(a7, b7, acc, output_weight, other_output)
 
 
 def fits_ring(mesh):

time: 120 us -> 116 us (0.967)
  starting transfers between devices: 45.8 us -> 38.4 us
  waiting for transfers between devices: 44 us -> 49 us
  Pallas kernels: 26.3 us -> 24.8 us
    ppermute x28, starting transfers between devices: 37.5 us -> 29.8 us  [swapped(): return lax.ppermute(shard, ('tp', 'pair'), ring_swap(later))]
    ppermute x28, waiting for transfers between devices: 40.3 us -> 47 us  [swapped(): return lax.ppermute(shard, ('tp', 'pair'), ring_swap(later))]
    ppermute x3, waiting for transfers between devices: 3.68 us -> 1.98 us  [summed_over_tp(): value = value + lax.ppermute(value, ('tp', 'pair'), pairs)]
    pallas_call x6 -> x5, Pallas kernels: 12 us -> 10.5 us  [the longest x1 3.77 us: ring_layer(): kernel_call(middle_kernel, out_shape=(half_shape, half_shape), in_specs=[...]
  transfers between devices with their start and end apart: 35 -> 35, of which waited for: 17 -> 17; matrix products, arithmetic and copies ran while one was open for 2% -> 2% of each run, Pallas kernels for 21% -> 20%
where the time goes in v7:
time: 116 us
  waiting for transfers between devices  49 us (42%)
  starting transfers between devices  38.4 us (33%)
  Pallas kernels  24.8 us (21%)
  other arithmetic  1.73 us (1%)
  local copies, waits for them, and re-layouts  1.52 us (1%)
    ppermute x28, waiting for transfers between devices, swapped(): return lax.ppermute(shard, ('tp', 'pair'), ring_swap(later))  47 us
    ppermute x28, starting transfers between devices, swapped(): return lax.ppermute(shard, ('tp', 'pair'), ring_swap(later))  29.8 us
    ppermute x3, starting transfers between devices, summed_over_tp(): value = value + lax.ppermute(value, ('tp', 'pair'), pairs)  8.17 us
    pallas_call x1, Pallas kernels, ring_layer(): kernel_call(early_kernel, out_shape=(acc_shape, half_query, half_query, b...  5.7 us
    pallas_call x1, Pallas kernels, ring_layer(): kernel_call(middle_kernel, out_shape=(half_shape, half_shape), in_specs=[...  3.77 us
    pallas_call x2, Pallas kernels, attend_stream(): kernel_call(lambda *refs: attend_kernel(half, *refs), out_shape=(jax.Shap...  3.57 us
    pallas_call x1, Pallas kernels, ring_layer(): kernel_call(out_early_kernel, out_shape=acc_shape, in_specs=[VM] * 10, ou...  3.37 us
    pallas_call x1, Pallas kernels, ring_layer(): kernel_call(out_middle_kernel, out_shape=acc_shape, in_specs=[VM] * 10, o...  2.56 us
  transfers between devices with their start and end apart: 35, of which 17 were waited for; matrix products, arithmetic and copies ran while one was open for 2% of the time, Pallas kernels for 20%

profile of v7, /device:TPU:0, one launch (start us, length us, event | category | flops | bytes accessed | tf_op | source)
XLA Modules:
  0.0 115.6 jit_solution(10730105204462060330)
XLA Ops:
  1.7 3.0 %collective-permute-start = (f32[2,128]{1,0:T(2,128)S(1)}, f32[2,128]{1,0:T(2,128)S(1)}, u32[]{:S(2)}, u32[]{:S(2)}) collective-permute-start(f32[2,128]{1,0:T(2,128)S(1)} %bitcast.13), channel_id=1, source_target_pairs={{0,2},{1,5},{2,0},{3,7},{4,6},{5,1},{6,4},{7,3},{8,10},{9,13},{10,... | collective-permute-start | bytes 3080 | tf_op jit(solution)/shard_map/ppermute | solution.py:406
  6.3 2.1 %collective-permute-start.1 = (f32[2,128]{1,0:T(2,128)S(1)}, f32[2,128]{1,0:T(2,128)S(1)}, u32[]{:S(2)}, u32[]{:S(2)}) collective-permute-start(f32[2,128]{1,0:T(2,128)S(1)} %bitcast_add_fusion), channel_id=1, source_target_pairs={{0,4},{1,3},{2,6},{3,1},{4,0},{5,7},{6,2},{7,5},{8,12},{9,11},{10,... | collective-permute-start | bytes 3080 | tf_op jit(solution)/shard_map/ppermute | solution.py:406
  10.0 3.0 %collective-permute-start.2 = (f32[2,128]{1,0:T(2,128)S(1)}, f32[2,128]{1,0:T(2,128)S(1)}, u32[]{:S(2)}, u32[]{:S(2)}) collective-permute-start(f32[2,128]{1,0:T(2,128)S(1)} %fusion.3), channel_id=1, source_target_pairs={{0,8},{1,9},{2,10},{3,11},{4,12},{5,13},{6,14},{7,15},{8,0},{9,1},... | collective-permute-start | bytes 3080 | tf_op jit(solution)/shard_map/ppermute | solution.py:406
  17.4 4.5 %collective-permute-done.7.b1 = bf16[128,1024]{1,0:T(8,128)(2,1)S(1)} collective-permute-done((bf16[128,1024]{1,0:T(8,128)(2,1)S(1)}, bf16[128,1024]{1,0:T(8,128)(2,1)S(1)}, u32[]{:S(2)}, u32[]{:S(2)}) %collective-permute-start.7) | collective-permute-done | bytes 262176 | tf_op jit(solution)/shard_map/ppermute | solution.py:193
  23.9 4.1 %collective-permute-start.14 = (bf16[128,1024]{1,0:T(8,128)(2,1)S(1)}, bf16[128,1024]{1,0:T(8,128)(2,1)S(1)}, u32[]{:S(2)}, u32[]{:S(2)}) collective-permute-start(bf16[128,1024]{1,0:T(8,128)(2,1)S(1)} %collective-permute-done.6.a2), channel_id=1, source_target_pairs={{0,4},{1,3},{2,6},{3,1},{4,0},{5,9},{6,2},{7,11},{8,12},{9,5},{10,... | collective-permute-start | bytes 786440 | tf_op jit(solution)/shard_map/ppermute | solution.py:193
  29.4 4.5 %collective-permute-done.9.b3 = bf16[128,1024]{1,0:T(8,128)(2,1)S(1)} collective-permute-done((bf16[128,1024]{1,0:T(8,128)(2,1)S(1)}, bf16[128,1024]{1,0:T(8,128)(2,1)S(1)}, u32[]{:S(2)}, u32[]{:S(2)}) %collective-permute-start.9) | collective-permute-done | bytes 262176 | tf_op jit(solution)/shard_map/ppermute | solution.py:193
  33.9 2.6 %collective-permute-start.16 = (bf16[128,1024]{1,0:T(8,128)(2,1)S(1)}, bf16[128,1024]{1,0:T(8,128)(2,1)S(1)}, u32[]{:S(2)}, u32[]{:S(2)}) collective-permute-start(bf16[128,1024]{1,0:T(8,128)(2,1)S(1)} %collective-permute-done.8.b2), channel_id=1, source_target_pairs={{0,4},{1,3},{2,6},{3,1},{4,0},{5,9},{6,2},{7,11},{8,12},{9,5},{10,... | collective-permute-start | bytes 786440 | tf_op jit(solution)/shard_map/ppermute | solution.py:193
  36.5 4.3 %collective-permute-done.16.b4 = bf16[128,1024]{1,0:T(8,128)(2,1)S(1)} collective-permute-done((bf16[128,1024]{1,0:T(8,128)(2,1)S(1)}, bf16[128,1024]{1,0:T(8,128)(2,1)S(1)}, u32[]{:S(2)}, u32[]{:S(2)}) %collective-permute-start.16) | collective-permute-done | bytes 262176 | tf_op jit(solution)/shard_map/ppermute | solution.py:193
  40.8 2.0 %collective-permute-start.17 = (bf16[128,1024]{1,0:T(8,128)(2,1)S(1)}, bf16[128,1024]{1,0:T(8,128)(2,1)S(1)}, u32[]{:S(2)}, u32[]{:S(2)}) collective-permute-start(bf16[128,1024]{1,0:T(8,128)(2,1)S(1)} %collective-permute-done.9.b3), channel_id=1, source_target_pairs={{0,4},{1,3},{2,6},{3,1},{4,0},{5,9},{6,2},{7,11},{8,12},{9,5},{10,... | collective-permute-start | bytes 786440 | tf_op jit(solution)/shard_map/ppermute | solution.py:193
  44.6 2.6 %collective-permute-done.17.b5 = bf16[128,1024]{1,0:T(8,128)(2,1)S(1)} collective-permute-done((bf16[128,1024]{1,0:T(8,128)(2,1)S(1)}, bf16[128,1024]{1,0:T(8,128)(2,1)S(1)}, u32[]{:S(2)}, u32[]{:S(2)}) %collective-permute-start.17) | collective-permute-done | bytes 262176 | tf_op jit(solution)/shard_map/ppermute | solution.py:193
  47.2 2.0 %collective-permute-start.5 = (bf16[128,1024]{1,0:T(8,128)(2,1)S(1)}, bf16[128,1024]{1,0:T(8,128)(2,1)S(1)}, u32[]{:S(2)}, u32[]{:S(2)}) collective-permute-start(bf16[128,1024]{1,0:T(8,128)(2,1)S(1)} %collective-permute-done.4.a3), channel_id=1, source_target_pairs={{0,4},{1,3},{2,6},{3,1},{4,0},{5,9},{6,2},{7,11},{8,12},{9,5},{10,... | collective-permute-start | bytes 786440 | tf_op jit(solution)/shard_map/ppermute | solution.py:193
  49.3 2.5 %collective-permute-start.15 = (bf16[128,1024]{1,0:T(8,128)(2,1)S(1)}, bf16[128,1024]{1,0:T(8,128)(2,1)S(1)}, u32[]{:S(2)}, u32[]{:S(2)}) collective-permute-start(bf16[128,1024]{1,0:T(8,128)(2,1)S(1)} %collective-permute-done.14.a4), channel_id=1, source_target_pairs={{0,2},{1,5},{2,0},{3,7},{4,8},{5,1},{6,10},{7,3},{8,4},{9,13},{10,... | collective-permute-start | bytes 786440 | tf_op jit(solution)/shard_map/ppermute | solution.py:193
  54.6 5.7 %shard_map.75 = (f32[256,1280]{1,0:T(8,128)S(1)}, bf16[512,4096]{1,0:T(8,128)(2,1)S(1)}, bf16[512,4096]{1,0:T(8,128)(2,1)S(1)}, bf16[256,4096]{1,0:T(8,128)(2,1)S(1)}) custom-call(bf16[128,1024]{1,0:T(8,128)(2,1)S(1)} %get-tuple-element.26.a0, bf16[128,1024]{1,0:T(8,128)(2,1)S(1)} %collective-permute-done.3.a1, ...), custom_call_target="tpu_custom_call" | custom-call | flops 2684354560 | bytes 11796480 | tf_op jit(solution)/shard_map/pallas_call | solution.py:495
  60.5 3.8 %shard_map.76 = (f32[128,1280]{1,0:T(8,128)S(1)}, f32[128,1280]{1,0:T(8,128)S(1)}) custom-call(bf16[128,1024]{1,0:T(8,128)(2,1)S(1)} %collective-permute-done.14.a4, bf16[128,1024]{1,0:T(8,128)(2,1)S(1)} %collective-permute-done.5.a5, bf16[128,1024]{1,0:T(8,128)(2,1)S(1)} %collective-permute-done.15.a6, bf16[128,1024]{1,0:T(8,128)(2,1)S(1)} %collective-permute-done.16.b4, ...), custom_call_target="tpu_custom_call" | custom-call | flops 2013265920 | bytes 9175040 | tf_op jit(solution)/shard_map/pallas_call | solution.py:515
  69.6 2.1 %shard_map.80 = (bf16[128,1024]{1,0:T(8,128)(2,1)S(1)}, bf16[128,128]{1,0:T(8,128)(2,1)}, bf16[128,128]{1,0:T(8,128)(2,1)}) custom-call(s32[1,4]{1,0:T(1,128)S(1)} %copy-done.3, f32[128,1280]{1,0:T(8,128)S(1)} %shard_map.79.refs_1_, f32[256,128]{1,0:T(8,128)S(1)} %get-tuple-element.36.refs_2_, f32[256,128]{1,0:T(8,128)S(1)} %get-tuple-element.37.refs_3_, ...), custom_call_target="tpu_custom_call" | custom-call | flops 671088640 | bytes 5898240 | tf_op jit(solution)/shard_map/pallas_call | solution.py:538
  71.7 2.1 %collective-permute-start.24 = (bf16[128,1024]{1,0:T(8,128)(2,1)S(1)}, bf16[128,1024]{1,0:T(8,128)(2,1)S(1)}, u32[]{:S(2)}, u32[]{:S(2)}) collective-permute-start(bf16[128,1024]{1,0:T(8,128)(2,1)S(1)} %get-tuple-element.42.b0), channel_id=1, source_target_pairs={{0,4},{1,3},{2,6},{3,1},{4,0},{5,9},{6,2},{7,11},{8,12},{9,5},{10,... | collective-permute-start | bytes 786440 | tf_op jit(solution)/shard_map/ppermute | solution.py:193
  75.8 2.7 %collective-permute-done.19.a1 = bf16[128,1024]{1,0:T(8,128)(2,1)S(1)} collective-permute-done((bf16[128,1024]{1,0:T(8,128)(2,1)S(1)}, bf16[128,1024]{1,0:T(8,128)(2,1)S(1)}, u32[]{:S(2)}, u32[]{:S(2)}) %collective-permute-start.19) | collective-permute-done | bytes 262176 | tf_op jit(solution)/shard_map/ppermute | solution.py:193
  78.6 5.6 %collective-permute-done.24.b1 = bf16[128,1024]{1,0:T(8,128)(2,1)S(1)} collective-permute-done((bf16[128,1024]{1,0:T(8,128)(2,1)S(1)}, bf16[128,1024]{1,0:T(8,128)(2,1)S(1)}, u32[]{:S(2)}, u32[]{:S(2)}) %collective-permute-start.24) | collective-permute-done | bytes 262176 | tf_op jit(solution)/shard_map/ppermute | solution.py:193
  86.2 3.7 %collective-permute-done.20.a3 = bf16[128,1024]{1,0:T(8,128)(2,1)S(1)} collective-permute-done((bf16[128,1024]{1,0:T(8,128)(2,1)S(1)}, bf16[128,1024]{1,0:T(8,128)(2,1)S(1)}, u32[]{:S(2)}, u32[]{:S(2)}) %collective-permute-start.20) | collective-permute-done | bytes 262176 | tf_op jit(solution)/shard_map/ppermute | solution.py:193
  89.9 5.6 %collective-permute-done.26.b3 = bf16[128,1024]{1,0:T(8,128)(2,1)S(1)} collective-permute-done((bf16[128,1024]{1,0:T(8,128)(2,1)S(1)}, bf16[128,1024]{1,0:T(8,128)(2,1)S(1)}, u32[]{:S(2)}, u32[]{:S(2)}) %collective-permute-start.26) | collective-permute-done | bytes 262176 | tf_op jit(solution)/shard_map/ppermute | solution.py:193
  97.6 3.4 %shard_map.81.acc_in = f32[256,1024]{1,0:T(8,128)S(1)} custom-call(bf16[128,1024]{1,0:T(8,128)(2,1)S(1)} %get-tuple-element.38.a0, bf16[128,1024]{1,0:T(8,128)(2,1)S(1)} %collective-permute-done.19.a1, bf16[128,1024]{1,0:T(8,128)(2,1)S(1)} %collective-permute-done.22.a2, bf16[128,1024]{1,0:T(8,128)(2,1)S(1)} %collective-permute-done.20.a3, ...), custom_call_target="tpu_custom_call" | custom-call | flops 2147483648 | bytes 9437184 | tf_op jit(solution)/shard_map/pallas_call | solution.py:558
  101.9 5.6 %collective-permute-done.29.b5 = bf16[128,1024]{1,0:T(8,128)(2,1)S(1)} collective-permute-done((bf16[128,1024]{1,0:T(8,128)(2,1)S(1)}, bf16[128,1024]{1,0:T(8,128)(2,1)S(1)}, u32[]{:S(2)}, u32[]{:S(2)}) %collective-permute-start.29) | collective-permute-done | bytes 262176 | tf_op jit(solution)/shard_map/ppermute | solution.py:193
  107.5 2.6 %shard_map.82.acc = f32[256,1024]{1,0:T(8,128)S(1)} custom-call(bf16[128,1024]{1,0:T(8,128)(2,1)S(1)} %collective-permute-done.31.a4, bf16[128,1024]{1,0:T(8,128)(2,1)S(1)} %collective-permute-done.21.a5, bf16[128,1024]{1,0:T(8,128)(2,1)S(1)} %collective-permute-done.32.a6, bf16[128,1024]{1,0:T(8,128)(2,1)S(1)} %collective-permute-done.33.b4, ...), custom_call_target="tpu_custom_call" | custom-call | flops 1610612736 | bytes 7340032 | tf_op jit(solution)/shard_map/pallas_call | solution.py:569
  110.1 3.8 %collective-permute-done.30.b7 = bf16[128,1024]{1,0:T(8,128)(2,1)S(1)} collective-permute-done((bf16[128,1024]{1,0:T(8,128)(2,1)S(1)}, bf16[128,1024]{1,0:T(8,128)(2,1)S(1)}, u32[]{:S(2)}, u32[]{:S(2)}) %collective-permute-start.30) | collective-permute-done | bytes 262176 | tf_op jit(solution)/shard_map/ppermute | solution.py:193
  (78 shorter events, 31.4 us)
Async XLA Ops:
  0.0 51.9 %collective-permute-start.10 = (bf16[1024,4096]{1,0:T(8,128)(2,1)}, bf16[1024,4096]{1,0:T(8,128)(2,1)S(1)}, u32[]{:S(2)}, u32[]{:S(2)}) collective-permute-start(bf16[1024,4096]{1,0:T(8,128)(2,1)} %refs_0_.1), channel_id=1, source_target_pairs={{0,1},{1,0},{2,3},{3,2},{4,5},{5,4},{6,7},{7,6},{8,9},{9,8},{10,11... | collective-permute-start | bytes 25165832 | tf_op jit(solution)/shard_map/ppermute | solution.py:29
  0.5 97.1 %collective-permute-start.27 = (bf16[1024,4096]{1,0:T(8,128)(2,1)}, bf16[1024,4096]{1,0:T(8,128)(2,1)S(1)}, u32[]{:S(2)}, u32[]{:S(2)}) collective-permute-start(bf16[1024,4096]{1,0:T(8,128)(2,1)} %w0.5), channel_id=1, source_target_pairs={{0,1},{1,0},{2,3},{3,2},{4,5},{5,4},{6,7},{7,6},{8,9},{9,8},{10,11... | collective-permute-start | bytes 25165832 | tf_op jit(solution)/shard_map/ppermute | solution.py:29
  13.0 8.9 %collective-permute-start.7 = (bf16[128,1024]{1,0:T(8,128)(2,1)S(1)}, bf16[128,1024]{1,0:T(8,128)(2,1)S(1)}, u32[]{:S(2)}, u32[]{:S(2)}) collective-permute-start(bf16[128,1024]{1,0:T(8,128)(2,1)S(1)} %get-tuple-element.27.b0), channel_id=1, source_target_pairs={{0,4},{1,3},{2,6},{3,1},{4,0},{5,9},{6,2},{7,11},{8,12},{9,5},{10,... | collective-permute-start | bytes 786440 | tf_op jit(solution)/shard_map/ppermute | solution.py:193
  14.6 9.1 %collective-permute-start.6 = (bf16[128,1024]{1,0:T(8,128)(2,1)S(1)}, bf16[128,1024]{1,0:T(8,128)(2,1)S(1)}, u32[]{:S(2)}, u32[]{:S(2)}) collective-permute-start(bf16[128,1024]{1,0:T(8,128)(2,1)S(1)} %get-tuple-element.26.a0), channel_id=1, source_target_pairs={{0,2},{1,5},{2,0},{3,7},{4,8},{5,1},{6,10},{7,3},{8,4},{9,13},{10,... | collective-permute-start | bytes 786440 | tf_op jit(solution)/shard_map/ppermute | solution.py:193
  23.7 10.2 %collective-permute-start.9 = (bf16[128,1024]{1,0:T(8,128)(2,1)S(1)}, bf16[128,1024]{1,0:T(8,128)(2,1)S(1)}, u32[]{:S(2)}, u32[]{:S(2)}) collective-permute-start(bf16[128,1024]{1,0:T(8,128)(2,1)S(1)} %collective-permute-done.7.b1), channel_id=1, source_target_pairs={{0,2},{1,5},{2,0},{3,7},{4,8},{5,1},{6,10},{7,3},{8,4},{9,13},{10,... | collective-permute-start | bytes 786440 | tf_op jit(solution)/shard_map/ppermute | solution.py:193
  23.9 10.0 %collective-permute-start.14 = (bf16[128,1024]{1,0:T(8,128)(2,1)S(1)}, bf16[128,1024]{1,0:T(8,128)(2,1)S(1)}, u32[]{:S(2)}, u32[]{:S(2)}) collective-permute-start(bf16[128,1024]{1,0:T(8,128)(2,1)S(1)} %collective-permute-done.6.a2), channel_id=1, source_target_pairs={{0,4},{1,3},{2,6},{3,1},{4,0},{5,9},{6,2},{7,11},{8,12},{9,5},{10,... | collective-permute-start | bytes 786440 | tf_op jit(solution)/shard_map/ppermute | solution.py:193
  29.3 20.0 %collective-permute-start.11 = (bf16[128,4096]{1,0:T(8,128)(2,1)}, bf16[128,4096]{1,0:T(8,128)(2,1)S(1)}, u32[]{:S(2)}, u32[]{:S(2)}) collective-permute-start(bf16[128,4096]{1,0:T(8,128)(2,1)} %refs_1_.1), channel_id=1, source_target_pairs={{0,1},{1,0},{2,3},{3,2},{4,5},{5,4},{6,7},{7,6},{8,9},{9,8},{10,11... | collective-permute-start | bytes 3145736 | tf_op jit(solution)/shard_map/ppermute | solution.py:29
  33.9 18.0 %collective-permute-start.12 = (bf16[128,4096]{1,0:T(8,128)(2,1)}, bf16[128,4096]{1,0:T(8,128)(2,1)S(1)}, u32[]{:S(2)}, u32[]{:S(2)}) collective-permute-start(bf16[128,4096]{1,0:T(8,128)(2,1)} %refs_2_.1), channel_id=1, source_target_pairs={{0,1},{1,0},{2,3},{3,2},{4,5},{5,4},{6,7},{7,6},{8,9},{9,8},{10,11... | collective-permute-start | bytes 3145736 | tf_op jit(solution)/shard_map/ppermute | solution.py:29
  47.2 13.2 %collective-permute-start.5 = (bf16[128,1024]{1,0:T(8,128)(2,1)S(1)}, bf16[128,1024]{1,0:T(8,128)(2,1)S(1)}, u32[]{:S(2)}, u32[]{:S(2)}) collective-permute-start(bf16[128,1024]{1,0:T(8,128)(2,1)S(1)} %collective-permute-done.4.a3), channel_id=1, source_target_pairs={{0,4},{1,3},{2,6},{3,1},{4,0},{5,9},{6,2},{7,11},{8,12},{9,5},{10,... | collective-permute-start | bytes 786440 | tf_op jit(solution)/shard_map/ppermute | solution.py:193
  49.3 11.2 %collective-permute-start.15 = (bf16[128,1024]{1,0:T(8,128)(2,1)S(1)}, bf16[128,1024]{1,0:T(8,128)(2,1)S(1)}, u32[]{:S(2)}, u32[]{:S(2)}) collective-permute-start(bf16[128,1024]{1,0:T(8,128)(2,1)S(1)} %collective-permute-done.14.a4), channel_id=1, source_target_pairs={{0,2},{1,5},{2,0},{3,7},{4,8},{5,1},{6,10},{7,3},{8,4},{9,13},{10,... | collective-permute-start | bytes 786440 | tf_op jit(solution)/shard_map/ppermute | solution.py:193
  51.8 8.7 %collective-permute-start.18 = (bf16[128,1024]{1,0:T(8,128)(2,1)S(1)}, bf16[128,1024]{1,0:T(8,128)(2,1)S(1)}, u32[]{:S(2)}, u32[]{:S(2)}) collective-permute-start(bf16[128,1024]{1,0:T(8,128)(2,1)S(1)} %collective-permute-done.16.b4), channel_id=1, source_target_pairs={{0,2},{1,5},{2,0},{3,7},{4,8},{5,1},{6,10},{7,3},{8,4},{9,13},{10,... | collective-permute-start | bytes 786440 | tf_op jit(solution)/shard_map/ppermute | solution.py:193
  51.9 12.4 %collective-permute-start.23 = (bf16[128,1024]{1,0:T(8,128)(2,1)S(1)}, bf16[128,1024]{1,0:T(8,128)(2,1)S(1)}, u32[]{:S(2)}, u32[]{:S(2)}) collective-permute-start(bf16[128,1024]{1,0:T(8,128)(2,1)S(1)} %collective-permute-done.17.b5), channel_id=1, source_target_pairs={{0,2},{1,5},{2,0},{3,7},{4,8},{5,1},{6,10},{7,3},{8,4},{9,13},{10,... | collective-permute-start | bytes 786440 | tf_op jit(solution)/shard_map/ppermute | solution.py:193
  69.5 9.0 %collective-permute-start.19 = (bf16[128,1024]{1,0:T(8,128)(2,1)S(1)}, bf16[128,1024]{1,0:T(8,128)(2,1)S(1)}, u32[]{:S(2)}, u32[]{:S(2)}) collective-permute-start(bf16[128,1024]{1,0:T(8,128)(2,1)S(1)} %get-tuple-element.38.a0), channel_id=1, source_target_pairs={{0,4},{1,3},{2,6},{3,1},{4,0},{5,9},{6,2},{7,11},{8,12},{9,5},{10,... | collective-permute-start | bytes 786440 | tf_op jit(solution)/shard_map/ppermute | solution.py:193
  71.7 12.4 %collective-permute-start.24 = (bf16[128,1024]{1,0:T(8,128)(2,1)S(1)}, bf16[128,1024]{1,0:T(8,128)(2,1)S(1)}, u32[]{:S(2)}, u32[]{:S(2)}) collective-permute-start(bf16[128,1024]{1,0:T(8,128)(2,1)S(1)} %get-tuple-element.42.b0), channel_id=1, source_target_pairs={{0,4},{1,3},{2,6},{3,1},{4,0},{5,9},{6,2},{7,11},{8,12},{9,5},{10,... | collective-permute-start | bytes 786440 | tf_op jit(solution)/shard_map/ppermute | solution.py:193
  73.8 10.4 %collective-permute-start.25 = (bf16[128,1024]{1,0:T(8,128)(2,1)S(1)}, bf16[128,1024]{1,0:T(8,128)(2,1)S(1)}, u32[]{:S(2)}, u32[]{:S(2)}) collective-permute-start(bf16[128,1024]{1,0:T(8,128)(2,1)S(1)} %get-tuple-element.42.b0), channel_id=1, source_target_pairs={{0,2},{1,5},{2,0},{3,7},{4,8},{5,1},{6,10},{7,3},{8,4},{9,13},{10,... | collective-permute-start | bytes 786440 | tf_op jit(solution)/shard_map/ppermute | solution.py:193
  74.4 9.9 %collective-permute-start.22 = (bf16[128,1024]{1,0:T(8,128)(2,1)S(1)}, bf16[128,1024]{1,0:T(8,128)(2,1)S(1)}, u32[]{:S(2)}, u32[]{:S(2)}) collective-permute-start(bf16[128,1024]{1,0:T(8,128)(2,1)S(1)} %get-tuple-element.38.a0), channel_id=1, source_target_pairs={{0,2},{1,5},{2,0},{3,7},{4,8},{5,1},{6,10},{7,3},{8,4},{9,13},{10,... | collective-permute-start | bytes 786440 | tf_op jit(solution)/shard_map/ppermute | solution.py:193
  78.6 11.4 %collective-permute-start.20 = (bf16[128,1024]{1,0:T(8,128)(2,1)S(1)}, bf16[128,1024]{1,0:T(8,128)(2,1)S(1)}, u32[]{:S(2)}, u32[]{:S(2)}) collective-permute-start(bf16[128,1024]{1,0:T(8,128)(2,1)S(1)} %collective-permute-done.19.a1), channel_id=1, source_target_pairs={{0,2},{1,5},{2,0},{3,7},{4,8},{5,1},{6,10},{7,3},{8,4},{9,13},{10,... | collective-permute-start | bytes 786440 | tf_op jit(solution)/shard_map/ppermute | solution.py:193
  84.2 11.4 %collective-permute-start.26 = (bf16[128,1024]{1,0:T(8,128)(2,1)S(1)}, bf16[128,1024]{1,0:T(8,128)(2,1)S(1)}, u32[]{:S(2)}, u32[]{:S(2)}) collective-permute-start(bf16[128,1024]{1,0:T(8,128)(2,1)S(1)} %collective-permute-done.24.b1), channel_id=1, source_target_pairs={{0,2},{1,5},{2,0},{3,7},{4,8},{5,1},{6,10},{7,3},{8,4},{9,13},{10,... | collective-permute-start | bytes 786440 | tf_op jit(solution)/shard_map/ppermute | solution.py:193
  84.2 11.4 %collective-permute-start.33 = (bf16[128,1024]{1,0:T(8,128)(2,1)S(1)}, bf16[128,1024]{1,0:T(8,128)(2,1)S(1)}, u32[]{:S(2)}, u32[]{:S(2)}) collective-permute-start(bf16[128,1024]{1,0:T(8,128)(2,1)S(1)} %collective-permute-done.25.b2), channel_id=1, source_target_pairs={{0,4},{1,3},{2,6},{3,1},{4,0},{5,9},{6,2},{7,11},{8,12},{9,5},{10,... | collective-permute-start | bytes 786440 | tf_op jit(solution)/shard_map/ppermute | solution.py:193
  84.3 12.0 %collective-permute-start.31 = (bf16[128,1024]{1,0:T(8,128)(2,1)S(1)}, bf16[128,1024]{1,0:T(8,128)(2,1)S(1)}, u32[]{:S(2)}, u32[]{:S(2)}) collective-permute-start(bf16[128,1024]{1,0:T(8,128)(2,1)S(1)} %collective-permute-done.22.a2), channel_id=1, source_target_pairs={{0,4},{1,3},{2,6},{3,1},{4,0},{5,9},{6,2},{7,11},{8,12},{9,5},{10,... | collective-permute-start | bytes 786440 | tf_op jit(solution)/shard_map/ppermute | solution.py:193
  89.9 12.0 %collective-permute-start.21 = (bf16[128,1024]{1,0:T(8,128)(2,1)S(1)}, bf16[128,1024]{1,0:T(8,128)(2,1)S(1)}, u32[]{:S(2)}, u32[]{:S(2)}) collective-permute-start(bf16[128,1024]{1,0:T(8,128)(2,1)S(1)} %collective-permute-done.20.a3), channel_id=1, source_target_pairs={{0,4},{1,3},{2,6},{3,1},{4,0},{5,9},{6,2},{7,11},{8,12},{9,5},{10,... | collective-permute-start | bytes 786440 | tf_op jit(solution)/shard_map/ppermute | solution.py:193
  95.6 12.0 %collective-permute-start.29 = (bf16[128,1024]{1,0:T(8,128)(2,1)S(1)}, bf16[128,1024]{1,0:T(8,128)(2,1)S(1)}, u32[]{:S(2)}, u32[]{:S(2)}) collective-permute-start(bf16[128,1024]{1,0:T(8,128)(2,1)S(1)} %collective-permute-done.26.b3), channel_id=1, source_target_pairs={{0,4},{1,3},{2,6},{3,1},{4,0},{5,9},{6,2},{7,11},{8,12},{9,5},{10,... | collective-permute-start | bytes 786440 | tf_op jit(solution)/shard_map/ppermute | solution.py:193
  95.6 12.0 %collective-permute-start.34 = (bf16[128,1024]{1,0:T(8,128)(2,1)S(1)}, bf16[128,1024]{1,0:T(8,128)(2,1)S(1)}, u32[]{:S(2)}, u32[]{:S(2)}) collective-permute-start(bf16[128,1024]{1,0:T(8,128)(2,1)S(1)} %collective-permute-done.33.b4), channel_id=1, source_target_pairs={{0,2},{1,5},{2,0},{3,7},{4,8},{5,1},{6,10},{7,3},{8,4},{9,13},{10,... | collective-permute-start | bytes 786440 | tf_op jit(solution)/shard_map/ppermute | solution.py:193
  96.3 11.2 %collective-permute-start.32 = (bf16[128,1024]{1,0:T(8,128)(2,1)S(1)}, bf16[128,1024]{1,0:T(8,128)(2,1)S(1)}, u32[]{:S(2)}, u32[]{:S(2)}) collective-permute-start(bf16[128,1024]{1,0:T(8,128)(2,1)S(1)} %collective-permute-done.31.a4), channel_id=1, source_target_pairs={{0,2},{1,5},{2,0},{3,7},{4,8},{5,1},{6,10},{7,3},{8,4},{9,13},{10,... | collective-permute-start | bytes 786440 | tf_op jit(solution)/shard_map/ppermute | solution.py:193
  (17 other events, 169.2 us)
